TPU v7x, 128 devices: a whole 4x4x4 slice. The times are simulated.
128 devices in a mesh: tensor: 8 (over y, core), context: 16 (over z, x).
Axes of the slice: x: 4, y: 4, z: 4, core: 2. Of those that a mesh axis runs over, the one named last changes fastest.
Arguments:
- tokens: bfloat16 [4096, 5120], P('context', 'tensor'), may hold values from -6 to 6
- query_weight: bfloat16 [5120, 5120], P('context', 'tensor'), may hold values from -0.078125 to 0.078125
- key_weight: bfloat16 [5120, 5120], P('context', 'tensor'), may hold values from -0.078125 to 0.078125
- value_weight: bfloat16 [5120, 5120], P('context', 'tensor'), may hold values from -0.078125 to 0.078125
- cache_keys: bfloat16 [512, 64, 5120], P('context', None, 'tensor'), may hold values from -160 to 160
- cache_values: bfloat16 [512, 64, 5120], P('context', None, 'tensor'), may hold values from -6 to 6
- selected: int32 [32, 32], P('context'), may hold values from -1 to 511, as said below
- counts: int32 [32], P('context'), may hold values from 24 to 32, as said below
- block_slot: int32 [512], replicated, may hold values from 0 to 511, as said below
Outputs:
- attended: bfloat16 [4096, 5120], P('context', 'tensor')
Inputs may be any that keep to these rules, and one draw needn't show every extreme that they name: `selected`: row c names different block ids in its first counts[c] entries and -1 in the others. Among the valid entries of the 2 query blocks of one context device, at most 8 name blocks stored on one context device (block_slot[b] // 32), and exactly 8 do for some device in every draw. `counts`: some query block has 32 valid entries in every draw. `block_slot`: each row of the cache arrays stores exactly one block id.
All inputs are finite; a program needn't handle non-finite values.
Results may differ from a plain program's by a relative error of at most 0.012.
The roundings to bfloat16 on the way count: a program that leaves them out, or rounds other values in their place, can miss the bound.
Values may be sent and summed in bfloat16 or wider, within the bound.
A program may use at most 192 MiB of HBM per device.

v0:
```python
import jax
import jax.numpy as jnp
from jax import lax
from jax.sharding import PartitionSpec as P

HDIM = 128


NEGATIVE = -1e30


def from_behind(block, axis, distance):
    devices = range(lax.axis_size(axis))
    route = [(i - distance, i) for i in devices if i - distance in devices]
    return lax.ppermute(block, axis, route)


def attend_block(queries, keys_in, values_in, allowed):
    span_count, row_count, feature_width = queries.shape
    head_count = feature_width // HDIM
    query_heads = queries.reshape(span_count, row_count, head_count, HDIM)
    key_heads = keys_in.reshape(span_count, -1, head_count, HDIM)
    value_heads = values_in.reshape(span_count, -1, head_count, HDIM)
    scores = jnp.einsum(
        "cqhd,ckhd->chqk", query_heads, key_heads, preferred_element_type=jnp.float32
    ) * HDIM ** (-0.5)
    opened = allowed[:, None, :, :]
    masked = jnp.where(opened, scores, NEGATIVE)
    highest = jnp.max(masked, axis=3)
    weights = jnp.where(opened, jnp.exp(masked - highest[..., None]), 0.0)
    totals = jnp.sum(weights, axis=3)
    summed = jnp.einsum(
        "chqk,ckhd->chqd",
        weights.astype(jnp.bfloat16),
        value_heads,
        preferred_element_type=jnp.float32,
    )
    return (highest, totals, summed)


def earlier_count(same_group):
    entries = same_group.shape[0]
    position = jnp.arange(entries)
    before = position[None, :] < position[:, None]
    return jnp.sum(jnp.where(same_group & before, 1, 0), axis=1).astype(jnp.int32)


def fill_table(valid_entries, target, payload, length):
    position = jnp.arange(length)
    hits = valid_entries[:, None] & (target[:, None] == position[None, :])
    return jnp.sum(jnp.where(hits, payload[:, None] + 1, 0), axis=0) - 1


def shards(
    tokens,
    query_weight,
    key_weight,
    value_weight,
    cache_keys,
    cache_values,
    selected,
    counts,
    block_slot,
):
    features_all = lax.all_gather(tokens, "tensor", axis=1, tiled=True)
    token_count = features_all.shape[0]
    feature_width = query_weight.shape[1]
    pieces = (
        lax.all_gather(query_weight, "context", axis=0, tiled=True),
        lax.all_gather(key_weight, "context", axis=0, tiled=True),
        lax.all_gather(value_weight, "context", axis=0, tiled=True),
    )
    projected = tuple(
        (
            jnp.dot(features_all, weight_piece, preferred_element_type=jnp.float32)
            for weight_piece in pieces
        )
    )
    span_count = selected.shape[0]
    select_count = selected.shape[1]
    span_rows = token_count // span_count
    query_spans = projected[0].astype(jnp.bfloat16).reshape(span_count, span_rows, feature_width)
    key_spans = projected[1].astype(jnp.bfloat16).reshape(span_count, span_rows, feature_width)
    value_spans = projected[2].astype(jnp.bfloat16).reshape(span_count, span_rows, feature_width)
    before_keys, before_values = from_behind((key_spans[-1], value_spans[-1]), "context", 1)
    prior_keys = jnp.concatenate([before_keys[None], key_spans[:-1]], 0)
    prior_values = jnp.concatenate([before_values[None], value_spans[:-1]], 0)
    local_keys = jnp.concatenate([prior_keys, key_spans], 1)
    local_values = jnp.concatenate([prior_values, value_spans], 1)
    span_index = lax.axis_index("context") * span_count + jnp.arange(span_count)
    prior_open = jnp.broadcast_to(
        (span_index > 0)[:, None, None], (span_count, span_rows, span_rows)
    )
    row_index = jnp.arange(span_rows)
    causal = jnp.broadcast_to(
        (row_index[None, :] <= row_index[:, None])[None], (span_count, span_rows, span_rows)
    )
    local_open = jnp.concatenate([prior_open, causal], 2)
    devices = lax.axis_size("context")
    capacity = max(2, 2 * span_count * select_count // devices)
    stored = cache_keys.shape[0]
    block_rows = cache_keys.shape[1]
    chosen = selected.reshape(-1)
    live_entries = (jnp.arange(select_count)[None, :] < counts[:, None]).reshape(-1)
    matches = chosen[:, None] == jnp.arange(block_slot.shape[0])[None, :]
    slot_rows = jnp.sum(jnp.where(matches, block_slot[None, :], 0), axis=1)
    owner_device = slot_rows // stored
    local_row = slot_rows % stored
    same_owner = (owner_device[:, None] == owner_device[None, :]) & live_entries[None, :]
    target = owner_device * capacity + earlier_count(same_owner)
    wanted = fill_table(live_entries, target, local_row, devices * capacity).reshape(
        devices, capacity
    )
    rows_used = jnp.clip(
        lax.all_to_all(wanted, "context", split_axis=0, concat_axis=0, tiled=True), 0, stored - 1
    )
    arrived_keys = lax.all_to_all(
        jnp.take(cache_keys, rows_used, axis=0), "context", split_axis=0, concat_axis=0, tiled=True
    )
    arrived_values = lax.all_to_all(
        jnp.take(cache_values, rows_used, axis=0),
        "context",
        split_axis=0,
        concat_axis=0,
        tiled=True,
    )
    placed = jnp.clip(target, 0, devices * capacity - 1).reshape(span_count, select_count)
    flat_keys = arrived_keys.reshape(devices * capacity, block_rows, feature_width)
    flat_values = arrived_values.reshape(devices * capacity, block_rows, feature_width)
    far_keys = jnp.take(flat_keys, placed, axis=0).reshape(
        span_count, select_count * block_rows, feature_width
    )
    far_values = jnp.take(flat_values, placed, axis=0).reshape(
        span_count, select_count * block_rows, feature_width
    )
    far_open = jnp.repeat(live_entries.reshape(span_count, select_count), block_rows, axis=1)
    all_open = jnp.concatenate(
        [
            jnp.broadcast_to(
                far_open[:, None, :], (span_count, span_rows, select_count * block_rows)
            ),
            local_open,
        ],
        2,
    )
    highest, totals, summed = attend_block(
        query_spans,
        jnp.concatenate([far_keys, local_keys], 1),
        jnp.concatenate([far_values, local_values], 1),
        all_open,
    )
    result = summed / totals[..., None]
    merged = jnp.transpose(result, (0, 2, 1, 3)).reshape(token_count, feature_width)
    return merged.astype(jnp.bfloat16)


def solution(mesh):
    placed = (
        P("context", "tensor"),
        P("context", "tensor"),
        P("context", "tensor"),
        P("context", "tensor"),
        P("context", None, "tensor"),
        P("context", None, "tensor"),
        P("context", None),
        P("context"),
        P(),
    )
    return jax.shard_map(
        shards, mesh=mesh, in_specs=placed, out_specs=P("context", "tensor"), check_vma=False
    )
```

profile of v0, /device:TPU:0, one launch (start us, length us, event | category | flops | bytes accessed | tf_op | source)
XLA Modules:
  0.0 503.2 jit_solution(6026133484324396968)
XLA Ops:
  6.5 0.7 all-gather.5.cloned.1.call-update
  7.3 0.7 all-gather.9.cloned.1.call-update
  8.1 0.7 all-gather.11.cloned.1.call-update
  8.7 0.8 eq.22
  9.5 0.9 select_reduce_fusion
  10.4 0.7 iota_compare_fusion.4
  11.2 0.2 select_reduce_fusion.2
  11.4 0.1 select_reduce_fusion.1
  11.5 0.1 sub.24
  11.6 15.4 %all_to_all.16 = s32[16,1,8]{2,1,0:T(1,128)S(1)} all-to-all(s32[16,1,8]{2,1,0:T(1,128)S(1)} %bitcast.48), channel_id=1, replica_groups=mesh['tensor'=8,'context'=16] {'context'}, dimensions={0} | all-to-all | bytes 1024 | tf_op jit(solution)/shard_map/all_to_all | solution.py:115
  27.1 0.1 reshape.218
  27.2 7.6 %gather_fusion = bf16[128,64,640]{2,1,0:T(8,128)(2,1)} fusion(bf16[32,64,640]{2,1,0:T(8,128)(2,1)S(1)} %copy-done, s32[1024]{0:T(1024)S(1)} %pad_clamp_fusion.1), kind=kCustom, calls=%fused_computation.clone | custom fusion | bytes 20972032 | tf_op jit(solution)/shard_map/jit(_take)/gather | solution.py:118
  34.8 9.3 %gather_fusion.2 = bf16[128,64,640]{2,1,0:T(8,128)(2,1)} fusion(bf16[32,64,640]{2,1,0:T(8,128)(2,1)} %param.18, s32[1024]{0:T(1024)S(1)} %pad_clamp_fusion.1), kind=kCustom, calls=%fused_computation.2.clone | custom fusion | bytes 20972032 | tf_op jit(solution)/shard_map/jit(_take)/gather | solution.py:121
  44.3 13.3 %broadcast_select_fusion.1 = (bf16[16,8,64,640]{3,2,1,0:T(8,128)(2,1)S(1)}, bf16[16,8,64,640]{3,2,1,0:T(8,128)(2,1)}) fusion(bf16[16,8,64,640]{3,2,1,0:T(8,128)(2,1)} %bitcast.38, pred[16,8]{1,0:T(8,128)(4,1)S(1)} %copy.72, bf16[16,8,64,640]{3,2,1,0:T(8,128)(2,1)} %bitcast.39), kind=kLoop, calls=%fused_computation.8 | loop fusion | flops 10485760 | bytes 41943168 | tf_op jit(solution)/shard_map/jit(_take)/select_n | solution.py:118
  57.6 148.1 %all_to_all.17 = bf16[16,8,64,640]{3,2,1,0:T(8,128)(2,1)} all-to-all(bf16[16,8,64,640]{3,2,1,0:T(8,128)(2,1)S(1)} %get-tuple-element.13), channel_id=1, replica_groups=mesh['tensor'=8,'context'=16] {'context'}, dimensions={0} | all-to-all | bytes 20971520 | tf_op jit(solution)/shard_map/all_to_all | solution.py:117
  205.7 4.8 all-to-all-start.2
  210.5 0.2 all-gather.7.cloned.1.call-start
  210.8 0.3 all-gather.7.cloned.1.call-update
  211.4 0.1 broadcast_in_dim.109
  211.6 0.2 broadcast_in_dim.110
  212.0 7.8 %gather_fusion.1 = bf16[64,64,640]{2,1,0:T(8,128)(2,1)} fusion(bf16[128,64,640]{2,1,0:T(8,128)(2,1)} %bitcast.40, s32[1024]{0:T(1024)S(1)} %pad_clamp_fusion), kind=kCustom, calls=%fused_computation.1.clone | custom fusion | bytes 10486016 | tf_op jit(solution)/shard_map/jit(_take)/gather | solution.py:130
  219.8 173.0 %all-to-all-done.2 = bf16[16,8,64,640]{3,2,1,0:T(8,128)(2,1)} async-done(((bf16[16,8,64,640]{3,2,1,0:T(8,128)(2,1)}), bf16[16,8,64,640]{3,2,1,0:T(8,128)(2,1)}, u32[]{:S(2)}, u32[]{:S(2)}) %all-to-all-start.2) | async-done | bytes 10485792 | tf_op jit(solution)/shard_map/all_to_all | solution.py:120
  392.8 7.4 %gather_fusion.3 = bf16[64,64,640]{2,1,0:T(8,128)(2,1)} fusion(bf16[128,64,640]{2,1,0:T(8,128)(2,1)} %bitcast.8, s32[1024]{0:T(1024)S(1)} %pad_clamp_fusion), kind=kCustom, calls=%fused_computation.3.clone | custom fusion | bytes 10486016 | tf_op jit(solution)/shard_map/jit(_take)/gather | solution.py:133
  400.2 9.2 %broadcast_select_fusion.3 = (bf16[2,32,64,640]{3,2,1,0:T(8,128)(2,1)}, bf16[2,32,64,640]{3,2,1,0:T(8,128)(2,1)}) fusion(bf16[2,32,64,640]{3,2,1,0:T(8,128)(2,1)} %bitcast.41, pred[2,32]{1,0:T(4,128)(4,1)S(1)} %get-tuple-element.6, bf16[2,32,64,640]{3,2,1,0:T(8,128)(2,1)} %bitcast.42), kind=kLoop, calls=%fused_computation.31 | loop fusion | flops 5242880 | bytes 20971584 | tf_op jit(solution)/shard_map/jit(_take)/select_n | solution.py:130
  409.5 12.7 %concatenate.36 = bf16[2,2048,5,128]{3,2,1,0:T(8,128)(2,1)} reshape(bf16[2,32,64,640]{3,2,1,0:T(8,128)(2,1)} %get-tuple-element.15) | data formatting | bytes 10485760 | tf_op jit(solution)/shard_map/concatenate | solution.py:148
  422.1 6.6 %copy.79 = bf16[2,2048,5,128]{3,1,2,0:T(8,128)(2,1)} copy(bf16[2,2048,5,128]{3,2,1,0:T(8,128)(2,1)} %concatenate.36) | data formatting | bytes 10485760 | tf_op jit(solution)/shard_map/concatenate | solution.py:148
  428.8 12.7 %concatenate.42 = bf16[2,2048,5,128]{3,2,1,0:T(8,128)(2,1)} reshape(bf16[2,32,64,640]{3,2,1,0:T(8,128)(2,1)} %get-tuple-element.16) | data formatting | bytes 10485760 | tf_op jit(solution)/shard_map/concatenate | solution.py:149
  441.5 6.7 %copy.89 = bf16[2,2048,5,128]{3,1,2,0:T(8,128)(2,1)} copy(bf16[2,2048,5,128]{3,2,1,0:T(8,128)(2,1)} %concatenate.42) | data formatting | bytes 10485760 | tf_op jit(solution)/shard_map/concatenate | solution.py:149
  448.1 6.0 %convolution_convert_fusion.1 = bf16[256,640]{1,0:T(8,128)(2,1)S(1)} fusion(bf16[256,5120]{1,0:T(8,128)(2,1)} %all-gather.5.cloned.1.call-done, bf16[5120,640]{1,0:T(8,128)(2,1)} %all-gather.9.cloned.1.call-done), kind=kOutput, calls=%fused_computation.35 | convolution fusion | flops 1677885440 | bytes 9502720 | tf_op jit(solution)/shard_map/dot_general | solution.py:75
  454.2 1.3 collective-permute-start
  455.5 5.9 %convolution_convert_fusion = bf16[256,640]{1,0:T(8,128)(2,1)S(1)} fusion(bf16[256,5120]{1,0:T(8,128)(2,1)} %all-gather.5.cloned.1.call-done, bf16[5120,640]{1,0:T(8,128)(2,1)} %all-gather.11.cloned.1.call-done), kind=kOutput, calls=%fused_computation.34 | convolution fusion | flops 1677885440 | bytes 9502720 | tf_op jit(solution)/shard_map/dot_general | solution.py:75
  461.4 3.2 collective-permute-start.1
  464.7 5.9 %convolution_convert_fusion.2 = bf16[256,640]{1,0:T(8,128)(2,1)S(1)} fusion(bf16[256,5120]{1,0:T(8,128)(2,1)} %all-gather.5.cloned.1.call-done, bf16[5120,640]{1,0:T(8,128)(2,1)} %all-gather.7.cloned.1.call-done), kind=kOutput, calls=%fused_computation.36 | convolution fusion | flops 1677885440 | bytes 9502720 | tf_op jit(solution)/shard_map/dot_general | solution.py:75
  470.5 0.4 reshape.235
  470.9 0.4 reshape.236
  471.3 0.2 copy.75
  471.5 0.2 copy.77
  471.7 0.4 reshape.234
  472.1 0.2 copy.85
  472.2 0.8 copy.87
  473.1 0.2 copy.74
  473.3 0.2 copy.76
  473.5 0.2 copy.84
  473.6 0.2 copy.86
  473.8 15.8 %fusion.59 = (f32[2,5,128]{2,1,0:T(8,128)S(1)}, bf16[2,5,128,2304]{3,2,1,0:T(8,128)(2,1)}) fusion(pred[2,128,2304]{2,1,0:T(8,128)(4,1)S(1)} %pad_add_fusion, bf16[2,128,5,128]{3,1,2,0:T(8,128)(2,1)S(1)} %copy.80, bf16[1,128,5,128]{3,1,2,0:T(8,128)(2,1)S(1)} %copy.77, bf16[1,128,5,128]{3,1,2,0:T(8,128)(2,1)S(1)} %copy.76, ...), kind=kOutput, calls=%fused_computation.78 | convolution fusion | flops 796264704 | bytes 12719104 | tf_op jit(solution)/shard_map/sub | solution.py:30
  489.6 6.0 %fusion.32 = bf16[2,128,5,128]{3,1,2,0:T(8,128)(2,1)S(1)} fusion(bf16[2,128,5,128]{3,1,2,0:T(8,128)(2,1)S(1)} %copy.90, bf16[1,128,5,128]{3,1,2,0:T(8,128)(2,1)S(1)} %copy-done.2, bf16[1,128,5,128]{3,1,2,0:T(8,128)(2,1)S(1)} %copy.86, bf16[2,2048,5,128]{3,1,2,0:T(8,128)(2,1)} %copy.89, bf16[2,5,128,2304]{3,2,1,0:T(8,128)(2,1)} %get-tuple-element.20, ...), kind=kOutput, calls=%fused_computation.38 | convolution fusion | flops 778895360 | bytes 12129280 | tf_op jit(solution)/shard_map/chqk,ckhd->chqd/dot_general | solution.py:32
  495.6 0.2 copy.99
  495.9 0.8 copy.112
  (40 shorter events, 1.2 us)
Async XLA Ops:
  6.5 20.7 %copy-start = (bf16[32,64,640]{2,1,0:T(8,128)(2,1)S(1)}, bf16[32,64,640]{2,1,0:T(8,128)(2,1)}, u32[]{:S(2)}) copy-start(bf16[32,64,640]{2,1,0:T(8,128)(2,1)} %param.17) | copy-start | bytes 7864324
  6.5 441.6 %all-gather.5.cloned.1.call-start = ((), (), s32[]{:S(2)}) async-start(), calls=%async_computation.3 | async-start | bytes 2949120 | tf_op jit(solution)/shard_map/all_gather | solution.py:65
  7.3 440.9 %all-gather.9.cloned.1.call-start = ((), (), s32[]{:S(2)}) async-start(), calls=%async_computation.5 | async-start | bytes 6963200 | tf_op jit(solution)/shard_map/all_gather | solution.py:70
  8.0 447.5 %all-gather.11.cloned.1.call-start = ((), (), s32[]{:S(2)}) async-start(), calls=%async_computation.6 | async-start | bytes 6963200 | tf_op jit(solution)/shard_map/all_gather | solution.py:71
  205.7 187.1 %all-to-all-start.2 = ((bf16[16,8,64,640]{3,2,1,0:T(8,128)(2,1)}), bf16[16,8,64,640]{3,2,1,0:T(8,128)(2,1)}, u32[]{:S(2)}, u32[]{:S(2)}) async-start(bf16[16,8,64,640]{3,2,1,0:T(8,128)(2,1)} %get-tuple-element.14), calls=%async_computation.2 | async-start | bytes 20971520 | tf_op jit(solution)/shard_map/all_to_all | solution.py:120
  210.5 254.1 %all-gather.7.cloned.1.call-start = ((), (), s32[]{:S(2)}) async-start(), calls=%async_computation.4 | async-start | bytes 6963200 | tf_op jit(solution)/shard_map/all_gather | solution.py:69
  454.2 19.0 %collective-permute-start = (bf16[128,640]{1,0:T(8,128)(2,1)S(1)}, bf16[128,640]{1,0:T(8,128)(2,1)S(1)}, u32[]{:S(2)}, u32[]{:S(2)}) collective-permute-start(bf16[128,640]{1,0:T(8,128)(2,1)S(1)} %get-tuple-element.9), channel_id=1, source_target_pairs={{0,1},{1,2},{2,3},{3,4},{4,5},{5,6},{6,7},{7,8},{8,9},{9,10},{10,1... | collective-permute-start | bytes 491528 | tf_op jit(solution)/shard_map/ppermute | solution.py:15
  461.4 12.1 %collective-permute-start.1 = (bf16[128,640]{1,0:T(8,128)(2,1)S(1)}, bf16[128,640]{1,0:T(8,128)(2,1)S(1)}, u32[]{:S(2)}, u32[]{:S(2)}) collective-permute-start(bf16[128,640]{1,0:T(8,128)(2,1)S(1)} %get-tuple-element.11), channel_id=1, source_target_pairs={{0,1},{1,2},{2,3},{3,4},{4,5},{5,6},{6,7},{7,8},{8,9},{9,10},{10,1... | collective-permute-start | bytes 491528 | tf_op jit(solution)/shard_map/ppermute | solution.py:15
  473.8 15.8 %copy-start.2 = (bf16[1,128,5,128]{3,1,2,0:T(8,128)(2,1)S(1)}, bf16[1,128,5,128]{3,1,2,0:T(8,128)(2,1)}, u32[]{:S(2)}) copy-start(bf16[1,128,5,128]{3,1,2,0:T(8,128)(2,1)} %copy.87) | copy-start | bytes 491524
  489.6 7.1 %copy-start.1 = (bf16[32,64,640]{2,1,0:T(8,128)(2,1)S(1)}, bf16[32,64,640]{2,1,0:T(8,128)(2,1)}, u32[]{:S(2)}) copy-start(bf16[32,64,640]{2,1,0:T(8,128)(2,1)} %param.17) | copy-start | bytes 7864324
Sparse Core Ops, SparseCore 0:
  9.0 28.9 all-gather.4
  40.2 160.6 all-gather.8
  203.0 187.3 all-gather.10
  392.4 66.9 all-gather.6
where the time goes:
time: 507 us; the launch traced here: 503 us
  waiting for transfers between devices  175 us (35%)
  blocking collectives  163 us (32%)
  local copies, waits for them, and re-layouts  77.1 us (15%)
  matrix products  39.5 us (8%)
  other arithmetic  24.6 us (5%)
  between operations  13.4 us (3%)
  starting transfers between devices  9.66 us (2%)
    all_to_all x1, waiting for transfers between devices, shards(): lax.all_to_all(jnp.take(cache_values, rows_used, axis=0), 'context', spli...  173 us
    all_to_all x1, blocking collectives, shards(): lax.all_to_all(jnp.take(cache_keys, rows_used, axis=0), 'context', split_...  148 us
    concatenate x4, local copies, waits for them, and re-layouts, shards(): jnp.concatenate([far_values, local_values], 1)  19.8 us
    concatenate x4, local copies, waits for them, and re-layouts, shards(): jnp.concatenate([far_keys, local_keys], 1)  19.7 us
    dot_general x3, matrix products, shards(): jnp.dot(features_all, weight_piece, preferred_element_type=jnp.float32)  17.7 us
    sub x1, matrix products, attend_block(): weights = jnp.where(opened, jnp.exp(masked - highest[..., None]), 0.0)  15.8 us
    all_to_all x1, blocking collectives, shards(): lax.all_to_all(wanted, 'context', split_axis=0, concat_axis=0, tiled=True)  15.4 us
    select_n x2, other arithmetic, shards(): jnp.take(cache_keys, rows_used, axis=0)  13.3 us
  transfers between devices with their start and end apart: 7, of which 1 were waited for; matrix products, arithmetic and copies ran while one was open for 23% of the time, Pallas kernels for 0%

commit v1 on v0

v1 whole, which is shorter than its diff:
```python
import functools

import jax
import jax.numpy as jnp
from jax import lax
from jax.experimental import pallas as pl
from jax.experimental.pallas import tpu as pltpu
from jax.sharding import PartitionSpec as P

HDIM = 128
NEG = -1e30
SCALE = HDIM ** (-0.5) * 1.4426950408889634


def dot_nt(a, b):
    return lax.dot_general(a, b, (((1,), (1,)), ((), ())), preferred_element_type=jnp.float32)


def dot_tn(a, b):
    return lax.dot_general(a, b, (((0,), (0,)), ((), ())), preferred_element_type=jnp.float32)


def owner_kernel(heads, cap, rows_ref, n_ref, q_ref, k_ref, v_ref, o_ref, st_ref, acc_ref):
    src = pl.program_id(0)
    span_count = o_ref.shape[1]
    span = q_ref.shape[1] // span_count
    block = k_ref.shape[1]
    for half in range(span_count):
        c = src * span_count + half
        n = n_ref[c]
        rows = slice(half * span, (half + 1) * span)

        def pair(j, first):
            r0 = rows_ref[c * cap + 2 * j]
            r1 = rows_ref[c * cap + jnp.minimum(2 * j + 1, cap - 1)]
            bias = jnp.where(2 * j + 1 < n, 0.0, NEG)
            for h in range(heads):
                cols = slice(h * HDIM, (h + 1) * HDIM)
                q = q_ref[0, rows, cols]
                k = jnp.concatenate([k_ref[r0, :, cols], k_ref[r1, :, cols]], 0)
                v = jnp.concatenate([v_ref[r0, :, cols], v_ref[r1, :, cols]], 0)
                s = dot_nt(k, q) * SCALE
                s = jnp.concatenate([s[:block], s[block:] + bias], 0)
                m = jnp.max(s, axis=0, keepdims=True)
                if not first:
                    old = st_ref[0, half, h : h + 1, :]
                    m = jnp.maximum(m, old)
                    decay = jnp.exp2(old - m)
                p = jnp.exp2(s - m)
                l = jnp.sum(p, axis=0, keepdims=True)
                a = dot_tn(v, p.astype(jnp.bfloat16))
                if not first:
                    l = l + st_ref[0, half, 8 + h : 9 + h, :] * decay
                    a = a + acc_ref[cols, :] * decay
                st_ref[0, half, h : h + 1, :] = m
                st_ref[0, half, 8 + h : 9 + h, :] = l
                acc_ref[cols, :] = a

        @pl.when(n == 0)
        def _():
            o_ref[0, half] = jnp.zeros_like(o_ref[0, half])
            st_ref[0, half, 0:8, :] = jnp.full_like(st_ref[0, half, 0:8, :], NEG)
            st_ref[0, half, 8:16, :] = jnp.zeros_like(st_ref[0, half, 8:16, :])

        @pl.when(n > 0)
        def _():
            pair(0, True)

            @pl.loop(1, (n + 1) // 2)
            def _(j):
                pair(j, False)

            for h in range(heads):
                cols = slice(h * HDIM, (h + 1) * HDIM)
                o_ref[0, half, cols, :] = (
                    acc_ref[cols, :] / st_ref[0, half, 8 + h : 9 + h, :]
                ).astype(jnp.bfloat16)


def owner_attention(rows, n, q_all, cache_keys, cache_values, heads, cap):
    devices, tokens, width = q_all.shape
    span_count = n.shape[0] // devices
    span = tokens // span_count
    whole = pl.BlockSpec(cache_keys.shape, lambda s, *_: (0, 0, 0), pipeline_mode=pl.Buffered(1))
    return pl.pallas_call(
        functools.partial(owner_kernel, heads, cap),
        grid_spec=pltpu.PrefetchScalarGridSpec(
            num_scalar_prefetch=2,
            grid=(devices,),
            in_specs=[
                pl.BlockSpec((1, tokens, width), lambda s, *_: (s, 0, 0)),
                whole,
                whole,
            ],
            out_specs=[
                pl.BlockSpec((1, span_count, width, span), lambda s, *_: (s, 0, 0, 0)),
                pl.BlockSpec((1, span_count, 16, span), lambda s, *_: (s, 0, 0, 0)),
            ],
            scratch_shapes=[pltpu.VMEM((width, span), jnp.float32)],
        ),
        out_shape=[
            jax.ShapeDtypeStruct((devices, span_count, width, span), jnp.bfloat16),
            jax.ShapeDtypeStruct((devices, span_count, 16, span), jnp.float32),
        ],
    )(rows, n, q_all, cache_keys, cache_values)


def local_kernel(heads, first_ref, q_ref, pk_ref, pv_ref, k_ref, v_ref, o_ref, st_ref, out_ref):
    half = pl.program_id(0)
    span = q_ref.shape[0]
    bias = jnp.where((first_ref[0] + half) > 0, 0.0, NEG)
    key = lax.broadcasted_iota(jnp.int32, (span, span), 0)
    row = lax.broadcasted_iota(jnp.int32, (span, span), 1)
    for h in range(heads):
        cols = slice(h * HDIM, (h + 1) * HDIM)
        q = q_ref[:, cols]
        s0 = dot_nt(pk_ref[0, :, cols], q) * SCALE + bias
        s1 = jnp.where(key <= row, dot_nt(k_ref[:, cols], q) * SCALE, NEG)
        far_m = st_ref[:, 0, h, :]
        far_l = st_ref[:, 0, 8 + h, :]
        m = jnp.maximum(
            jnp.maximum(jnp.max(s0, axis=0, keepdims=True), jnp.max(s1, axis=0, keepdims=True)),
            jnp.max(far_m, axis=0, keepdims=True),
        )
        p0 = jnp.exp2(s0 - m)
        p1 = jnp.exp2(s1 - m)
        w = far_l * jnp.exp2(far_m - m)
        total = (
            jnp.sum(p0, axis=0, keepdims=True)
            + jnp.sum(p1, axis=0, keepdims=True)
            + jnp.sum(w, axis=0, keepdims=True)
        )
        a = dot_tn(pv_ref[0, :, cols], p0.astype(jnp.bfloat16))
        a = a + dot_tn(v_ref[:, cols], p1.astype(jnp.bfloat16))
        for i in range(o_ref.shape[0]):
            a = a + o_ref[i, 0, cols, :].astype(jnp.float32) * w[i : i + 1, :]
        out_ref[:, cols] = jnp.transpose(a / total).astype(out_ref.dtype)


def local_attention(first, q, prior_k, prior_v, k, v, o, st, heads):
    devices, span_count, width, span = o.shape
    rows = pl.BlockSpec((span, width), lambda c, *_: (c, 0))
    before = pl.BlockSpec((1, span, width), lambda c, *_: (c, 0, 0))
    return pl.pallas_call(
        functools.partial(local_kernel, heads),
        grid_spec=pltpu.PrefetchScalarGridSpec(
            num_scalar_prefetch=1,
            grid=(span_count,),
            in_specs=[
                rows,
                before,
                before,
                rows,
                rows,
                pl.BlockSpec((devices, 1, width, span), lambda c, *_: (0, c, 0, 0)),
                pl.BlockSpec((devices, 1, 16, span), lambda c, *_: (0, c, 0, 0)),
            ],
            out_specs=rows,
        ),
        out_shape=jax.ShapeDtypeStruct(q.shape, jnp.bfloat16),
    )(first, q, prior_k, prior_v, k, v, o, st)


def from_behind(block, axis, distance):
    devices = range(lax.axis_size(axis))
    route = [(i - distance, i) for i in devices if i - distance in devices]
    return lax.ppermute(block, axis, route)


def owner_table(selected, counts, block_slot, stored, cap):
    select_count = selected.shape[1]
    live = jnp.arange(select_count)[None, :] < counts[:, None]
    hit = selected[:, :, None] == jnp.arange(block_slot.shape[0])[None, None, :]
    slot = jnp.sum(jnp.where(hit, block_slot[None, None, :], 0), axis=2)
    slot = jnp.where(live, slot, -1).astype(jnp.int32)
    slots = lax.all_gather(slot, "context", axis=0, tiled=True)
    low = lax.axis_index("context") * stored
    mine = (slots >= low) & (slots < low + stored)
    position = jnp.arange(select_count)
    earlier = position[None, :] < position[:, None]
    rank = jnp.sum(jnp.where(mine[:, None, :] & earlier[None], 1, 0), axis=2)
    place = mine[:, :, None] & (rank[:, :, None] == jnp.arange(cap)[None, None, :])
    rows = jnp.sum(jnp.where(place, (slots - low)[:, :, None], 0), axis=1)
    return rows.reshape(-1).astype(jnp.int32), jnp.sum(mine, axis=1).astype(jnp.int32)


def shards(
    tokens,
    query_weight,
    key_weight,
    value_weight,
    cache_keys,
    cache_values,
    selected,
    counts,
    block_slot,
):
    token_count = tokens.shape[0]
    width = query_weight.shape[1]
    heads = width // HDIM
    span_count, select_count = selected.shape
    devices = lax.axis_size("context")
    cap = max(2, 2 * span_count * select_count // devices)
    span = token_count // span_count

    features = lax.all_gather(tokens, "tensor", axis=1, tiled=True)

    def project(weight):
        whole = lax.all_gather(weight, "context", axis=0, tiled=True)
        return jnp.dot(features, whole, preferred_element_type=jnp.float32).astype(jnp.bfloat16)

    q = project(query_weight)
    q_all = lax.all_gather(q, "context", axis=0, tiled=False)
    rows, n = owner_table(selected, counts, block_slot, cache_keys.shape[0], cap)
    o, st = owner_attention(rows, n, q_all, cache_keys, cache_values, heads, cap)
    o = lax.all_to_all(o, "context", split_axis=0, concat_axis=0, tiled=True)
    st = lax.all_to_all(st, "context", split_axis=0, concat_axis=0, tiled=True)
    k = project(key_weight)
    v = project(value_weight)
    last = token_count - span
    before_k, before_v = from_behind((k[last:], v[last:]), "context", 1)

    def prior(before, own):
        return jnp.concatenate([before, own[:last]], 0).reshape(span_count, span, width)

    first = (lax.axis_index("context") * span_count).astype(jnp.int32).reshape(1)
    return local_attention(first, q, prior(before_k, k), prior(before_v, v), k, v, o, st, heads)


def solution(mesh):
    placed = (
        P("context", "tensor"),
        P("context", "tensor"),
        P("context", "tensor"),
        P("context", "tensor"),
        P("context", None, "tensor"),
        P("context", None, "tensor"),
        P("context", None),
        P("context"),
        P(),
    )
    return jax.shard_map(
        shards, mesh=mesh, in_specs=placed, out_specs=P("context", "tensor"), check_vma=False
    )
```

time: 507 us -> 377 us (0.74)
  blocking collectives: 163 us -> 47.8 us
  local copies, waits for them, and re-layouts: 77.1 us -> 0.79 us
  waiting for transfers between devices: 175 us -> 228 us
  Pallas kernels: 0 us -> 50.2 us
  matrix products: 39.5 us -> 18.3 us
  other arithmetic: 24.6 us -> 3.75 us
    all_gather x4 -> x5, waiting for transfers between devices: 0.04 us -> 222 us  [the longest x3 163 us: project(): whole = lax.all_gather(weight, 'context', axis=0, tiled=True)]
    all_to_all x1, waiting for transfers between devices: 173 us -> 0.01 us  [shards(): o = lax.all_to_all(o, 'context', split_axis=0, concat_axis=0, tiled=True)]
    all_to_all x2 -> x1, blocking collectives: 163 us -> 24.8 us  [shards(): st = lax.all_to_all(st, 'context', split_axis=0, concat_axis=0, tiled=True)]
    pallas_call x0 -> x2, Pallas kernels: none -> 50.2 us  [the longest x1 44.4 us: owner_attention(): pl.pallas_call(functools.partial(owner_kernel, heads, cap), grid_spec=plt...]
    concatenate x12 -> x0, local copies, waits for them, and re-layouts: 40.8 us -> none  [the longest x4 19.8 us: shards(): jnp.concatenate([far_values, local_values], 1)]
    gather x4 -> x0, local copies, waits for them, and re-layouts: 32.2 us -> none  [the longest x1 9.33 us: shards(): jnp.take(cache_values, rows_used, axis=0)]
    all_gather x0 -> x1, blocking collectives: none -> 23 us  [owner_table(): slots = lax.all_gather(slot, 'context', axis=0, tiled=True)]
    select_n x4 -> x0, other arithmetic: 22.5 us -> none  [the longest x2 13.3 us: shards(): jnp.take(cache_keys, rows_used, axis=0)]
  transfers between devices with their start and end apart: 7 -> 8, of which waited for: 1 -> 5; matrix products, arithmetic and copies ran while one was open for 23% -> 4% of each run, Pallas kernels for 0% -> 12%
where the time goes in v1:
time: 377 us; the launch traced here: 371 us
  waiting for transfers between devices  228 us (60%)
  Pallas kernels  50.2 us (13%)
  blocking collectives  47.8 us (13%)
  matrix products  18.3 us (5%)
  between operations  13.3 us (4%)
  starting transfers between devices  9.71 us (3%)
    all_gather x3, waiting for transfers between devices, project(): whole = lax.all_gather(weight, 'context', axis=0, tiled=True)  163 us
    pallas_call x1, Pallas kernels, owner_attention(): pl.pallas_call(functools.partial(owner_kernel, heads, cap), grid_spec=plt...  44.4 us
    all_gather x1, waiting for transfers between devices, shards(): features = lax.all_gather(tokens, 'tensor', axis=1, tiled=True)  29.9 us
    all_gather x1, waiting for transfers between devices, shards(): q_all = lax.all_gather(q, 'context', axis=0, tiled=False)  29 us
    all_to_all x1, blocking collectives, shards(): st = lax.all_to_all(st, 'context', split_axis=0, concat_axis=0, tiled=True)  24.8 us
    all_gather x1, blocking collectives, owner_table(): slots = lax.all_gather(slot, 'context', axis=0, tiled=True)  23 us
    dot_general x3, matrix products, project(): jnp.dot(features, whole, preferred_element_type=jnp.float32)  18.3 us
  transfers between devices with their start and end apart: 8, of which 5 were waited for; matrix products, arithmetic and copies ran while one was open for 4% of the time, Pallas kernels for 12%

profile of v1, /device:TPU:0, one launch (start us, length us, event | category | flops | bytes accessed | tf_op | source)
XLA Modules:
  0.0 371.5 jit_solution(18444989805864086169)
XLA Ops:
  6.5 0.0 all-gather.8.cloned.1.call-start
  6.5 0.7 all-gather.8.cloned.1.call-update
  7.3 0.0 all-gather.10.cloned.1.call-start
  7.3 0.7 all-gather.10.cloned.1.call-update
  8.0 0.0 copy-start.2
  8.0 0.0 copy-start.3
  8.0 0.0 copy-start.4
  8.0 0.0 all-gather.16.cloned.1.call-start
  8.1 29.9 %all-gather.8.cloned.1.call-done = bf16[256,5120]{1,0:T(8,128)(2,1)} async-done(((bf16[256,640]{1,0:T(8,128)(2,1)}), bf16[256,5120]{1,0:T(8,128)(2,1)}) %all-gather.8.cloned.1.call-update) | async-done | bytes 2621456 | tf_op jit(solution)/shard_map/all_gather | solution.py:206
  38.0 65.1 %all-gather.10.cloned.1.call-done = bf16[5120,640]{1,0:T(8,128)(2,1)} async-done(((bf16[320,640]{1,0:T(8,128)(2,1)}), bf16[5120,640]{1,0:T(8,128)(2,1)}) %all-gather.10.cloned.1.call-update) | async-done | bytes 6553616 | tf_op jit(solution)/shard_map/all_gather | solution.py:209
  103.2 6.6 %convolution_convert_fusion.2.q_ref = bf16[256,640]{1,0:T(8,128)(2,1)} fusion(bf16[256,5120]{1,0:T(8,128)(2,1)} %all-gather.8.cloned.1.call-done, bf16[5120,640]{1,0:T(8,128)(2,1)} %all-gather.10.cloned.1.call-done), kind=kOutput, calls=%fused_computation.2 | convolution fusion | flops 1677885440 | bytes 9502720 | tf_op jit(solution)/shard_map/dot_general | solution.py:210
  109.8 0.0 all-gather.16.cloned.1.call-update
  109.8 0.0 all-gather.12.cloned.1.call-start
  109.8 0.5 all-gather.12.cloned.1.call-update
  110.4 0.0 all-gather.14.cloned.1.call-start
  110.4 0.5 all-gather.14.cloned.1.call-update
  110.9 0.0 copy-done.2
  111.0 0.0 copy-done.3
  111.0 0.2 select_reduce_fusion.2
  111.2 0.0 copy-done.4
  111.2 0.1 fusion.1
  111.2 23.0 %all-gather.1 = s32[16,2,32]{2,1,0:T(2,128)S(1)} all-gather(s32[1,2,32]{2,1,0:T(2,128)S(1)} %fusion.1), channel_id=1, replica_groups=mesh['tensor'=8,'context'=16] {'context'}, dimensions={0}, use_global_device_ids=true | all-gather | bytes 4352 | tf_op jit(solution)/shard_map/all_gather | solution.py:176
  134.3 0.6 select_reduce_fusion
  134.9 0.6 select_reduce_fusion.1
  135.6 0.7 reshape.34.rows_ref
  136.2 0.7 convert_reduce_fusion.n_ref
  136.9 29.0 %all-gather.16.cloned.1.call-done = bf16[4096,640]{1,0:T(8,128)(2,1)} async-done(((bf16[256,640]{1,0:T(8,128)(2,1)}), bf16[4096,640]{1,0:T(8,128)(2,1)}) %all-gather.16.cloned.1.call-update) | async-done | bytes 5242896 | tf_op jit(solution)/shard_map/all_gather | solution.py:213
  166.0 44.4 %shard_map.91 = (bf16[16,2,640,128]{3,2,1,0:T(8,128)(2,1)}, f32[16,2,16,128]{3,2,1,0:T(8,128)}) custom-call(s32[256]{0:T(256)} %reshape.34.rows_ref, s32[32]{0:T(128)} %convert_reduce_fusion.n_ref, bf16[16,256,640]{2,1,0:T(8,128)(2,1)} %bitcast.15, bf16[32,64,640]{2,1,0:T(8,128)(2,1)} %k_ref.1, bf16[32,64,640]{2,1,0:T(8,128)(2,1)} %v_ref.1), custom_call_target="tpu_custom_call" | custom-call | tf_op jit(solution)/shard_map/pallas_call | solution.py:85
  210.4 24.8 %all_to_all.10.st_ref = f32[16,2,16,128]{3,2,1,0:T(8,128)} all-to-all(f32[16,2,16,128]{3,2,1,0:T(8,128)} %get-tuple-element.8), channel_id=1, replica_groups=mesh['tensor'=8,'context'=16] {'context'}, dimensions={0} | all-to-all | bytes 524288 | tf_op jit(solution)/shard_map/all_to_all | solution.py:217
  235.1 4.6 %all-to-all-start = ((bf16[16,2,640,128]{3,2,1,0:T(8,128)(2,1)}), bf16[16,2,640,128]{3,2,1,0:T(8,128)(2,1)}, u32[]{:S(2)}, u32[]{:S(2)}) async-start(bf16[16,2,640,128]{3,2,1,0:T(8,128)(2,1)} %get-tuple-element.7), calls=%async_computation | async-start | bytes 10485760 | tf_op jit(solution)/shard_map/all_to_all | solution.py:216
  239.7 0.0 all-gather.12.cloned.1.call-done
  239.8 5.9 %convolution_convert_fusion.1.k_ref = bf16[256,640]{1,0:T(8,128)(2,1)S(1)} fusion(bf16[256,5120]{1,0:T(8,128)(2,1)} %all-gather.8.cloned.1.call-done, bf16[5120,640]{1,0:T(8,128)(2,1)} %all-gather.12.cloned.1.call-done), kind=kOutput, calls=%fused_computation.1 | convolution fusion | flops 1677885440 | bytes 9502720 | tf_op jit(solution)/shard_map/dot_general | solution.py:210
  245.6 0.0 copy-start
  245.7 3.7 collective-permute-start
  249.3 98.1 %all-gather.14.cloned.1.call-done = bf16[5120,640]{1,0:T(8,128)(2,1)} async-done(((bf16[320,640]{1,0:T(8,128)(2,1)}), bf16[5120,640]{1,0:T(8,128)(2,1)}) %all-gather.14.cloned.1.call-update) | async-done | bytes 6553616 | tf_op jit(solution)/shard_map/all_gather | solution.py:209
  347.5 5.9 %convolution_convert_fusion.v_ref = bf16[256,640]{1,0:T(8,128)(2,1)S(1)} fusion(bf16[256,5120]{1,0:T(8,128)(2,1)} %all-gather.8.cloned.1.call-done, bf16[5120,640]{1,0:T(8,128)(2,1)} %all-gather.14.cloned.1.call-done), kind=kOutput, calls=%fused_computation | convolution fusion | flops 1677885440 | bytes 9502720 | tf_op jit(solution)/shard_map/dot_general | solution.py:210
  353.3 0.0 copy-done
  353.3 0.0 copy-start.1
  353.4 1.3 collective-permute-start.1
  354.7 0.0 collective-permute-done
  354.7 0.8 pad_maximum_fusion
  355.5 3.0 collective-permute-done.1
  358.5 0.7 pad_maximum_fusion.1
  359.2 0.0 all-to-all-done.o_ref
  359.2 0.0 copy-done.1
  359.2 5.8 %shard_map.92 = bf16[256,640]{1,0:T(8,128)(2,1)} custom-call(s32[1]{0:T(128)} %bitcast.first_ref, bf16[256,640]{1,0:T(8,128)(2,1)} %convolution_convert_fusion.2.q_ref, bf16[2,128,640]{2,1,0:T(8,128)(2,1)} %bitcast.16, bf16[2,128,640]{2,1,0:T(8,128)(2,1)} %bitcast.17, bf16[256,640]{1,0:T(8,128)(2,1)} %copy-done, bf16[256,640]{1,0:T(8,128)(2,1)} %copy-done.1, ...), custom_call_target="tpu_custom_call" | custom-call | tf_op jit(solution)/shard_map/pallas_call | solution.py:144
  (6 shorter events, 0.1 us)
Async XLA Ops:
  6.5 31.5 %all-gather.8.cloned.1.call-start = ((), (), s32[]{:S(2)}) async-start(), calls=%async_computation.2 | async-start | bytes 2949120 | tf_op jit(solution)/shard_map/all_gather | solution.py:206
  7.3 95.9 %all-gather.10.cloned.1.call-start = ((), (), s32[]{:S(2)}) async-start(), calls=%async_computation.3 | async-start | bytes 6963200 | tf_op jit(solution)/shard_map/all_gather | solution.py:209
  8.0 102.9 %copy-start.2 = (s32[512]{0:T(512)S(1)}, s32[512]{0:T(512)}, u32[]{:S(2)}) copy-start(s32[512]{0:T(512)} %param.17) | copy-start | bytes 6148
  8.0 102.9 %copy-start.3 = (s32[2,32]{1,0:T(2,128)S(1)}, s32[2,32]{1,0:T(2,128)}, u32[]{:S(2)}) copy-start(s32[2,32]{1,0:T(2,128)} %param.15) | copy-start | bytes 772
  8.0 103.1 %copy-start.4 = (s32[2]{0:T(128)S(1)}, s32[2]{0:T(128)}, u32[]{:S(2)}) copy-start(s32[2]{0:T(128)} %param.16) | copy-start | bytes 28
  8.0 157.9 %all-gather.16.cloned.1.call-start = ((), (), s32[]{:S(2)}) async-start(), calls=%async_computation.6 | async-start | bytes 5570560 | tf_op jit(solution)/shard_map/all_gather | solution.py:213
  109.8 130.0 %all-gather.12.cloned.1.call-start = ((), (), s32[]{:S(2)}) async-start(), calls=%async_computation.4 | async-start | bytes 6963200 | tf_op jit(solution)/shard_map/all_gather | solution.py:209
  110.4 237.1 %all-gather.14.cloned.1.call-start = ((), (), s32[]{:S(2)}) async-start(), calls=%async_computation.5 | async-start | bytes 6963200 | tf_op jit(solution)/shard_map/all_gather | solution.py:209
  235.1 124.1 %all-to-all-start = ((bf16[16,2,640,128]{3,2,1,0:T(8,128)(2,1)}), bf16[16,2,640,128]{3,2,1,0:T(8,128)(2,1)}, u32[]{:S(2)}, u32[]{:S(2)}) async-start(bf16[16,2,640,128]{3,2,1,0:T(8,128)(2,1)} %get-tuple-element.7), calls=%async_computation | async-start | bytes 10485760 | tf_op jit(solution)/shard_map/all_to_all | solution.py:216
  245.6 107.7 %copy-start = (bf16[256,640]{1,0:T(8,128)(2,1)}, bf16[256,640]{1,0:T(8,128)(2,1)S(1)}, u32[]{:S(2)}) copy-start(bf16[256,640]{1,0:T(8,128)(2,1)S(1)} %convolution_convert_fusion.1.k_ref) | copy-start | bytes 983044
  245.7 109.0 %collective-permute-start = (bf16[128,640]{1,0:T(8,128)(2,1)S(1)}, bf16[128,640]{1,0:T(8,128)(2,1)S(1)}, u32[]{:S(2)}, u32[]{:S(2)}) collective-permute-start(bf16[128,640]{1,0:T(8,128)(2,1)S(1)} %get-tuple-element.11), channel_id=1, source_target_pairs={{0,1},{1,2},{2,3},{3,4},{4,5},{5,6},{6,7},{7,8},{8,9},{9,10},{10,1... | collective-permute-start | bytes 491528 | tf_op jit(solution)/shard_map/ppermute | solution.py:167
  353.3 5.9 %copy-start.1 = (bf16[256,640]{1,0:T(8,128)(2,1)}, bf16[256,640]{1,0:T(8,128)(2,1)S(1)}, u32[]{:S(2)}) copy-start(bf16[256,640]{1,0:T(8,128)(2,1)S(1)} %convolution_convert_fusion.v_ref) | copy-start | bytes 983044
  353.4 5.1 %collective-permute-start.1 = (bf16[128,640]{1,0:T(8,128)(2,1)S(1)}, bf16[128,640]{1,0:T(8,128)(2,1)S(1)}, u32[]{:S(2)}, u32[]{:S(2)}) collective-permute-start(bf16[128,640]{1,0:T(8,128)(2,1)S(1)} %get-tuple-element.9), channel_id=1, source_target_pairs={{0,1},{1,2},{2,3},{3,4},{4,5},{5,6},{6,7},{7,8},{8,9},{9,10},{10,1... | collective-permute-start | bytes 491528 | tf_op jit(solution)/shard_map/ppermute | solution.py:167
Sparse Core Ops, SparseCore 0:
  9.0 28.9 all-gather.7
  40.2 62.9 all-gather.9
  109.9 56.0 all-gather.15
  168.0 64.8 all-gather.11
  234.9 112.5 all-gather.13

commit v2 on v1

--- a/solution.py
+++ b/solution.py
@@ -9,6 +9,8 @@
 
 HDIM = 128
 NEG = -1e30
+MESH = pl.DeviceIdType.MESH
+EXTRA = 16
 SCALE = HDIM ** (-0.5) * 1.4426950408889634
 
 
@@ -18,12 +20,289 @@
 
 def dot_tn(a, b):
     return lax.dot_general(a, b, (((0,), (0,)), ((), ())), preferred_element_type=jnp.float32)
+
+
+RING = 4
+OFFSETS = (0, -1, 1, 2)
+
+
+def halves(total, extra):
+    half = (total - extra) // 2
+    part = half // 2
+    first = ((0, half), (0, part), (part, half - part))
+    second = ((half, half + extra), (half, part), (half + part, half - part + extra))
+    return (first, second)
+
+
+class ContextGather:
+    def __init__(self, buf, ranges, send, recv, zpos, xpos):
+        self.buf, self.ranges, self.send, self.recv = buf, ranges, send, recv
+        self.zpos, self.xpos = zpos, xpos
+        self.waited, self.sent = set(), []
+
+    def on_x(self, half, phase):
+        return (half == 0) == (phase == 0)
+
+    def chunk(self, half, phase, step):
+        first = 0 if phase == 0 else OFFSETS[phase - 1]
+        if self.on_x(half, phase):
+            dz, dx = (0, step) if phase == 0 else (first, step)
+        else:
+            dz, dx = (step, 0) if phase == 0 else (step, first)
+        return context_of(self.zpos + dz, self.xpos + dx)
+
+    def copy(self, half, phase, index, step):
+        start, size = self.ranges[half][max(0, index - 1)]
+        ref = self.buf.at[self.chunk(half, phase, step), pl.ds(start, size), :]
+        way = 1 if index % 2 == 0 else -1
+        if self.on_x(half, phase):
+            to = context_of(self.zpos, self.xpos + way)
+        else:
+            to = context_of(self.zpos + way, self.xpos)
+        slot = half * 20 + phase * 4 + index
+        return pltpu.make_async_remote_copy(
+            src_ref=ref,
+            dst_ref=ref,
+            send_sem=self.send.at[slot],
+            recv_sem=self.recv.at[slot],
+            device_id={"context": to},
+            device_id_type=MESH,
+        )
+
+    def start(self, half, phase, index):
+        copy = self.copy(half, phase, index, (0, 0, -1, 1)[index])
+        copy.start()
+        self.sent.append(copy)
+
+    def arrive(self, half, phase, index):
+        if (half, phase, index) not in self.waited:
+            self.waited.add((half, phase, index))
+            self.copy(half, phase, index, (-1, 1, 2, 2)[index]).wait_recv()
+
+    def whole(self, half, phase):
+        self.start(half, phase, 0)
+        self.start(half, phase, 1)
+
+    def onward(self, half, phase):
+        self.arrive(half, phase, 0)
+        self.start(half, phase, 2)
+        self.arrive(half, phase, 1)
+        self.start(half, phase, 3)
+
+    def opposite(self, half, phase):
+        self.arrive(half, phase, 2)
+        self.arrive(half, phase, 3)
+
+    def stages(self):
+        def own():
+            for half in (0, 1):
+                self.whole(half, 0)
+                self.whole(half, 1)
+
+        def neighbours():
+            for half in (0, 1):
+                self.onward(half, 0)
+                self.whole(half, 2)
+                self.whole(half, 3)
+            for half in (0, 1):
+                self.onward(half, 1)
+
+        def far():
+            for half in (0, 1):
+                self.opposite(half, 0)
+                self.whole(half, 4)
+
+        def corners():
+            for half in (0, 1):
+                self.onward(half, 2)
+                self.onward(half, 3)
+
+        def last():
+            for half in (0, 1):
+                self.onward(half, 4)
+
+        def rest():
+            for half in (0, 1):
+                for phase in (1, 2, 3, 4):
+                    self.opposite(half, phase)
+
+        return [own, neighbours, far, corners, last, rest]
+
+    def drain(self):
+        for copy in self.sent:
+            copy.wait_send()
+
+
+def context_of(zpos, xpos):
+    return lax.rem(zpos + RING, RING) * RING + lax.rem(xpos + RING, RING)
+
+
+def project_kernel(
+    tok_ref, wq_ref, wk_ref, wv_ref, ex_ref,
+    q_ref, k_ref, v_ref,
+    tok, wq, wk, wv, acc,
+    wsend, wrecv, tsend, trecv, local_sem,
+):
+    me = lax.axis_index("context")
+    zpos, xpos = me // RING, lax.rem(me, RING)
+    col = lax.axis_index("tensor")
+    ypos, core = col // 2, lax.rem(col, 2)
+    mate = ypos * 2 + 1 - core
+    up = lax.rem(ypos + 1, RING) * 2 + core
+    down = lax.rem(ypos + RING - 1, RING) * 2 + core
+    token_count = tok.shape[1]
+
+    loads = [
+        pltpu.make_async_copy(tok_ref, tok.at[col], local_sem.at[0]),
+        pltpu.make_async_copy(wq_ref, wq.at[me], local_sem.at[1]),
+        pltpu.make_async_copy(wk_ref, wk.at[me], local_sem.at[2]),
+        pltpu.make_async_copy(wv_ref, wv.at[me], local_sem.at[3]),
+        pltpu.make_async_copy(
+            ex_ref, q_ref.at[me, pl.ds(token_count, EXTRA), :], local_sem.at[4]
+        ),
+    ]
+    for load in loads:
+        load.start()
+
+    barrier = pltpu.get_barrier_semaphore()
+    for dz, dx in ((1, 0), (-1, 0), (0, 1), (0, -1)):
+        pl.semaphore_signal(
+            barrier,
+            inc=1,
+            device_id={"context": context_of(zpos + dz, xpos + dx)},
+            device_id_type=MESH,
+        )
+    for other in (up, down, mate):
+        pl.semaphore_signal(barrier, inc=1, device_id={"tensor": other}, device_id_type=MESH)
+    pl.semaphore_wait(barrier, 7)
+
+    tsent = []
+    part = token_count // 2
+
+    def tcopy(index, block, rows, to):
+        ref = tok.at[block, rows, :]
+        return pltpu.make_async_remote_copy(
+            src_ref=ref, dst_ref=ref, send_sem=tsend.at[index], recv_sem=trecv.at[index],
+            device_id={"tensor": to}, device_id_type=MESH,
+        )
+
+    def tstart(index, block, rows, to):
+        copy = tcopy(index, block, rows, to)
+        copy.start()
+        tsent.append(copy)
+
+    every = pl.ds(0, token_count)
+    low, high = pl.ds(0, part), pl.ds(part, part)
+    across = lax.rem(ypos + 2, RING) * 2 + core
+
+    gathers = [
+        ContextGather(buf, halves(buf.shape[1], extra), wsend.at[i], wrecv.at[i], zpos, xpos)
+        for i, (buf, extra) in enumerate(((wq, 0), (q_ref, EXTRA), (wk, 0), (wv, 0)))
+    ]
+    for_q, for_all, for_k, for_v = [g.stages() for g in gathers]
+
+    loads[0].wait()
+    loads[1].wait()
+    tstart(0, col, every, up)
+    tstart(1, col, every, down)
+    tstart(4, col, every, mate)
+    for_q[0]()
+    tcopy(0, down, every, up).wait_recv()
+    tstart(2, down, low, up)
+    tcopy(1, up, every, down).wait_recv()
+    tstart(3, up, high, down)
+    tstart(5, down, every, mate)
+    tstart(6, up, every, mate)
+    for_q[1]()
+    tcopy(2, across, low, up).wait_recv()
+    tcopy(3, across, high, down).wait_recv()
+    tstart(7, across, every, mate)
+    for stage in for_q[2:5]:
+        stage()
+    loads[2].wait()
+    for_k[0]()
+    for index, block in ((4, mate), (5, down), (6, up), (7, across)):
+        other = lax.rem(block, 2) * 0 + block // 2 * 2 + 1 - core
+        tcopy(index, other, every, mate).wait_recv()
+    for_q[5]()
+
+    def project(w):
+        @pl.loop(0, tok.shape[0])
+        def _(t):
+            base = pl.multiple_of(t * 2, 2)
+            piece = w[pl.ds(base, 2)].reshape(tok.shape[2], w.shape[2])
+            new = jnp.dot(tok[t], piece, preferred_element_type=jnp.float32)
+
+            @pl.when(t == 0)
+            def _():
+                acc[...] = new
+
+            @pl.when(t > 0)
+            def _():
+                acc[...] += new
+
+    project(wq)
+    q_ref[me, 0:token_count, :] = acc[...].astype(jnp.bfloat16)
+    loads[4].wait()
+    for_all[0]()
+    for step in range(1, 6):
+        for_all[step]()
+        for_k[step]()
+        if step == 3:
+            loads[3].wait()
+            for_v[0]()
+    project(wk)
+    k_ref[...] = acc[...].astype(jnp.bfloat16)
+    for step in range(1, 6):
+        for_v[step]()
+    project(wv)
+    v_ref[...] = acc[...].astype(jnp.bfloat16)
+    for copy in tsent:
+        copy.wait_send()
+    for gather in gathers:
+        gather.drain()
+
+
+def gather_project(tokens, wq, wk, wv, extra):
+    token_count, depth = tokens.shape
+    rows, width = wq.shape
+    devices = lax.axis_size("context")
+    columns = lax.axis_size("tensor")
+    hbm = pl.BlockSpec(memory_space=pl.ANY)
+    vmem = pl.BlockSpec(memory_space=pltpu.VMEM)
+    weight = pltpu.VMEM((devices, rows, width), jnp.bfloat16)
+    return pl.pallas_call(
+        project_kernel,
+        in_specs=[hbm] * 5,
+        out_specs=[vmem] * 3,
+        out_shape=[
+            jax.ShapeDtypeStruct((devices, token_count + EXTRA, width), jnp.bfloat16),
+            jax.ShapeDtypeStruct((token_count, width), jnp.bfloat16),
+            jax.ShapeDtypeStruct((token_count, width), jnp.bfloat16),
+        ],
+        scratch_shapes=[
+            pltpu.VMEM((columns, token_count, depth), jnp.bfloat16),
+            weight,
+            weight,
+            weight,
+            pltpu.VMEM((token_count, width), jnp.float32),
+            pltpu.SemaphoreType.DMA((4, 40)),
+            pltpu.SemaphoreType.DMA((4, 40)),
+            pltpu.SemaphoreType.DMA((8,)),
+            pltpu.SemaphoreType.DMA((8,)),
+            pltpu.SemaphoreType.DMA((5,)),
+        ],
+        compiler_params=pltpu.CompilerParams(
+            collective_id=0, has_side_effects=True, vmem_limit_bytes=60 << 20
+        ),
+        name="gather_project",
+    )(tokens, wq, wk, wv, extra)
 
 
 def owner_kernel(heads, cap, rows_ref, n_ref, q_ref, k_ref, v_ref, o_ref, st_ref, acc_ref):
     src = pl.program_id(0)
     span_count = o_ref.shape[1]
-    span = q_ref.shape[1] // span_count
+    span = o_ref.shape[3]
     block = k_ref.shape[1]
     for half in range(span_count):
         c = src * span_count + half
@@ -80,7 +359,7 @@
 def owner_attention(rows, n, q_all, cache_keys, cache_values, heads, cap):
     devices, tokens, width = q_all.shape
     span_count = n.shape[0] // devices
-    span = tokens // span_count
+    span = (tokens - EXTRA) // span_count
     whole = pl.BlockSpec(cache_keys.shape, lambda s, *_: (0, 0, 0), pipeline_mode=pl.Buffered(1))
     return pl.pallas_call(
         functools.partial(owner_kernel, heads, cap),
@@ -167,20 +446,26 @@
     return lax.ppermute(block, axis, route)
 
 
-def owner_table(selected, counts, block_slot, stored, cap):
-    select_count = selected.shape[1]
+def chosen_slots(selected, counts, block_slot, stored, width):
+    span_count, select_count = selected.shape
     live = jnp.arange(select_count)[None, :] < counts[:, None]
     hit = selected[:, :, None] == jnp.arange(block_slot.shape[0])[None, None, :]
     slot = jnp.sum(jnp.where(hit, block_slot[None, None, :], 0), axis=2)
-    slot = jnp.where(live, slot, -1).astype(jnp.int32)
-    slots = lax.all_gather(slot, "context", axis=0, tiled=True)
-    low = lax.axis_index("context") * stored
-    mine = (slots >= low) & (slots < low + stored)
+    owner = jnp.where(live, slot // stored, -1)
+    both = jnp.concatenate([owner, slot % stored], 0).astype(jnp.bfloat16)
+    return jnp.pad(both, ((0, EXTRA - 2 * span_count), (0, width - select_count)))
+
+
+def owner_table(extra, span_count, select_count, cap):
+    owner = extra[:, :span_count, :select_count].reshape(-1, select_count).astype(jnp.int32)
+    row = extra[:, span_count : 2 * span_count, :select_count]
+    row = row.reshape(-1, select_count).astype(jnp.int32)
+    mine = owner == lax.axis_index("context")
     position = jnp.arange(select_count)
     earlier = position[None, :] < position[:, None]
     rank = jnp.sum(jnp.where(mine[:, None, :] & earlier[None], 1, 0), axis=2)
     place = mine[:, :, None] & (rank[:, :, None] == jnp.arange(cap)[None, None, :])
-    rows = jnp.sum(jnp.where(place, (slots - low)[:, :, None], 0), axis=1)
+    rows = jnp.sum(jnp.where(place, row[:, :, None], 0), axis=1)
     return rows.reshape(-1).astype(jnp.int32), jnp.sum(mine, axis=1).astype(jnp.int32)
 
 
@@ -203,27 +488,21 @@
     cap = max(2, 2 * span_count * select_count // devices)
     span = token_count // span_count
 
-    features = lax.all_gather(tokens, "tensor", axis=1, tiled=True)
-
-    def project(weight):
-        whole = lax.all_gather(weight, "context", axis=0, tiled=True)
-        return jnp.dot(features, whole, preferred_element_type=jnp.float32).astype(jnp.bfloat16)
-
-    q = project(query_weight)
-    q_all = lax.all_gather(q, "context", axis=0, tiled=False)
-    rows, n = owner_table(selected, counts, block_slot, cache_keys.shape[0], cap)
+    extra = chosen_slots(selected, counts, block_slot, cache_keys.shape[0], width)
+    q_all, k, v = gather_project(tokens, query_weight, key_weight, value_weight, extra)
+    rows, n = owner_table(q_all[:, token_count:], span_count, select_count, cap)
     o, st = owner_attention(rows, n, q_all, cache_keys, cache_values, heads, cap)
     o = lax.all_to_all(o, "context", split_axis=0, concat_axis=0, tiled=True)
     st = lax.all_to_all(st, "context", split_axis=0, concat_axis=0, tiled=True)
-    k = project(key_weight)
-    v = project(value_weight)
     last = token_count - span
     before_k, before_v = from_behind((k[last:], v[last:]), "context", 1)
 
     def prior(before, own):
         return jnp.concatenate([before, own[:last]], 0).reshape(span_count, span, width)
 
-    first = (lax.axis_index("context") * span_count).astype(jnp.int32).reshape(1)
+    me = lax.axis_index("context")
+    q = lax.dynamic_slice(q_all, (me, 0, 0), (1, token_count, width))[0]
+    first = (me * span_count).astype(jnp.int32).reshape(1)
     return local_attention(first, q, prior(before_k, k), prior(before_v, v), k, v, o, st, heads)
 
 

time: 377 us -> 306 us (0.81)
  waiting for transfers between devices: 228 us -> 57.4 us
  Pallas kernels: 50.2 us -> 208 us
  blocking collectives: 47.8 us -> 13.9 us
  matrix products: 18.3 us -> 0 us
  between operations: 13.3 us -> 0.1 us
    all_gather x5 -> x0, waiting for transfers between devices: 222 us -> none  [the longest x3 163 us: project(): whole = lax.all_gather(weight, 'context', axis=0, tiled=True)]
    pallas_call x0 -> x1, Pallas kernels: none -> 152 us  [gather_project(): pl.pallas_call(project_kernel, in_specs=[hbm] * 5, out_specs=[vmem] * 3,...]
    ppermute x2, waiting for transfers between devices: 2.97 us -> 53.2 us  [from_behind(): return lax.ppermute(block, axis, route)]
    all_gather x1 -> x0, blocking collectives: 23 us -> none  [owner_table(): slots = lax.all_gather(slot, 'context', axis=0, tiled=True)]
    dot_general x3 -> x0, matrix products: 18.3 us -> none  [project(): jnp.dot(features, whole, preferred_element_type=jnp.float32)]
    all_to_all x1, blocking collectives: 24.8 us -> 13.9 us  [shards(): st = lax.all_to_all(st, 'context', split_axis=0, concat_axis=0, tiled=True)]
    pallas_call x1, Pallas kernels: 44.4 us -> 50.2 us  [owner_attention(): pl.pallas_call(functools.partial(owner_kernel, heads, cap), grid_spec=plt...]
    all_to_all x1, waiting for transfers between devices: 0.01 us -> 4.17 us  [shards(): o = lax.all_to_all(o, 'context', split_axis=0, concat_axis=0, tiled=True)]
  transfers between devices with their start and end apart: 8 -> 3, of which waited for: 5 -> 3; matrix products, arithmetic and copies ran while one was open for 4% -> 1% of each run, Pallas kernels for 12% -> 0%
where the time goes in v2:
time: 306 us; the launch traced here: 301 us
  Pallas kernels  208 us (68%)
  waiting for transfers between devices  57.4 us (19%)
  blocking collectives  13.9 us (5%)
  starting transfers between devices  11.8 us (4%)
  other arithmetic  6.08 us (2%)
  local copies, waits for them, and re-layouts  3.96 us (1%)
    pallas_call x1, Pallas kernels, gather_project(): pl.pallas_call(project_kernel, in_specs=[hbm] * 5, out_specs=[vmem] * 3,...  152 us
    ppermute x2, waiting for transfers between devices, from_behind(): return lax.ppermute(block, axis, route)  53.2 us
    pallas_call x1, Pallas kernels, owner_attention(): pl.pallas_call(functools.partial(owner_kernel, heads, cap), grid_spec=plt...  50.2 us
    all_to_all x1, blocking collectives, shards(): st = lax.all_to_all(st, 'context', split_axis=0, concat_axis=0, tiled=True)  13.9 us
    ppermute x2, starting transfers between devices, from_behind(): return lax.ppermute(block, axis, route)  7.04 us
  transfers between devices with their start and end apart: 3, of which 3 were waited for; matrix products, arithmetic and copies ran while one was open for 1% of the time, Pallas kernels for 0%

profile of v2, /device:TPU:0, one launch (start us, length us, event | category | flops | bytes accessed | tf_op | source)
XLA Modules:
  0.0 301.2 jit_solution(2803577141852819941)
XLA Ops:
  0.0 0.9 select_reduce_fusion.2
  0.9 0.7 fusion.7
  1.6 0.6 fusion.6.ex_ref
  2.2 152.1 %gather_project.1 = (bf16[16,272,640]{2,1,0:T(8,128)(2,1)}, bf16[256,640]{1,0:T(8,128)(2,1)}, bf16[256,640]{1,0:T(8,128)(2,1)}) custom-call(bf16[256,640]{1,0:T(8,128)(2,1)} %tok_ref.1, bf16[320,640]{1,0:T(8,128)(2,1)} %wq_ref.1, bf16[320,640]{1,0:T(8,128)(2,1)} %wk_ref.1, bf16[320,640]{1,0:T(8,128)(2,1)} %wv_ref.1, bf16[16,640]{1,0:T(8,128)(2,1)} %fusion.6.ex_ref), custom_call_target="tpu_custom_call" | custom-call | tf_op jit(solution)/shard_map/gather_project/pallas_call | solution.py:274
  154.4 0.8 slice.26
  155.2 1.1 convert_reduce_fusion
  156.3 0.7 reduce_sum.42.n_ref
  157.0 0.6 select_reduce_fusion
  157.6 0.6 select_reduce_fusion.1
  158.2 0.7 reshape.56.rows_ref
  158.9 50.2 %shard_map.91 = (bf16[16,2,640,128]{3,2,1,0:T(8,128)(2,1)}, f32[16,2,16,128]{3,2,1,0:T(8,128)}) custom-call(s32[256]{0:T(256)} %reshape.56.rows_ref, s32[32]{0:T(128)} %reduce_sum.42.n_ref, bf16[16,272,640]{2,1,0:T(8,128)(2,1)} %get-tuple-element.10.q_ref, bf16[32,64,640]{2,1,0:T(8,128)(2,1)} %k_ref.1, bf16[32,64,640]{2,1,0:T(8,128)(2,1)} %v_ref.1), custom_call_target="tpu_custom_call" | custom-call | tf_op jit(solution)/shard_map/pallas_call | solution.py:364
  209.1 13.9 %all_to_all.10.st_ref = f32[16,2,16,128]{3,2,1,0:T(8,128)} all-to-all(f32[16,2,16,128]{3,2,1,0:T(8,128)} %get-tuple-element.14), channel_id=1, replica_groups=mesh['tensor'=8,'context'=16] {'context'}, dimensions={0} | all-to-all | bytes 524288 | tf_op jit(solution)/shard_map/all_to_all | solution.py:496
  223.0 0.0 copy-start
  223.0 0.0 copy-start.1
  223.0 4.7 %all-to-all-start = ((bf16[16,2,640,128]{3,2,1,0:T(8,128)(2,1)}), bf16[16,2,640,128]{3,2,1,0:T(8,128)(2,1)}, u32[]{:S(2)}, u32[]{:S(2)}) async-start(bf16[16,2,640,128]{3,2,1,0:T(8,128)(2,1)} %get-tuple-element.13), calls=%async_computation | async-start | bytes 10485760 | tf_op jit(solution)/shard_map/all_to_all | solution.py:495
  227.7 0.0 copy-done
  227.8 3.7 %collective-permute-start = (bf16[128,640]{1,0:T(8,128)(2,1)S(1)}, bf16[128,640]{1,0:T(8,128)(2,1)S(1)}, u32[]{:S(2)}, u32[]{:S(2)}) collective-permute-start(bf16[128,640]{1,0:T(8,128)(2,1)S(1)} %get-tuple-element.19), channel_id=1, source_target_pairs={{0,1},{1,2},{2,3},{3,4},{4,5},{5,6},{6,7},{7,8},{8,9},{9,10},{10,1... | collective-permute-start | bytes 491528 | tf_op jit(solution)/shard_map/ppermute | solution.py:446
  231.4 0.0 copy-done.1
  231.5 3.4 %collective-permute-start.1 = (bf16[128,640]{1,0:T(8,128)(2,1)S(1)}, bf16[128,640]{1,0:T(8,128)(2,1)S(1)}, u32[]{:S(2)}, u32[]{:S(2)}) collective-permute-start(bf16[128,640]{1,0:T(8,128)(2,1)S(1)} %get-tuple-element.17), channel_id=1, source_target_pairs={{0,1},{1,2},{2,3},{3,4},{4,5},{5,6},{6,7},{7,8},{8,9},{9,10},{10,1... | collective-permute-start | bytes 491528 | tf_op jit(solution)/shard_map/ppermute | solution.py:446
  234.9 1.7 dynamic-slice_bitcast_fusion.q_ref
  236.6 52.2 %collective-permute-done = bf16[128,640]{1,0:T(8,128)(2,1)S(1)} collective-permute-done((bf16[128,640]{1,0:T(8,128)(2,1)S(1)}, bf16[128,640]{1,0:T(8,128)(2,1)S(1)}, u32[]{:S(2)}, u32[]{:S(2)}) %collective-permute-start) | collective-permute-done | bytes 163872 | tf_op jit(solution)/shard_map/ppermute | solution.py:446
  288.8 0.7 pad_maximum_fusion
  289.5 1.0 collective-permute-done.1
  290.6 0.8 pad_maximum_fusion.1
  291.3 4.2 %all-to-all-done.o_ref = bf16[16,2,640,128]{3,2,1,0:T(8,128)(2,1)} async-done(((bf16[16,2,640,128]{3,2,1,0:T(8,128)(2,1)}), bf16[16,2,640,128]{3,2,1,0:T(8,128)(2,1)}, u32[]{:S(2)}, u32[]{:S(2)}) %all-to-all-start) | async-done | bytes 5242912 | tf_op jit(solution)/shard_map/all_to_all | solution.py:495
  295.5 5.7 %shard_map.92 = bf16[256,640]{1,0:T(8,128)(2,1)} custom-call(s32[1]{0:T(128)} %bitcast.first_ref, bf16[256,640]{1,0:T(8,128)(2,1)} %dynamic-slice_bitcast_fusion.q_ref, bf16[2,128,640]{2,1,0:T(8,128)(2,1)} %bitcast.7, bf16[2,128,640]{2,1,0:T(8,128)(2,1)} %bitcast.8, bf16[256,640]{1,0:T(8,128)(2,1)} %get-tuple-element.11.k_ref, ...), custom_call_target="tpu_custom_call" | custom-call | tf_op jit(solution)/shard_map/pallas_call | solution.py:423
  (5 shorter events, 0.1 us)
Async XLA Ops:
  223.0 4.8 %copy-start = (bf16[256,640]{1,0:T(8,128)(2,1)S(1)}, bf16[256,640]{1,0:T(8,128)(2,1)}, u32[]{:S(2)}) copy-start(bf16[256,640]{1,0:T(8,128)(2,1)} %get-tuple-element.11.k_ref) | copy-start | bytes 983044
  223.0 8.5 %copy-start.1 = (bf16[256,640]{1,0:T(8,128)(2,1)S(1)}, bf16[256,640]{1,0:T(8,128)(2,1)}, u32[]{:S(2)}) copy-start(bf16[256,640]{1,0:T(8,128)(2,1)} %get-tuple-element.12.v_ref) | copy-start | bytes 983044
  223.0 72.5 %all-to-all-start = ((bf16[16,2,640,128]{3,2,1,0:T(8,128)(2,1)}), bf16[16,2,640,128]{3,2,1,0:T(8,128)(2,1)}, u32[]{:S(2)}, u32[]{:S(2)}) async-start(bf16[16,2,640,128]{3,2,1,0:T(8,128)(2,1)} %get-tuple-element.13), calls=%async_computation | async-start | bytes 10485760 | tf_op jit(solution)/shard_map/all_to_all | solution.py:495
  227.8 61.0 %collective-permute-start = (bf16[128,640]{1,0:T(8,128)(2,1)S(1)}, bf16[128,640]{1,0:T(8,128)(2,1)S(1)}, u32[]{:S(2)}, u32[]{:S(2)}) collective-permute-start(bf16[128,640]{1,0:T(8,128)(2,1)S(1)} %get-tuple-element.19), channel_id=1, source_target_pairs={{0,1},{1,2},{2,3},{3,4},{4,5},{5,6},{6,7},{7,8},{8,9},{9,10},{10,1... | collective-permute-start | bytes 491528 | tf_op jit(solution)/shard_map/ppermute | solution.py:446
  231.5 59.1 %collective-permute-start.1 = (bf16[128,640]{1,0:T(8,128)(2,1)S(1)}, bf16[128,640]{1,0:T(8,128)(2,1)S(1)}, u32[]{:S(2)}, u32[]{:S(2)}) collective-permute-start(bf16[128,640]{1,0:T(8,128)(2,1)S(1)} %get-tuple-element.17), channel_id=1, source_target_pairs={{0,1},{1,2},{2,3},{3,4},{4,5},{5,6},{6,7},{7,8},{8,9},{9,10},{10,1... | collective-permute-start | bytes 491528 | tf_op jit(solution)/shard_map/ppermute | solution.py:446

commit v3 on v2

--- a/solution.py
+++ b/solution.py
@@ -304,55 +304,63 @@
     span_count = o_ref.shape[1]
     span = o_ref.shape[3]
     block = k_ref.shape[1]
-    for half in range(span_count):
+    columns = [slice(h * HDIM, (h + 1) * HDIM) for h in range(heads)]
+
+    def scores(half, j):
         c = src * span_count + half
         n = n_ref[c]
-        rows = slice(half * span, (half + 1) * span)
-
-        def pair(j, first):
-            r0 = rows_ref[c * cap + 2 * j]
-            r1 = rows_ref[c * cap + jnp.minimum(2 * j + 1, cap - 1)]
-            bias = jnp.where(2 * j + 1 < n, 0.0, NEG)
-            for h in range(heads):
-                cols = slice(h * HDIM, (h + 1) * HDIM)
-                q = q_ref[0, rows, cols]
-                k = jnp.concatenate([k_ref[r0, :, cols], k_ref[r1, :, cols]], 0)
-                v = jnp.concatenate([v_ref[r0, :, cols], v_ref[r1, :, cols]], 0)
-                s = dot_nt(k, q) * SCALE
-                s = jnp.concatenate([s[:block], s[block:] + bias], 0)
-                m = jnp.max(s, axis=0, keepdims=True)
-                if not first:
-                    old = st_ref[0, half, h : h + 1, :]
-                    m = jnp.maximum(m, old)
-                    decay = jnp.exp2(old - m)
-                p = jnp.exp2(s - m)
-                l = jnp.sum(p, axis=0, keepdims=True)
-                a = dot_tn(v, p.astype(jnp.bfloat16))
-                if not first:
-                    l = l + st_ref[0, half, 8 + h : 9 + h, :] * decay
-                    a = a + acc_ref[cols, :] * decay
-                st_ref[0, half, h : h + 1, :] = m
-                st_ref[0, half, 8 + h : 9 + h, :] = l
-                acc_ref[cols, :] = a
-
-        @pl.when(n == 0)
+        r0 = rows_ref[c * cap + 2 * j]
+        r1 = rows_ref[c * cap + 2 * j + 1]
+        bias0 = jnp.where(2 * j < n, 0.0, NEG)
+        bias1 = jnp.where(2 * j + 1 < n, 0.0, NEG)
+        out = []
+        for cols in columns:
+            q = q_ref[0, half * span : (half + 1) * span, cols]
+            k = jnp.concatenate([k_ref[r0, :, cols], k_ref[r1, :, cols]], 0)
+            v = jnp.concatenate([v_ref[r0, :, cols], v_ref[r1, :, cols]], 0)
+            s = dot_nt(k, q) * SCALE
+            out.append((jnp.concatenate([s[:block] + bias0, s[block:] + bias1], 0), v))
+        return out
+
+    for half in range(span_count):
+        results = []
+        for s, v in scores(half, 0):
+            m = jnp.max(s, axis=0, keepdims=True)
+            p = jnp.exp2(s - m)
+            l = jnp.sum(p, axis=0, keepdims=True)
+            results.append((m, l, dot_tn(v, p.astype(jnp.bfloat16))))
+        for h, (m, l, a) in enumerate(results):
+            st_ref[0, half, h : h + 1, :] = m
+            st_ref[0, half, 8 + h : 9 + h, :] = l
+            acc_ref[half, columns[h], :] = a
+            o_ref[0, half, columns[h], :] = (a * (1.0 / l)).astype(jnp.bfloat16)
+
+    for half in range(span_count):
+        n = n_ref[src * span_count + half]
+
+        @pl.when(n > 2)
         def _():
-            o_ref[0, half] = jnp.zeros_like(o_ref[0, half])
-            st_ref[0, half, 0:8, :] = jnp.full_like(st_ref[0, half, 0:8, :], NEG)
-            st_ref[0, half, 8:16, :] = jnp.zeros_like(st_ref[0, half, 8:16, :])
-
-        @pl.when(n > 0)
-        def _():
-            pair(0, True)
-
             @pl.loop(1, (n + 1) // 2)
             def _(j):
-                pair(j, False)
+                results = []
+                for h, (s, v) in enumerate(scores(half, j)):
+                    old = st_ref[0, half, h : h + 1, :]
+                    m = jnp.maximum(jnp.max(s, axis=0, keepdims=True), old)
+                    decay = jnp.exp2(old - m)
+                    p = jnp.exp2(s - m)
+                    l = jnp.sum(p, axis=0, keepdims=True)
+                    l = l + st_ref[0, half, 8 + h : 9 + h, :] * decay
+                    a = dot_tn(v, p.astype(jnp.bfloat16)) + acc_ref[half, columns[h], :] * decay
+                    results.append((m, l, a))
+                for h, (m, l, a) in enumerate(results):
+                    st_ref[0, half, h : h + 1, :] = m
+                    st_ref[0, half, 8 + h : 9 + h, :] = l
+                    acc_ref[half, columns[h], :] = a
 
             for h in range(heads):
-                cols = slice(h * HDIM, (h + 1) * HDIM)
-                o_ref[0, half, cols, :] = (
-                    acc_ref[cols, :] / st_ref[0, half, 8 + h : 9 + h, :]
+                l = st_ref[0, half, 8 + h : 9 + h, :]
+                o_ref[0, half, columns[h], :] = (
+                    acc_ref[half, columns[h], :] * (1.0 / l)
                 ).astype(jnp.bfloat16)
 
 
@@ -375,7 +383,7 @@
                 pl.BlockSpec((1, span_count, width, span), lambda s, *_: (s, 0, 0, 0)),
                 pl.BlockSpec((1, span_count, 16, span), lambda s, *_: (s, 0, 0, 0)),
             ],
-            scratch_shapes=[pltpu.VMEM((width, span), jnp.float32)],
+            scratch_shapes=[pltpu.VMEM((span_count, width, span), jnp.float32)],
         ),
         out_shape=[
             jax.ShapeDtypeStruct((devices, span_count, width, span), jnp.bfloat16),
@@ -384,66 +392,282 @@
     )(rows, n, q_all, cache_keys, cache_values)
 
 
-def local_kernel(heads, first_ref, q_ref, pk_ref, pv_ref, k_ref, v_ref, o_ref, st_ref, out_ref):
-    half = pl.program_id(0)
-    span = q_ref.shape[0]
-    bias = jnp.where((first_ref[0] + half) > 0, 0.0, NEG)
+def combine_kernel(
+    heads,
+    o_ref, st_ref, q_ref, k_ref, v_ref,
+    out_ref,
+    before, relay, relay_st, got, got_st, mid, mid_st,
+    relay2, relay2_st, got2, got2_st, acc, acc_st,
+    send, recv, send_st, recv_st, psend, precv,
+):
+    me = lax.axis_index("context")
+    zpos, xpos = me // RING, lax.rem(me, RING)
+    devices = RING * RING
+    behind, ahead = lax.rem(me + devices - 1, devices), lax.rem(me + 1, devices)
+    span = o_ref.shape[-1]
+    cut = (heads + 1) // 2 * HDIM
+    parts = ((0, cut), (cut, heads * HDIM - cut))
+
+    barrier = pltpu.get_barrier_semaphore()
+    for other in (
+        context_of(zpos + 1, xpos),
+        context_of(zpos - 1, xpos),
+        context_of(zpos, xpos + 1),
+        context_of(zpos, xpos - 1),
+        behind,
+        ahead,
+    ):
+        pl.semaphore_signal(barrier, inc=1, device_id={"context": other}, device_id_type=MESH)
+    pl.semaphore_wait(barrier, 6)
+
+    started = []
+
+    def near(half, first, way):
+        if (half == 0) == first:
+            return context_of(zpos, xpos + way)
+        return context_of(zpos + way, xpos)
+
+    def copies(half, index, src, src_st, dst, dst_st):
+        slot = half * 12 + index
+        to = near(half, index < 6, 1 if index % 2 == 0 else -1)
+        make = pltpu.make_async_remote_copy
+        where = dict(device_id={"context": to}, device_id_type=MESH)
+        return (
+            make(src, dst, send.at[slot], recv.at[slot], **where),
+            make(src_st, dst_st, send_st.at[slot], recv_st.at[slot], **where),
+        )
+
+    def start(*args):
+        for copy in copies(*args):
+            copy.start()
+            started.append(copy)
+
+    def arrive(half, index, dst, dst_st):
+        for copy in copies(half, index, dst, dst_st, dst, dst_st):
+            copy.wait_recv()
+
+    def first_at(half):
+        return xpos if half == 0 else zpos
+
+    def second_at(half):
+        return zpos if half == 0 else xpos
+
+    def wrap(position):
+        return lax.rem(position + RING, RING)
+
+    def held(ref, half, step, low):
+        to = wrap(first_at(half) + step)
+        if half == 0:
+            return ref.at[pl.ds(low, 2), to, 0]
+        return ref.at[to, pl.ds(low, 2), 1]
+
+    def merge(out, out_st, sources, head_range):
+        @pl.loop(*head_range)
+        def _(h):
+            rows = pl.ds(pl.multiple_of(h * HDIM, HDIM), HDIM)
+            ms = [st[pl.ds(h, 1), :] for _, st in sources]
+            m = functools.reduce(jnp.maximum, ms)
+            ws = [st[pl.ds(8 + h, 1), :] * jnp.exp2(x - m) for (_, st), x in zip(sources, ms)]
+            total = functools.reduce(jnp.add, ws)
+            inverse = 1.0 / total
+            terms = [
+                part[rows, :].astype(jnp.float32) * (w * inverse)
+                for (part, _), w in zip(sources, ws)
+            ]
+            out[rows, :] = functools.reduce(jnp.add, terms).astype(jnp.bfloat16)
+            out_st[pl.ds(h, 1), :] = m
+            out_st[pl.ds(8 + h, 1), :] = total
+
+    for half in (0, 1):
+        for index, low in ((0, 0), (1, 2)):
+            start(
+                half, index, held(o_ref, half, 2, low), held(st_ref, half, 2, low),
+                relay.at[half, index], relay_st.at[half, index],
+            )
+    for half in (0, 1):
+        for index, low, way in ((2, 2, 1), (3, 0, -1)):
+            start(
+                half, index, held(o_ref, half, way, low), held(st_ref, half, way, low),
+                got.at[half, index - 2, pl.ds(low, 2)], got_st.at[half, index - 2, pl.ds(low, 2)],
+            )
+    prior = []
+    for i, ref in enumerate((k_ref, v_ref)):
+        prior.append(
+            pltpu.make_async_remote_copy(
+                ref.at[pl.ds(ref.shape[0] - span, span), :], before.at[i],
+                psend.at[i], precv.at[i],
+                device_id={"context": ahead}, device_id_type=MESH,
+            )
+        )
+        prior[-1].start()
+
     key = lax.broadcasted_iota(jnp.int32, (span, span), 0)
     row = lax.broadcasted_iota(jnp.int32, (span, span), 1)
+
+    def local(half, h, keys, values, bias, first):
+        cols = slice(h * HDIM, (h + 1) * HDIM)
+        q = q_ref[0, half * span : (half + 1) * span, cols]
+        s = dot_nt(keys, q) * SCALE
+        s = jnp.where(key <= row, s, NEG) if bias is None else s + bias
+        m = jnp.max(s, axis=0, keepdims=True)
+        if not first:
+            old = acc_st[half, h : h + 1, :]
+            m = jnp.maximum(m, old)
+            decay = jnp.exp2(old - m)
+        p = jnp.exp2(s - m)
+        l = jnp.sum(p, axis=0, keepdims=True)
+        a = dot_tn(values, p.astype(jnp.bfloat16))
+        if not first:
+            l = l + acc_st[half, 8 + h : 9 + h, :] * decay
+            a = a + acc[half, cols, :] * decay
+        acc_st[half, h : h + 1, :] = m
+        acc_st[half, 8 + h : 9 + h, :] = l
+        acc[half, cols, :] = a
+
+    for half in (0, 1):
+        rows = slice(half * span, (half + 1) * span)
+        for h in range(heads):
+            cols = slice(h * HDIM, (h + 1) * HDIM)
+            local(half, h, k_ref[rows, cols], v_ref[rows, cols], None, True)
     for h in range(heads):
         cols = slice(h * HDIM, (h + 1) * HDIM)
-        q = q_ref[:, cols]
-        s0 = dot_nt(pk_ref[0, :, cols], q) * SCALE + bias
-        s1 = jnp.where(key <= row, dot_nt(k_ref[:, cols], q) * SCALE, NEG)
-        far_m = st_ref[:, 0, h, :]
-        far_l = st_ref[:, 0, 8 + h, :]
-        m = jnp.maximum(
-            jnp.maximum(jnp.max(s0, axis=0, keepdims=True), jnp.max(s1, axis=0, keepdims=True)),
-            jnp.max(far_m, axis=0, keepdims=True),
-        )
-        p0 = jnp.exp2(s0 - m)
-        p1 = jnp.exp2(s1 - m)
-        w = far_l * jnp.exp2(far_m - m)
-        total = (
-            jnp.sum(p0, axis=0, keepdims=True)
-            + jnp.sum(p1, axis=0, keepdims=True)
-            + jnp.sum(w, axis=0, keepdims=True)
-        )
-        a = dot_tn(pv_ref[0, :, cols], p0.astype(jnp.bfloat16))
-        a = a + dot_tn(v_ref[:, cols], p1.astype(jnp.bfloat16))
-        for i in range(o_ref.shape[0]):
-            a = a + o_ref[i, 0, cols, :].astype(jnp.float32) * w[i : i + 1, :]
-        out_ref[:, cols] = jnp.transpose(a / total).astype(out_ref.dtype)
-
-
-def local_attention(first, q, prior_k, prior_v, k, v, o, st, heads):
-    devices, span_count, width, span = o.shape
-    rows = pl.BlockSpec((span, width), lambda c, *_: (c, 0))
-    before = pl.BlockSpec((1, span, width), lambda c, *_: (c, 0, 0))
+        local(1, h, k_ref[0:span, cols], v_ref[0:span, cols], 0.0, False)
+
+    for half in (0, 1):
+        for index, low, way in ((0, 0, 1), (1, 2, -1)):
+            arrive(half, index, relay.at[half, index], relay_st.at[half, index])
+            to = wrap(first_at(half) + way)
+            for i in (0, 1):
+                part, st = relay.at[half, index, i], relay_st.at[half, index, i]
+                at = (low + i, to, 0) if half == 0 else (to, low + i, 1)
+                merge(part, st, [(part, st), (o_ref.at[at], st_ref.at[at])], (0, heads))
+            start(
+                half, 4 + index, relay.at[half, index], relay_st.at[half, index],
+                got.at[half, index, pl.ds(low, 2)], got_st.at[half, index, pl.ds(low, 2)],
+            )
+
+    for copy in prior:
+        copy.wait_recv()
+    bias = jnp.where(me > 0, 0.0, NEG)
+    for h in range(heads):
+        cols = slice(h * HDIM, (h + 1) * HDIM)
+        local(0, h, before[0, :, cols], before[1, :, cols], bias, False)
+
+    for half in (0, 1):
+        for index, low in ((2, 2), (3, 0), (4, 0), (5, 2)):
+            side = index % 2
+            arrive(
+                half, index,
+                got.at[half, side, pl.ds(low, 2)], got_st.at[half, side, pl.ds(low, 2)],
+            )
+        for step in (2, 1, -1, 0):
+            to = wrap(second_at(half) + step)
+            at = (to, xpos, 0) if half == 0 else (zpos, to, 1)
+            merge(
+                mid.at[half, to], mid_st.at[half, to],
+                [(o_ref.at[at], st_ref.at[at])]
+                + [(got.at[half, i, to], got_st.at[half, i, to]) for i in (0, 1)],
+                (0, heads),
+            )
+            for side in (0, 1):
+                rows = pl.ds(*parts[side])
+                if step == 2:
+                    start(
+                        half, 6 + side, mid.at[half, to, rows], mid_st.at[half, to],
+                        relay2.at[half, rows], relay2_st.at[half, side],
+                    )
+            if step in (1, -1):
+                side = 0 if step == 1 else 1
+                other = pl.ds(*parts[1 - side])
+                start(
+                    half, 8 + side, mid.at[half, to, other], mid_st.at[half, to],
+                    got2.at[half, side, other], got2_st.at[half, side, 1 - side],
+                )
+
+    for half in (0, 1):
+        for side, way in ((0, 1), (1, -1)):
+            rows = pl.ds(*parts[side])
+            arrive(half, 6 + side, relay2.at[half, rows], relay2_st.at[half, side])
+            to = wrap(second_at(half) + way)
+            merge(
+                relay2.at[half], relay2_st.at[half, side],
+                [
+                    (relay2.at[half], relay2_st.at[half, side]),
+                    (mid.at[half, to], mid_st.at[half, to]),
+                ],
+                (parts[side][0] // HDIM, sum(parts[side]) // HDIM),
+            )
+            start(
+                half, 10 + side, relay2.at[half, rows], relay2_st.at[half, side],
+                got2.at[half, side, rows], got2_st.at[half, side, side],
+            )
+
+    for half in (0, 1):
+        for side in (0, 1):
+            for index, which in ((8 + side, 1 - side), (10 + side, side)):
+                arrive(
+                    half, index,
+                    got2.at[half, side, pl.ds(*parts[which])], got2_st.at[half, side, which],
+                )
+        at = second_at(half)
+        for h in range(heads):
+            cols = slice(h * HDIM, (h + 1) * HDIM)
+            which = 0 if h * HDIM < cut else 1
+            sources = [(mid.at[half, at], mid_st.at[half, at])]
+            sources += [(got2.at[half, i], got2_st.at[half, i, which]) for i in (0, 1)]
+            old = acc_st[half, h : h + 1, :]
+            ms = [st[h : h + 1, :] for _, st in sources]
+            m = functools.reduce(jnp.maximum, ms, old)
+            decay = jnp.exp2(old - m)
+            total = acc_st[half, 8 + h : 9 + h, :] * decay
+            a = acc[half, cols, :] * decay
+            for (part, st), x in zip(sources, ms):
+                w = st[8 + h : 9 + h, :] * jnp.exp2(x - m)
+                total = total + w
+                a = a + part[cols, :].astype(jnp.float32) * w
+            out_ref[half * span : (half + 1) * span, cols] = jnp.transpose(a / total).astype(
+                out_ref.dtype
+            )
+
+    for copy in started + prior:
+        copy.wait_send()
+
+
+def combine(o, st, q, k, v, heads):
+    span_count, width, span = o.shape[1:]
+    rows = st.shape[2]
+    o = o.reshape(RING, RING, span_count, width, span)
+    st = st.reshape(RING, RING, span_count, rows, span)
+    vmem = pl.BlockSpec(memory_space=pltpu.VMEM)
+
+    def pair(*lead):
+        return [
+            pltpu.VMEM(lead + (width, span), jnp.bfloat16),
+            pltpu.VMEM(lead + (rows, span), jnp.float32),
+        ]
+
     return pl.pallas_call(
-        functools.partial(local_kernel, heads),
-        grid_spec=pltpu.PrefetchScalarGridSpec(
-            num_scalar_prefetch=1,
-            grid=(span_count,),
-            in_specs=[
-                rows,
-                before,
-                before,
-                rows,
-                rows,
-                pl.BlockSpec((devices, 1, width, span), lambda c, *_: (0, c, 0, 0)),
-                pl.BlockSpec((devices, 1, 16, span), lambda c, *_: (0, c, 0, 0)),
-            ],
-            out_specs=rows,
+        functools.partial(combine_kernel, heads),
+        in_specs=[vmem] * 5,
+        out_specs=vmem,
+        out_shape=jax.ShapeDtypeStruct(k.shape, jnp.bfloat16),
+        scratch_shapes=[pltpu.VMEM((2, span, width), jnp.bfloat16)]
+        + pair(2, 2, 2)
+        + pair(2, 2, RING)
+        + pair(2, RING)
+        + [pltpu.VMEM((2, width, span), jnp.bfloat16), pltpu.VMEM((2, 2, rows, span), jnp.float32)]
+        + [
+            pltpu.VMEM((2, 2, width, span), jnp.bfloat16),
+            pltpu.VMEM((2, 2, 2, rows, span), jnp.float32),
+        ]
+        + [pltpu.VMEM((2, width, span), jnp.float32), pltpu.VMEM((2, rows, span), jnp.float32)]
+        + [pltpu.SemaphoreType.DMA((24,))] * 4
+        + [pltpu.SemaphoreType.DMA((2,))] * 2,
+        compiler_params=pltpu.CompilerParams(
+            collective_id=1, has_side_effects=True, vmem_limit_bytes=60 << 20
         ),
-        out_shape=jax.ShapeDtypeStruct(q.shape, jnp.bfloat16),
-    )(first, q, prior_k, prior_v, k, v, o, st)
-
-
-def from_behind(block, axis, distance):
-    devices = range(lax.axis_size(axis))
-    route = [(i - distance, i) for i in devices if i - distance in devices]
-    return lax.ppermute(block, axis, route)
+        name="combine",
+    )(o, st, q, k, v)
 
 
 def chosen_slots(selected, counts, block_slot, stored, width):
@@ -486,24 +710,14 @@
     span_count, select_count = selected.shape
     devices = lax.axis_size("context")
     cap = max(2, 2 * span_count * select_count // devices)
-    span = token_count // span_count
 
     extra = chosen_slots(selected, counts, block_slot, cache_keys.shape[0], width)
     q_all, k, v = gather_project(tokens, query_weight, key_weight, value_weight, extra)
     rows, n = owner_table(q_all[:, token_count:], span_count, select_count, cap)
     o, st = owner_attention(rows, n, q_all, cache_keys, cache_values, heads, cap)
-    o = lax.all_to_all(o, "context", split_axis=0, concat_axis=0, tiled=True)
-    st = lax.all_to_all(st, "context", split_axis=0, concat_axis=0, tiled=True)
-    last = token_count - span
-    before_k, before_v = from_behind((k[last:], v[last:]), "context", 1)
-
-    def prior(before, own):
-        return jnp.concatenate([before, own[:last]], 0).reshape(span_count, span, width)
-
     me = lax.axis_index("context")
-    q = lax.dynamic_slice(q_all, (me, 0, 0), (1, token_count, width))[0]
-    first = (me * span_count).astype(jnp.int32).reshape(1)
-    return local_attention(first, q, prior(before_k, k), prior(before_v, v), k, v, o, st, heads)
+    q = lax.dynamic_slice(q_all, (me, 0, 0), (1, token_count, width))
+    return combine(o, st, q, k, v, heads)
 
 
 def solution(mesh):

time: 306 us -> 231 us (0.75)
  waiting for transfers between devices: 57.4 us -> 0 us
  blocking collectives: 13.9 us -> 0 us
  starting transfers between devices: 11.8 us -> 0 us
  Pallas kernels: 208 us -> 219 us
    ppermute x2 -> x0, waiting for transfers between devices: 53.2 us -> none  [from_behind(): return lax.ppermute(block, axis, route)]
    pallas_call x1, Pallas kernels: 5.74 us -> 45.6 us  [combine(): pl.pallas_call(functools.partial(combine_kernel, heads), in_specs=[vmem]...]
    pallas_call x1, Pallas kernels: 50.2 us -> 21 us  [owner_attention(): pl.pallas_call(functools.partial(owner_kernel, heads, cap), grid_spec=plt...]
    all_to_all x1 -> x0, blocking collectives: 13.9 us -> none  [shards(): st = lax.all_to_all(st, 'context', split_axis=0, concat_axis=0, tiled=True)]
    ppermute x2 -> x0, starting transfers between devices: 7.04 us -> none  [from_behind(): return lax.ppermute(block, axis, route)]
    all_to_all x1 -> x0, starting transfers between devices: 4.74 us -> none  [shards(): o = lax.all_to_all(o, 'context', split_axis=0, concat_axis=0, tiled=True)]
    all_to_all x1 -> x0, waiting for transfers between devices: 4.17 us -> none  [shards(): o = lax.all_to_all(o, 'context', split_axis=0, concat_axis=0, tiled=True)]
  transfers between devices with their start and end apart: 3 -> 0, of which waited for: 3 -> 0; matrix products, arithmetic and copies ran while one was open for 1% -> 0% of each run, Pallas kernels for 0% -> 0%
where the time goes in v3:
time: 231 us; the launch traced here: 229 us
  Pallas kernels  219 us (95%)
  local copies, waits for them, and re-layouts  5.59 us (2%)
  other arithmetic  4.58 us (2%)
    pallas_call x1, Pallas kernels, gather_project(): pl.pallas_call(project_kernel, in_specs=[hbm] * 5, out_specs=[vmem] * 3,...  152 us
    pallas_call x1, Pallas kernels, combine(): pl.pallas_call(functools.partial(combine_kernel, heads), in_specs=[vmem]...  45.6 us
    pallas_call x1, Pallas kernels, owner_attention(): pl.pallas_call(functools.partial(owner_kernel, heads, cap), grid_spec=plt...  21 us

profile of v3, /device:TPU:0, one launch (start us, length us, event | category | flops | bytes accessed | tf_op | source)
XLA Modules:
  0.0 228.9 jit_solution(4163138828504480674)
XLA Ops:
  0.0 0.9 select_reduce_fusion.2
  0.9 0.7 fusion.7
  1.6 0.6 fusion.6.ex_ref
  2.2 152.1 %gather_project.1 = (bf16[16,272,640]{2,1,0:T(8,128)(2,1)}, bf16[256,640]{1,0:T(8,128)(2,1)}, bf16[256,640]{1,0:T(8,128)(2,1)}) custom-call(bf16[256,640]{1,0:T(8,128)(2,1)} %tok_ref.1, bf16[320,640]{1,0:T(8,128)(2,1)} %wq_ref.1, bf16[320,640]{1,0:T(8,128)(2,1)} %wk_ref.1, bf16[320,640]{1,0:T(8,128)(2,1)} %wv_ref.1, bf16[16,640]{1,0:T(8,128)(2,1)} %fusion.6.ex_ref), custom_call_target="tpu_custom_call" | custom-call | tf_op jit(solution)/shard_map/gather_project/pallas_call | solution.py:274
  154.3 1.1 convert_reduce_fusion
  155.5 0.6 select_reduce_fusion
  156.1 0.8 slice.10
  156.9 0.6 select_reduce_fusion.1
  157.5 0.7 reshape.50.rows_ref
  158.2 0.7 reduce_sum.42.n_ref
  158.9 21.0 %shard_map.91 = (bf16[16,2,640,128]{3,2,1,0:T(8,128)(2,1)}, f32[16,2,16,128]{3,2,1,0:T(8,128)}) custom-call(s32[256]{0:T(256)} %reshape.50.rows_ref, s32[32]{0:T(128)} %reduce_sum.42.n_ref, bf16[16,272,640]{2,1,0:T(8,128)(2,1)} %get-tuple-element.10.q_ref, bf16[32,64,640]{2,1,0:T(8,128)(2,1)} %k_ref.1, bf16[32,64,640]{2,1,0:T(8,128)(2,1)} %v_ref.1), custom_call_target="tpu_custom_call" | custom-call | tf_op jit(solution)/shard_map/pallas_call | solution.py:372
  179.8 1.7 constant_dynamic-slice_fusion.q_ref
  181.5 45.6 %combine.1 = bf16[256,640]{1,0:T(8,128)(2,1)} custom-call(bf16[4,4,2,640,128]{4,3,2,1,0:T(8,128)(2,1)} %bitcast.4, f32[4,4,2,16,128]{4,3,2,1,0:T(8,128)} %bitcast.5, bf16[1,256,640]{2,1,0:T(8,128)(2,1)} %constant_dynamic-slice_fusion.q_ref, bf16[256,640]{1,0:T(8,128)(2,1)} %get-tuple-element.13.k_ref, bf16[256,640]{1,0:T(8,128)(2,1)} %get-tuple-element.14.v_ref), custom_call_target="tpu_custom_call" | custom-call | tf_op jit(solution)/shard_map/combine/pallas_call | solution.py:649
  227.2 1.7 copy.11
  (3 shorter events, 0.0 us)

commit v4 on v3

--- a/solution.py
+++ b/solution.py
@@ -26,272 +26,425 @@
 OFFSETS = (0, -1, 1, 2)
 
 
-def halves(total, extra):
-    half = (total - extra) // 2
-    part = half // 2
-    first = ((0, half), (0, part), (part, half - part))
-    second = ((half, half + extra), (half, part), (half + part, half - part + extra))
-    return (first, second)
-
-
-class ContextGather:
-    def __init__(self, buf, ranges, send, recv, zpos, xpos):
-        self.buf, self.ranges, self.send, self.recv = buf, ranges, send, recv
-        self.zpos, self.xpos = zpos, xpos
-        self.waited, self.sent = set(), []
-
-    def on_x(self, half, phase):
-        return (half == 0) == (phase == 0)
-
-    def chunk(self, half, phase, step):
-        first = 0 if phase == 0 else OFFSETS[phase - 1]
-        if self.on_x(half, phase):
-            dz, dx = (0, step) if phase == 0 else (first, step)
-        else:
-            dz, dx = (step, 0) if phase == 0 else (step, first)
-        return context_of(self.zpos + dz, self.xpos + dx)
-
-    def copy(self, half, phase, index, step):
-        start, size = self.ranges[half][max(0, index - 1)]
-        ref = self.buf.at[self.chunk(half, phase, step), pl.ds(start, size), :]
-        way = 1 if index % 2 == 0 else -1
-        if self.on_x(half, phase):
-            to = context_of(self.zpos, self.xpos + way)
-        else:
-            to = context_of(self.zpos + way, self.xpos)
-        slot = half * 20 + phase * 4 + index
-        return pltpu.make_async_remote_copy(
-            src_ref=ref,
-            dst_ref=ref,
-            send_sem=self.send.at[slot],
-            recv_sem=self.recv.at[slot],
-            device_id={"context": to},
-            device_id_type=MESH,
-        )
-
-    def start(self, half, phase, index):
-        copy = self.copy(half, phase, index, (0, 0, -1, 1)[index])
+def wrap(position):
+    return lax.rem(position + RING, RING)
+
+
+def context_of(zpos, xpos):
+    return wrap(zpos) * RING + wrap(xpos)
+
+
+class Ring:
+    def __init__(self, view, to, sems, sent):
+        self.view, self.to, self.sems, self.sent = view, to, sems, sent
+        self.waited = set()
+
+    def copy(self, index, step):
+        ref = self.view(step, max(0, index - 1))
+        return remote(ref, ref, self.sems, index, self.to(1 if index % 2 == 0 else -1))
+
+    def start(self, index):
+        copy = self.copy(index, (0, 0, -1, 1)[index])
         copy.start()
         self.sent.append(copy)
 
-    def arrive(self, half, phase, index):
-        if (half, phase, index) not in self.waited:
-            self.waited.add((half, phase, index))
-            self.copy(half, phase, index, (-1, 1, 2, 2)[index]).wait_recv()
-
-    def whole(self, half, phase):
-        self.start(half, phase, 0)
-        self.start(half, phase, 1)
-
-    def onward(self, half, phase):
-        self.arrive(half, phase, 0)
-        self.start(half, phase, 2)
-        self.arrive(half, phase, 1)
-        self.start(half, phase, 3)
-
-    def opposite(self, half, phase):
-        self.arrive(half, phase, 2)
-        self.arrive(half, phase, 3)
-
-    def stages(self):
-        def own():
-            for half in (0, 1):
-                self.whole(half, 0)
-                self.whole(half, 1)
-
-        def neighbours():
-            for half in (0, 1):
-                self.onward(half, 0)
-                self.whole(half, 2)
-                self.whole(half, 3)
-            for half in (0, 1):
-                self.onward(half, 1)
-
-        def far():
-            for half in (0, 1):
-                self.opposite(half, 0)
-                self.whole(half, 4)
-
-        def corners():
-            for half in (0, 1):
-                self.onward(half, 2)
-                self.onward(half, 3)
-
-        def last():
-            for half in (0, 1):
-                self.onward(half, 4)
-
-        def rest():
-            for half in (0, 1):
-                for phase in (1, 2, 3, 4):
-                    self.opposite(half, phase)
-
-        return [own, neighbours, far, corners, last, rest]
-
-    def drain(self):
-        for copy in self.sent:
-            copy.wait_send()
-
-
-def context_of(zpos, xpos):
-    return lax.rem(zpos + RING, RING) * RING + lax.rem(xpos + RING, RING)
+    def arrive(self, index):
+        if index not in self.waited:
+            self.waited.add(index)
+            self.copy(index, (-1, 1, 2, 2)[index]).wait_recv()
+
+    def whole(self):
+        self.start(0)
+        self.start(1)
+
+    def onward(self):
+        self.arrive(0)
+        self.start(2)
+        self.arrive(1)
+        self.start(3)
+
+    def opposite(self):
+        self.arrive(2)
+        self.arrive(3)
+
+
+def remote(src, dst, sems, index, to):
+    send, recv, base = sems
+    return pltpu.make_async_remote_copy(
+        src_ref=src,
+        dst_ref=dst,
+        send_sem=send.at[base + index],
+        recv_sem=recv.at[base + index],
+        device_id=to,
+        device_id_type=MESH,
+    )
+
+
+def context_gather(buf, extra, send, recv, zpos, xpos, sent):
+    half_rows = (buf.shape[1] - extra) // 2
+    part_rows = half_rows // 2
+    spans = (
+        ((0, half_rows), (0, part_rows), (part_rows, half_rows - part_rows)),
+        (
+            (half_rows, half_rows + extra),
+            (half_rows, part_rows),
+            (half_rows + part_rows, half_rows - part_rows + extra),
+        ),
+    )
+    rings = {}
+
+    def make(half, phase):
+        along_x = (half == 0) == (phase == 0)
+        first = 0 if phase == 0 else OFFSETS[phase - 1]
+
+        def view(step, part):
+            start, size = spans[half][part]
+            dz, dx = (first, step) if along_x else (step, first)
+            return buf.at[context_of(zpos + dz, xpos + dx), pl.ds(start, size), :]
+
+        def to(way):
+            dz, dx = (0, way) if along_x else (way, 0)
+            return {"context": context_of(zpos + dz, xpos + dx)}
+
+        return Ring(view, to, (send, recv, half * 20 + phase * 4), sent)
+
+    for half in (0, 1):
+        for phase in range(5):
+            rings[half, phase] = make(half, phase)
+
+    def own():
+        for half in (0, 1):
+            rings[half, 0].whole()
+            rings[half, 1].whole()
+
+    def neighbours():
+        for half in (0, 1):
+            rings[half, 0].onward()
+            rings[half, 2].whole()
+            rings[half, 3].whole()
+        for half in (0, 1):
+            rings[half, 1].onward()
+
+    def far():
+        for half in (0, 1):
+            rings[half, 0].opposite()
+            rings[half, 4].whole()
+
+    def corners():
+        for half in (0, 1):
+            rings[half, 2].onward()
+            rings[half, 3].onward()
+
+    def last():
+        for half in (0, 1):
+            rings[half, 4].onward()
+
+    def rest():
+        for half in (0, 1):
+            for phase in (1, 2, 3, 4):
+                rings[half, phase].opposite()
+
+    return [own, neighbours, far, corners, last, rest]
 
 
 def project_kernel(
+    span_count, select_count, cap,
     tok_ref, wq_ref, wk_ref, wv_ref, ex_ref,
-    q_ref, k_ref, v_ref,
-    tok, wq, wk, wv, acc,
-    wsend, wrecv, tsend, trecv, local_sem,
+    q_ref, own_ref, k_ref, v_ref, tab_ref,
+    tok, stage, w, acc, done, back,
+    load_sem, tsend, trecv, wsend, wrecv, bsend, brecv, qsend, qrecv,
 ):
     me = lax.axis_index("context")
     zpos, xpos = me // RING, lax.rem(me, RING)
     col = lax.axis_index("tensor")
     ypos, core = col // 2, lax.rem(col, 2)
-    mate = ypos * 2 + 1 - core
-    up = lax.rem(ypos + 1, RING) * 2 + core
-    down = lax.rem(ypos + RING - 1, RING) * 2 + core
-    token_count = tok.shape[1]
-
-    loads = [
-        pltpu.make_async_copy(tok_ref, tok.at[col], local_sem.at[0]),
-        pltpu.make_async_copy(wq_ref, wq.at[me], local_sem.at[1]),
-        pltpu.make_async_copy(wk_ref, wk.at[me], local_sem.at[2]),
-        pltpu.make_async_copy(wv_ref, wv.at[me], local_sem.at[3]),
-        pltpu.make_async_copy(
-            ex_ref, q_ref.at[me, pl.ds(token_count, EXTRA), :], local_sem.at[4]
-        ),
-    ]
-    for load in loads:
-        load.start()
-
+    token_count, depth = tok.shape[2], tok.shape[3]
+    rows = w.shape[3]
+    sent = []
+
+    token_load = pltpu.make_async_copy(tok_ref, tok.at[col, zpos], load_sem.at[0])
+    token_load.start()
+    extra_load = pltpu.make_async_copy(
+        ex_ref, q_ref.at[me, pl.ds(token_count, EXTRA), :], load_sem.at[1]
+    )
+    extra_load.start()
+    loads = ([], [])
+    for part in (0, 1):
+        for to in range(RING):
+            left = (wq_ref, wk_ref, wv_ref, wq_ref)[to]
+            pair = ((wq_ref, to), (left, RING)) if part == 0 else ((wk_ref, to), (wv_ref, to))
+            for i, (ref, head) in enumerate(pair):
+                load = pltpu.make_async_copy(
+                    ref.at[:, pl.ds(head * HDIM, HDIM)],
+                    stage.at[part, to, :, pl.ds(i * HDIM, HDIM)],
+                    load_sem.at[2 + part * 8 + to * 2 + i],
+                )
+                load.start()
+                loads[part].append(load)
+
+    def at_x(way):
+        return {"context": context_of(zpos, xpos + way)}
+
+    def at_z(way):
+        return {"context": context_of(zpos + way, xpos)}
+
+    def at_y(way):
+        return {"tensor": wrap(ypos + way) * 2 + core}
+
+    mate = {"tensor": ypos * 2 + 1 - core}
     barrier = pltpu.get_barrier_semaphore()
-    for dz, dx in ((1, 0), (-1, 0), (0, 1), (0, -1)):
-        pl.semaphore_signal(
-            barrier,
-            inc=1,
-            device_id={"context": context_of(zpos + dz, xpos + dx)},
-            device_id_type=MESH,
+    partners = [at_x(1), at_x(-1), at_z(1), at_z(-1), at_z(2), at_y(1), at_y(-1), mate]
+    for other in partners:
+        pl.semaphore_signal(barrier, inc=1, device_id=other, device_id_type=MESH)
+    pl.semaphore_wait(barrier, len(partners))
+
+    def cut(size):
+        return (pl.ds(0, size), pl.ds(0, size // 2), pl.ds(size // 2, size // 2))
+
+    ztok = Ring(
+        lambda step, part: tok.at[col, wrap(zpos + step), cut(token_count)[part]],
+        at_z, (tsend, trecv, 0), sent,
+    )
+    ytok = {
+        o: Ring(
+            lambda step, part, o=o: tok.at[
+                wrap(ypos + step) * 2 + core, wrap(zpos + o), cut(token_count)[part]
+            ],
+            at_y, (tsend, trecv, 4 + 4 * i), sent,
         )
-    for other in (up, down, mate):
-        pl.semaphore_signal(barrier, inc=1, device_id={"tensor": other}, device_id_type=MESH)
-    pl.semaphore_wait(barrier, 7)
-
-    tsent = []
-    part = token_count // 2
-
-    def tcopy(index, block, rows, to):
-        ref = tok.at[block, rows, :]
-        return pltpu.make_async_remote_copy(
-            src_ref=ref, dst_ref=ref, send_sem=tsend.at[index], recv_sem=trecv.at[index],
-            device_id={"tensor": to}, device_id_type=MESH,
+        for i, o in enumerate(OFFSETS)
+    }
+
+    def share(step, o, receive=False):
+        side = 1 - core if receive else core
+        ref = tok.at[wrap(ypos + step) * 2 + side, wrap(zpos + o)]
+        index = 20 + OFFSETS.index(step) * 4 + OFFSETS.index(o)
+        copy = remote(ref, ref, (tsend, trecv, 0), index, mate)
+        if receive:
+            copy.wait_recv()
+        else:
+            copy.start()
+            sent.append(copy)
+
+    def exchange(part, step, receive=False):
+        index = part * 3 + OFFSETS.index(step) - 1
+        src = stage.at[part, wrap(zpos + step)]
+        if receive:
+            dst = w.at[part, wrap(zpos - step), xpos]
+            remote(src, dst, (wsend, wrecv, 0), index, at_z(step)).wait_recv()
+        else:
+            copy = remote(src, w.at[part, zpos, xpos], (wsend, wrecv, 0), index, at_z(step))
+            copy.start()
+            sent.append(copy)
+
+    xw = {
+        (part, o): Ring(
+            lambda step, piece, part=part, o=o: w.at[
+                part, wrap(zpos + o), wrap(xpos + step), cut(rows)[piece]
+            ],
+            at_x, (wsend, wrecv, 6 + part * 16 + 4 * i), sent,
         )
-
-    def tstart(index, block, rows, to):
-        copy = tcopy(index, block, rows, to)
+        for part in (0, 1)
+        for i, o in enumerate(OFFSETS)
+    }
+
+    def keep(part):
+        for load in loads[part]:
+            load.wait()
+        copy = pltpu.make_async_copy(
+            stage.at[part, zpos], w.at[part, zpos, xpos], load_sem.at[18 + part]
+        )
         copy.start()
-        tsent.append(copy)
-
-    every = pl.ds(0, token_count)
-    low, high = pl.ds(0, part), pl.ds(part, part)
-    across = lax.rem(ypos + 2, RING) * 2 + core
-
-    gathers = [
-        ContextGather(buf, halves(buf.shape[1], extra), wsend.at[i], wrecv.at[i], zpos, xpos)
-        for i, (buf, extra) in enumerate(((wq, 0), (q_ref, EXTRA), (wk, 0), (wv, 0)))
-    ]
-    for_q, for_all, for_k, for_v = [g.stages() for g in gathers]
-
-    loads[0].wait()
-    loads[1].wait()
-    tstart(0, col, every, up)
-    tstart(1, col, every, down)
-    tstart(4, col, every, mate)
-    for_q[0]()
-    tcopy(0, down, every, up).wait_recv()
-    tstart(2, down, low, up)
-    tcopy(1, up, every, down).wait_recv()
-    tstart(3, up, high, down)
-    tstart(5, down, every, mate)
-    tstart(6, up, every, mate)
-    for_q[1]()
-    tcopy(2, across, low, up).wait_recv()
-    tcopy(3, across, high, down).wait_recv()
-    tstart(7, across, every, mate)
-    for stage in for_q[2:5]:
-        stage()
-    loads[2].wait()
-    for_k[0]()
-    for index, block in ((4, mate), (5, down), (6, up), (7, across)):
-        other = lax.rem(block, 2) * 0 + block // 2 * 2 + 1 - core
-        tcopy(index, other, every, mate).wait_recv()
-    for_q[5]()
-
-    def project(w):
-        @pl.loop(0, tok.shape[0])
-        def _(t):
-            base = pl.multiple_of(t * 2, 2)
-            piece = w[pl.ds(base, 2)].reshape(tok.shape[2], w.shape[2])
-            new = jnp.dot(tok[t], piece, preferred_element_type=jnp.float32)
-
-            @pl.when(t == 0)
-            def _():
-                acc[...] = new
-
-            @pl.when(t > 0)
-            def _():
-                acc[...] += new
-
-    project(wq)
-    q_ref[me, 0:token_count, :] = acc[...].astype(jnp.bfloat16)
-    loads[4].wait()
-    for_all[0]()
-    for step in range(1, 6):
-        for_all[step]()
-        for_k[step]()
-        if step == 3:
-            loads[3].wait()
-            for_v[0]()
-    project(wk)
-    k_ref[...] = acc[...].astype(jnp.bfloat16)
-    for step in range(1, 6):
-        for_v[step]()
-    project(wv)
-    v_ref[...] = acc[...].astype(jnp.bfloat16)
-    for copy in tsent:
+        copy.wait()
+
+    token_load.wait()
+    ztok.whole()
+    ytok[0].whole()
+    share(0, 0)
+    keep(0)
+    xw[0, 0].whole()
+    exchange(0, 1)
+    exchange(0, -1)
+    keep(1)
+    xw[1, 0].whole()
+    xw[0, 0].onward()
+    ztok.onward()
+    for o in (-1, 1):
+        ytok[o].whole()
+        share(0, o)
+    ytok[0].onward()
+    exchange(0, 2)
+    exchange(1, 1)
+    exchange(1, -1)
+    exchange(1, 2)
+    share(-1, 0)
+    share(1, 0)
+    for step in (1, -1):
+        exchange(0, step, receive=True)
+        xw[0, -step].whole()
+    xw[1, 0].onward()
+    ztok.opposite()
+    ytok[2].whole()
+    share(0, 2)
+    exchange(0, 2, receive=True)
+    xw[0, 2].whole()
+    for o in (-1, 1):
+        ytok[o].onward()
+        share(-1, o)
+        share(1, o)
+    xw[0, -1].onward()
+    xw[0, 1].onward()
+    for step in (1, -1):
+        exchange(1, step, receive=True)
+        xw[1, -step].whole()
+    ytok[0].opposite()
+    share(2, 0)
+    xw[0, 2].onward()
+    exchange(1, 2, receive=True)
+    xw[1, 2].whole()
+    ytok[2].onward()
+    share(-1, 2)
+    share(1, 2)
+    for o in (-1, 1, 2):
+        xw[1, o].onward()
+    for o in (-1, 1):
+        ytok[o].opposite()
+        share(2, o)
+
+    def compute(part, step):
+        for side in (0, 1):
+            t = wrap(ypos + step) * 2 + side
+            piece = w[part, wrap(ypos + step), 2 * side : 2 * side + 2].reshape(depth, w.shape[4])
+
+            @pl.loop(0, RING)
+            def _(z):
+                new = jnp.dot(tok[t, z], piece, preferred_element_type=jnp.float32)
+                if step == 0 and side == 0:
+                    acc[z] = new
+                else:
+                    acc[z] += new
+
+    def give_back(part):
+        @pl.loop(0, RING)
+        def _(z):
+            done[part, z] = acc[z].astype(jnp.bfloat16)
+
+        back[part, zpos] = acc[zpos].astype(jnp.bfloat16)
+        for i, step in enumerate(OFFSETS[1:]):
+            copy = remote(
+                done.at[part, wrap(zpos + step)], back.at[part, zpos],
+                (bsend, brecv, 0), part * 3 + i, at_z(step),
+            )
+            copy.start()
+            sent.append(copy)
+
+    def take_back(part):
+        for i, step in enumerate(OFFSETS[1:]):
+            ref = back.at[part, wrap(zpos - step)]
+            remote(ref, ref, (bsend, brecv, 0), part * 3 + i, at_z(step)).wait_recv()
+
+    for o in OFFSETS:
+        xw[0, o].opposite()
+    for step in OFFSETS[:3]:
+        for o in OFFSETS:
+            share(step, o, receive=True)
+        compute(0, step)
+    ytok[2].opposite()
+    share(2, 2)
+    for o in OFFSETS:
+        share(2, o, receive=True)
+    compute(0, 2)
+    give_back(0)
+    gather = context_gather(q_ref, EXTRA, qsend, qrecv, zpos, xpos, sent)
+    extra_load.wait()
+    take_back(0)
+    for head in range(RING + 1):
+        cols = slice(head * HDIM, (head + 1) * HDIM)
+        if head < RING:
+            piece = back[0, head, :, 0:HDIM]
+        else:
+            piece = back[0, 0, :, HDIM : 2 * HDIM]
+        q_ref[me, 0:token_count, cols] = piece
+        own_ref[:, cols] = piece
+    gather[0]()
+    for o in OFFSETS:
+        xw[1, o].opposite()
+    compute(1, 0)
+    gather[1]()
+    compute(1, -1)
+    gather[2]()
+    compute(1, 1)
+    gather[3]()
+    compute(1, 2)
+    give_back(1)
+    gather[4]()
+    take_back(1)
+    for head in range(RING):
+        cols = slice(head * HDIM, (head + 1) * HDIM)
+        k_ref[:, cols] = back[1, head, :, 0:HDIM]
+        v_ref[:, cols] = back[1, head, :, HDIM : 2 * HDIM]
+    k_ref[:, RING * HDIM :] = back[0, 1, :, HDIM : 2 * HDIM]
+    v_ref[:, RING * HDIM :] = back[0, 2, :, HDIM : 2 * HDIM]
+    gather[5]()
+
+    devices = q_ref.shape[0]
+    lane = lax.broadcasted_iota(jnp.int32, (devices, HDIM), 1)
+    before = lax.broadcasted_iota(jnp.int32, (HDIM, HDIM), 0)
+    after = lax.broadcasted_iota(jnp.int32, (HDIM, HDIM), 1)
+    earlier = jnp.where(before < after, 1.0, 0.0).astype(jnp.bfloat16)
+    told = q_ref[:, token_count:, 0:HDIM].astype(jnp.float32)
+    for half in range(span_count):
+        owner = told[:, half, :]
+        row = told[:, span_count + half, :]
+        mine = jnp.where((owner == me.astype(jnp.float32)) & (lane < select_count), 1.0, 0.0)
+        rank = jnp.dot(mine.astype(jnp.bfloat16), earlier, preferred_element_type=jnp.float32)
+        table = jnp.where(lane == cap, jnp.sum(mine, axis=1, keepdims=True), 0.0)
+        for r in range(cap):
+            value = jnp.sum(jnp.where(rank == r, mine * row, 0.0), axis=1, keepdims=True)
+            table = jnp.where(lane == r, value, table)
+        tab_ref[half] = table.astype(jnp.int32)
+
+    for copy in sent:
         copy.wait_send()
-    for gather in gathers:
-        gather.drain()
-
-
-def gather_project(tokens, wq, wk, wv, extra):
+
+
+def gather_project(tokens, wq, wk, wv, extra, span_count, select_count, cap):
     token_count, depth = tokens.shape
     rows, width = wq.shape
     devices = lax.axis_size("context")
     columns = lax.axis_size("tensor")
     hbm = pl.BlockSpec(memory_space=pl.ANY)
     vmem = pl.BlockSpec(memory_space=pltpu.VMEM)
-    weight = pltpu.VMEM((devices, rows, width), jnp.bfloat16)
+    own = jax.ShapeDtypeStruct((token_count, width), jnp.bfloat16)
+    two = 2 * HDIM
+
+    def dma(count):
+        return [pltpu.SemaphoreType.DMA((count,))] * 2
+
     return pl.pallas_call(
-        project_kernel,
+        functools.partial(project_kernel, span_count, select_count, cap),
         in_specs=[hbm] * 5,
-        out_specs=[vmem] * 3,
+        out_specs=[vmem] * 5,
         out_shape=[
             jax.ShapeDtypeStruct((devices, token_count + EXTRA, width), jnp.bfloat16),
-            jax.ShapeDtypeStruct((token_count, width), jnp.bfloat16),
-            jax.ShapeDtypeStruct((token_count, width), jnp.bfloat16),
+            own,
+            own,
+            own,
+            jax.ShapeDtypeStruct((span_count, devices, HDIM), jnp.int32),
         ],
         scratch_shapes=[
-            pltpu.VMEM((columns, token_count, depth), jnp.bfloat16),
-            weight,
-            weight,
-            weight,
-            pltpu.VMEM((token_count, width), jnp.float32),
-            pltpu.SemaphoreType.DMA((4, 40)),
-            pltpu.SemaphoreType.DMA((4, 40)),
-            pltpu.SemaphoreType.DMA((8,)),
-            pltpu.SemaphoreType.DMA((8,)),
-            pltpu.SemaphoreType.DMA((5,)),
-        ],
+            pltpu.VMEM((columns, RING, token_count, depth), jnp.bfloat16),
+            pltpu.VMEM((2, RING, rows, two), jnp.bfloat16),
+            pltpu.VMEM((2, RING, RING, rows, two), jnp.bfloat16),
+            pltpu.VMEM((RING, token_count, two), jnp.float32),
+            pltpu.VMEM((2, RING, token_count, two), jnp.bfloat16),
+            pltpu.VMEM((2, RING, token_count, two), jnp.bfloat16),
+            pltpu.SemaphoreType.DMA((20,)),
+        ]
+        + dma(36)
+        + dma(38)
+        + dma(6)
+        + dma(40),
         compiler_params=pltpu.CompilerParams(
             collective_id=0, has_side_effects=True, vmem_limit_bytes=60 << 20
         ),
@@ -299,7 +452,7 @@
     )(tokens, wq, wk, wv, extra)
 
 
-def owner_kernel(heads, cap, rows_ref, n_ref, q_ref, k_ref, v_ref, o_ref, st_ref, acc_ref):
+def owner_kernel(heads, cap, tab_ref, q_ref, k_ref, v_ref, o_ref, st_ref, acc_ref):
     src = pl.program_id(0)
     span_count = o_ref.shape[1]
     span = o_ref.shape[3]
@@ -307,10 +460,9 @@
     columns = [slice(h * HDIM, (h + 1) * HDIM) for h in range(heads)]
 
     def scores(half, j):
-        c = src * span_count + half
-        n = n_ref[c]
-        r0 = rows_ref[c * cap + 2 * j]
-        r1 = rows_ref[c * cap + 2 * j + 1]
+        n = tab_ref[half, src, cap]
+        r0 = tab_ref[half, src, 2 * j]
+        r1 = tab_ref[half, src, 2 * j + 1]
         bias0 = jnp.where(2 * j < n, 0.0, NEG)
         bias1 = jnp.where(2 * j + 1 < n, 0.0, NEG)
         out = []
@@ -336,7 +488,7 @@
             o_ref[0, half, columns[h], :] = (a * (1.0 / l)).astype(jnp.bfloat16)
 
     for half in range(span_count):
-        n = n_ref[src * span_count + half]
+        n = tab_ref[half, src, cap]
 
         @pl.when(n > 2)
         def _():
@@ -364,15 +516,15 @@
                 ).astype(jnp.bfloat16)
 
 
-def owner_attention(rows, n, q_all, cache_keys, cache_values, heads, cap):
+def owner_attention(table, q_all, cache_keys, cache_values, heads, cap):
     devices, tokens, width = q_all.shape
-    span_count = n.shape[0] // devices
+    span_count = table.shape[0]
     span = (tokens - EXTRA) // span_count
     whole = pl.BlockSpec(cache_keys.shape, lambda s, *_: (0, 0, 0), pipeline_mode=pl.Buffered(1))
     return pl.pallas_call(
         functools.partial(owner_kernel, heads, cap),
         grid_spec=pltpu.PrefetchScalarGridSpec(
-            num_scalar_prefetch=2,
+            num_scalar_prefetch=1,
             grid=(devices,),
             in_specs=[
                 pl.BlockSpec((1, tokens, width), lambda s, *_: (s, 0, 0)),
@@ -389,7 +541,7 @@
             jax.ShapeDtypeStruct((devices, span_count, width, span), jnp.bfloat16),
             jax.ShapeDtypeStruct((devices, span_count, 16, span), jnp.float32),
         ],
-    )(rows, n, q_all, cache_keys, cache_values)
+    )(table, q_all, cache_keys, cache_values)
 
 
 def combine_kernel(
@@ -451,9 +603,6 @@
 
     def second_at(half):
         return zpos if half == 0 else xpos
-
-    def wrap(position):
-        return lax.rem(position + RING, RING)
 
     def held(ref, half, step, low):
         to = wrap(first_at(half) + step)
@@ -506,7 +655,7 @@
 
     def local(half, h, keys, values, bias, first):
         cols = slice(h * HDIM, (h + 1) * HDIM)
-        q = q_ref[0, half * span : (half + 1) * span, cols]
+        q = q_ref[half * span : (half + 1) * span, cols]
         s = dot_nt(keys, q) * SCALE
         s = jnp.where(key <= row, s, NEG) if bias is None else s + bias
         m = jnp.max(s, axis=0, keepdims=True)
@@ -680,19 +829,6 @@
     return jnp.pad(both, ((0, EXTRA - 2 * span_count), (0, width - select_count)))
 
 
-def owner_table(extra, span_count, select_count, cap):
-    owner = extra[:, :span_count, :select_count].reshape(-1, select_count).astype(jnp.int32)
-    row = extra[:, span_count : 2 * span_count, :select_count]
-    row = row.reshape(-1, select_count).astype(jnp.int32)
-    mine = owner == lax.axis_index("context")
-    position = jnp.arange(select_count)
-    earlier = position[None, :] < position[:, None]
-    rank = jnp.sum(jnp.where(mine[:, None, :] & earlier[None], 1, 0), axis=2)
-    place = mine[:, :, None] & (rank[:, :, None] == jnp.arange(cap)[None, None, :])
-    rows = jnp.sum(jnp.where(place, row[:, :, None], 0), axis=1)
-    return rows.reshape(-1).astype(jnp.int32), jnp.sum(mine, axis=1).astype(jnp.int32)
-
-
 def shards(
     tokens,
     query_weight,
@@ -712,11 +848,10 @@
     cap = max(2, 2 * span_count * select_count // devices)
 
     extra = chosen_slots(selected, counts, block_slot, cache_keys.shape[0], width)
-    q_all, k, v = gather_project(tokens, query_weight, key_weight, value_weight, extra)
-    rows, n = owner_table(q_all[:, token_count:], span_count, select_count, cap)
-    o, st = owner_attention(rows, n, q_all, cache_keys, cache_values, heads, cap)
-    me = lax.axis_index("context")
-    q = lax.dynamic_slice(q_all, (me, 0, 0), (1, token_count, width))
+    q_all, q, k, v, table = gather_project(
+        tokens, query_weight, key_weight, value_weight, extra, span_count, select_count, cap
+    )
+    o, st = owner_attention(table, q_all, cache_keys, cache_values, heads, cap)
     return combine(o, st, q, k, v, heads)
 
 

time: 231 us -> 185 us (0.80)
  Pallas kernels: 219 us -> 179 us
  local copies, waits for them, and re-layouts: 5.59 us -> 1.73 us
  other arithmetic: 4.58 us -> 2.23 us
    pallas_call x1, Pallas kernels: 152 us -> 109 us  [gather_project(): pl.pallas_call(functools.partial(project_kernel, span_count, select_count...]
    pallas_call x1, Pallas kernels: 21 us -> 23.4 us  [owner_attention(): pl.pallas_call(functools.partial(owner_kernel, heads, cap), grid_spec=plt...]
    reduce_sum x3 -> x0, other arithmetic: 2.34 us -> none  [the longest x1 1.1 us: owner_table(): jnp.sum(mine, axis=1).astype(jnp.int32)]
where the time goes in v4:
time: 185 us; the launch traced here: 183 us
  Pallas kernels  179 us (97%)
  other arithmetic  2.23 us (1%)
    pallas_call x1, Pallas kernels, gather_project(): pl.pallas_call(functools.partial(project_kernel, span_count, select_count...  109 us
    pallas_call x1, Pallas kernels, combine(): pl.pallas_call(functools.partial(combine_kernel, heads), in_specs=[vmem]...  46.9 us
    pallas_call x1, Pallas kernels, owner_attention(): pl.pallas_call(functools.partial(owner_kernel, heads, cap), grid_spec=plt...  23.4 us

profile of v4, /device:TPU:0, one launch (start us, length us, event | category | flops | bytes accessed | tf_op | source)
XLA Modules:
  0.0 183.3 jit_solution(8780033737863723560)
XLA Ops:
  0.0 0.9 select_reduce_fusion
  0.9 0.7 fusion.6
  1.6 0.6 fusion.5.ex_ref
  2.2 109.0 %gather_project.1 = (bf16[16,272,640]{2,1,0:T(8,128)(2,1)}, bf16[256,640]{1,0:T(8,128)(2,1)}, bf16[256,640]{1,0:T(8,128)(2,1)}, bf16[256,640]{1,0:T(8,128)(2,1)}, s32[2,16,128]{2,1,0:T(8,128)}) custom-call(bf16[256,640]{1,0:T(8,128)(2,1)} %tok_ref.1, bf16[320,640]{1,0:T(8,128)(2,1)} %wq_ref.1, bf16[320,640]{1,0:T(8,128)(2,1)} %wk_ref.1, ...), custom_call_target="tpu_custom_call" | custom-call | tf_op jit(solution)/shard_map/gather_project/pallas_call | solution.py:424
  111.3 23.4 %shard_map.91 = (bf16[16,2,640,128]{3,2,1,0:T(8,128)(2,1)}, f32[16,2,16,128]{3,2,1,0:T(8,128)}) custom-call(s32[2,16,128]{2,1,0:T(8,128)} %get-tuple-element.12.tab_ref, bf16[16,272,640]{2,1,0:T(8,128)(2,1)} %get-tuple-element.13.q_ref, bf16[32,64,640]{2,1,0:T(8,128)(2,1)} %k_ref.1, bf16[32,64,640]{2,1,0:T(8,128)(2,1)} %v_ref.1), custom_call_target="tpu_custom_call" | custom-call | tf_op jit(solution)/shard_map/pallas_call | solution.py:524
  134.7 46.9 %combine.1 = bf16[256,640]{1,0:T(8,128)(2,1)} custom-call(bf16[4,4,2,640,128]{4,3,2,1,0:T(8,128)(2,1)} %bitcast.2, f32[4,4,2,16,128]{4,3,2,1,0:T(8,128)} %bitcast.3, bf16[256,640]{1,0:T(8,128)(2,1)} %get-tuple-element.16.q_ref, bf16[256,640]{1,0:T(8,128)(2,1)} %get-tuple-element.17.k_ref, bf16[256,640]{1,0:T(8,128)(2,1)} %get-tuple-element.18.v_ref), custom_call_target="tpu_custom_call" | custom-call | tf_op jit(solution)/shard_map/combine/pallas_call | solution.py:798
  181.6 1.7 copy.11

commit v5 on v4

v5 whole, which is shorter than its diff:
```python
import functools

import jax
import jax.numpy as jnp
from jax import lax
from jax.experimental import pallas as pl
from jax.experimental.pallas import tpu as pltpu
from jax.sharding import PartitionSpec as P

HDIM = 128
NEG = -1e30
MESH = pl.DeviceIdType.MESH
EXTRA = 16
SCALE = HDIM ** (-0.5) * 1.4426950408889634


def dot_nt(a, b):
    return lax.dot_general(a, b, (((1,), (1,)), ((), ())), preferred_element_type=jnp.float32)


def dot_tn(a, b):
    return lax.dot_general(a, b, (((0,), (0,)), ((), ())), preferred_element_type=jnp.float32)


RING = 4
OFFSETS = (0, -1, 1, 2)


def wrap(position):
    return lax.rem(position + RING, RING)


def context_of(zpos, xpos):
    return wrap(zpos) * RING + wrap(xpos)


class Ring:
    def __init__(self, view, to, sems, sent, own=None):
        self.view, self.to, self.sems, self.sent, self.own = view, to, sems, sent, own
        self.waited = set()

    def copy(self, index, step):
        ref = self.view(step, max(0, index - 1))
        src = self.own if step == 0 and self.own is not None else ref
        return remote(src, ref, self.sems, index, self.to(1 if index % 2 == 0 else -1))

    def start(self, index):
        copy = self.copy(index, (0, 0, -1, 1)[index])
        copy.start()
        self.sent.append(copy)

    def arrive(self, index):
        if index not in self.waited:
            self.waited.add(index)
            self.copy(index, (-1, 1, 2, 2)[index]).wait_recv()

    def whole(self):
        self.start(0)
        self.start(1)

    def onward(self):
        self.arrive(0)
        self.start(2)
        self.arrive(1)
        self.start(3)

    def opposite(self):
        self.arrive(2)
        self.arrive(3)


def remote(src, dst, sems, index, to):
    send, recv, base = sems
    return pltpu.make_async_remote_copy(
        src_ref=src,
        dst_ref=dst,
        send_sem=send.at[base + index],
        recv_sem=recv.at[base + index],
        device_id=to,
        device_id_type=MESH,
    )


def context_gather(view, own, sems, zpos, xpos, sent):
    rings = {}

    def make(half, phase):
        along_x = (half == 0) == (phase == 0)
        first = 0 if phase == 0 else OFFSETS[phase - 1]

        def piece(step, part):
            dz, dx = (first, step) if along_x else (step, first)
            return view(wrap(zpos + dz), wrap(xpos + dx), half, part)

        def to(way):
            dz, dx = (0, way) if along_x else (way, 0)
            return {"context": context_of(zpos + dz, xpos + dx)}

        send, recv, base = sems
        source = own(half) if first == 0 else None
        return Ring(piece, to, (send, recv, base + half * 20 + phase * 4), sent, source)

    for half in (0, 1):
        for phase in range(5):
            rings[half, phase] = make(half, phase)

    def own():
        for half in (0, 1):
            rings[half, 0].whole()
            rings[half, 1].whole()

    def neighbours():
        for half in (0, 1):
            rings[half, 0].onward()
            rings[half, 2].whole()
            rings[half, 3].whole()
        for half in (0, 1):
            rings[half, 1].onward()

    def far():
        for half in (0, 1):
            rings[half, 0].opposite()
            rings[half, 4].whole()

    def corners():
        for half in (0, 1):
            rings[half, 2].onward()
            rings[half, 3].onward()

    def last():
        for half in (0, 1):
            rings[half, 4].onward()

    def rest():
        for half in (0, 1):
            for phase in (1, 2, 3, 4):
                rings[half, phase].opposite()

    return [own, neighbours, far, corners, last, rest]


def project_kernel(
    span_count, select_count, cap, stored,
    tok_ref, wq_ref, wk_ref, wv_ref, sel_ref, count_ref, slot_ref,
    q_ref, k_ref, v_ref, tab_ref,
    tok, stage, w, acc, done, back, fifth, small, told,
    load_sem, tsend, trecv, wsend, wrecv, bsend, brecv, qsend, qrecv,
):
    me = lax.axis_index("context")
    zpos, xpos = me // RING, lax.rem(me, RING)
    col = lax.axis_index("tensor")
    ypos, core = col // 2, lax.rem(col, 2)
    token_count, depth = tok.shape[2], tok.shape[3]
    rows = w.shape[3]
    sent = []

    token_load = pltpu.make_async_copy(tok_ref, tok.at[col, zpos], load_sem.at[0])
    token_load.start()
    loads = ([], [])
    for part in (0, 1):
        for to in range(RING):
            left = (wq_ref, wk_ref, wv_ref, wq_ref)[to]
            pair = ((wq_ref, to), (left, RING)) if part == 0 else ((wk_ref, to), (wv_ref, to))
            for i, (ref, head) in enumerate(pair):
                load = pltpu.make_async_copy(
                    ref.at[:, pl.ds(head * HDIM, HDIM)],
                    stage.at[part, to, :, pl.ds(i * HDIM, HDIM)],
                    load_sem.at[2 + part * 8 + to * 2 + i],
                )
                load.start()
                loads[part].append(load)

    def at_x(way):
        return {"context": context_of(zpos, xpos + way)}

    def at_z(way):
        return {"context": context_of(zpos + way, xpos)}

    def at_y(way):
        return {"tensor": wrap(ypos + way) * 2 + core}

    mate = {"tensor": ypos * 2 + 1 - core}
    barrier = pltpu.get_barrier_semaphore()
    partners = [at_x(1), at_x(-1), at_z(1), at_z(-1), at_z(2), at_y(1), at_y(-1), mate]
    for other in partners:
        pl.semaphore_signal(barrier, inc=1, device_id=other, device_id_type=MESH)
    pl.semaphore_wait(barrier, len(partners))

    def cut(size):
        return (pl.ds(0, size), pl.ds(0, size // 2), pl.ds(size // 2, size // 2))

    ztok = Ring(
        lambda step, part: tok.at[col, wrap(zpos + step), cut(token_count)[part]],
        at_z, (tsend, trecv, 0), sent,
    )
    ytok = {
        o: Ring(
            lambda step, part, o=o: tok.at[
                wrap(ypos + step) * 2 + core, wrap(zpos + o), cut(token_count)[part]
            ],
            at_y, (tsend, trecv, 4 + 4 * i), sent,
        )
        for i, o in enumerate(OFFSETS)
    }

    def share(step, o, receive=False):
        side = 1 - core if receive else core
        ref = tok.at[wrap(ypos + step) * 2 + side, wrap(zpos + o)]
        index = 20 + OFFSETS.index(step) * 4 + OFFSETS.index(o)
        copy = remote(ref, ref, (tsend, trecv, 0), index, mate)
        if receive:
            copy.wait_recv()
        else:
            copy.start()
            sent.append(copy)

    def exchange(part, step, receive=False):
        index = part * 3 + OFFSETS.index(step) - 1
        src = stage.at[part, wrap(zpos + step)]
        if receive:
            dst = w.at[part, wrap(zpos - step), xpos]
            remote(src, dst, (wsend, wrecv, 0), index, at_z(step)).wait_recv()
        else:
            copy = remote(src, w.at[part, zpos, xpos], (wsend, wrecv, 0), index, at_z(step))
            copy.start()
            sent.append(copy)

    xw = {
        (part, o): Ring(
            lambda step, piece, part=part, o=o: w.at[
                part, wrap(zpos + o), wrap(xpos + step), cut(rows)[piece]
            ],
            at_x, (wsend, wrecv, 6 + part * 16 + 4 * i), sent,
        )
        for part in (0, 1)
        for i, o in enumerate(OFFSETS)
    }

    def keep(part):
        for load in loads[part]:
            load.wait()
        copy = pltpu.make_async_copy(
            stage.at[part, zpos], w.at[part, zpos, xpos], load_sem.at[18 + part]
        )
        copy.start()
        copy.wait()

    token_load.wait()
    ztok.whole()
    ytok[0].whole()
    share(0, 0)
    keep(0)
    xw[0, 0].whole()
    exchange(0, 1)
    exchange(0, -1)
    keep(1)
    xw[1, 0].whole()
    xw[0, 0].onward()
    ztok.onward()
    for o in (-1, 1):
        ytok[o].whole()
        share(0, o)
    ytok[0].onward()
    exchange(0, 2)
    exchange(1, 1)
    exchange(1, -1)
    exchange(1, 2)
    share(-1, 0)
    share(1, 0)
    for step in (1, -1):
        exchange(0, step, receive=True)
        xw[0, -step].whole()
    xw[1, 0].onward()
    ztok.opposite()
    ytok[2].whole()
    share(0, 2)
    exchange(0, 2, receive=True)
    xw[0, 2].whole()
    for o in (-1, 1):
        ytok[o].onward()
        share(-1, o)
        share(1, o)
    xw[0, -1].onward()
    xw[0, 1].onward()
    for step in (1, -1):
        exchange(1, step, receive=True)
        xw[1, -step].whole()
    ytok[0].opposite()
    share(2, 0)
    xw[0, 2].onward()
    exchange(1, 2, receive=True)
    xw[1, 2].whole()
    ytok[2].onward()
    share(-1, 2)
    share(1, 2)
    for o in (-1, 1, 2):
        xw[1, o].onward()
    for o in (-1, 1):
        ytok[o].opposite()
        share(2, o)

    def compute(part, step):
        for side in (0, 1):
            t = wrap(ypos + step) * 2 + side
            piece = w[part, wrap(ypos + step), 2 * side : 2 * side + 2].reshape(depth, w.shape[4])

            @pl.loop(0, RING)
            def _(z):
                new = jnp.dot(tok[t, z], piece, preferred_element_type=jnp.float32)
                if step == 0 and side == 0:
                    acc[z] = new
                else:
                    acc[z] += new

    def give_back(part, buf, columns, base):
        buf[zpos] = acc[zpos, :, columns].astype(jnp.bfloat16)
        for i, step in enumerate(OFFSETS[1:]):
            copy = remote(
                done.at[part, wrap(zpos + step), :, columns], buf.at[zpos],
                (bsend, brecv, base), i, at_z(step),
            )
            copy.start()
            sent.append(copy)

    def take_back(buf, base):
        for i, step in enumerate(OFFSETS[1:]):
            ref = buf.at[wrap(zpos - step)]
            remote(ref, ref, (bsend, brecv, base), i, at_z(step)).wait_recv()

    def finish(part):
        @pl.loop(0, RING)
        def _(z):
            done[part, z] = acc[z].astype(jnp.bfloat16)

    lane = lax.broadcasted_iota(jnp.int32, (EXTRA, HDIM), 1)
    line = lax.broadcasted_iota(jnp.int32, (EXTRA, HDIM), 0)
    chosen = jnp.zeros((EXTRA, HDIM), jnp.int32)
    for half in range(span_count):

        def note(j, chosen, half=half):
            slot = slot_ref[jnp.maximum(sel_ref[half, j], 0)]
            owner = jnp.where(j < count_ref[half], slot // stored, -1)
            value = jnp.where(line == half, owner, slot % stored)
            here = (lane == j) & ((line == half) | (line == span_count + half))
            return jnp.where(here, value, chosen)

        chosen = lax.fori_loop(0, select_count, note, chosen)
    small[token_count:, :] = chosen.astype(jnp.float32).astype(jnp.bfloat16)

    for o in OFFSETS:
        xw[0, o].opposite()
    for step in OFFSETS[:3]:
        for o in OFFSETS:
            share(step, o, receive=True)
        compute(0, step)
    ytok[2].opposite()
    share(2, 2)
    for o in OFFSETS:
        share(2, o, receive=True)
    compute(0, 2)
    finish(0)

    groups = RING // 2

    def head_view(z, x, half, part):
        low, size = ((0, groups), (0, groups // 2), (groups // 2, groups // 2))[part]
        head = pl.ds(pl.multiple_of(z * HDIM, HDIM), HDIM)
        return q_ref.at[pl.ds(half * groups + low, size), x, pl.ds(0, token_count), head]

    def head_own(half):
        return done.at[0, pl.ds(half * groups, groups), :, pl.ds(0, HDIM)]

    heads = context_gather(head_view, head_own, (qsend, qrecv, 0), zpos, xpos, sent)

    half_rows = token_count // 2
    quarter = half_rows // 2
    ranges = (
        ((0, half_rows), (0, quarter), (quarter, quarter)),
        (
            (half_rows, half_rows + EXTRA),
            (half_rows, quarter),
            (half_rows + quarter, quarter + EXTRA),
        ),
    )

    def last_view(z, x, half, part):
        return q_ref.at[z, x, pl.ds(*ranges[half][part]), pl.ds(RING * HDIM, HDIM)]

    def last_own(half):
        return small.at[pl.ds(*ranges[half][0]), :]

    last = context_gather(last_view, last_own, (qsend, qrecv, 40), zpos, xpos, sent)

    heads[0]()
    give_back(0, fifth, slice(HDIM, 2 * HDIM), 0)
    keeps = [
        pltpu.make_async_copy(
            done.at[0, :, :, pl.ds(0, HDIM)],
            q_ref.at[
                :, xpos, pl.ds(0, token_count), pl.ds(pl.multiple_of(zpos * HDIM, HDIM), HDIM)
            ],
            load_sem.at[1],
        )
    ]
    keeps[0].start()
    for o in OFFSETS:
        xw[1, o].opposite()
    compute(1, 0)
    take_back(fifth, 0)
    small[0:token_count, :] = fifth[0]
    last[0]()
    keeps.append(
        pltpu.make_async_copy(
            small, q_ref.at[zpos, xpos, :, pl.ds(RING * HDIM, HDIM)], load_sem.at[20]
        )
    )
    keeps[1].start()
    heads[1]()
    compute(1, -1)
    heads[2]()
    last[1]()
    compute(1, 1)
    heads[3]()
    last[2]()
    compute(1, 2)
    finish(1)
    give_back(1, back, slice(0, 2 * HDIM), 3)
    heads[4]()
    last[3]()
    last[4]()
    for keep_copy in keeps:
        keep_copy.wait()
    heads[5]()
    last[5]()
    look = pltpu.make_async_copy(
        q_ref.at[:, :, pl.ds(token_count, EXTRA), pl.ds(RING * HDIM, HDIM)],
        told,
        load_sem.at[21],
    )
    look.start()
    take_back(back, 3)
    for head in range(RING):
        cols = slice(head * HDIM, (head + 1) * HDIM)
        k_ref[:, cols] = back[head, :, 0:HDIM]
        v_ref[:, cols] = back[head, :, HDIM : 2 * HDIM]
    k_ref[:, RING * HDIM :] = fifth[1]
    v_ref[:, RING * HDIM :] = fifth[2]
    look.wait()

    devices = RING * RING
    lane = lax.broadcasted_iota(jnp.int32, (devices, HDIM), 1)
    before = lax.broadcasted_iota(jnp.int32, (HDIM, HDIM), 0)
    after = lax.broadcasted_iota(jnp.int32, (HDIM, HDIM), 1)
    earlier = jnp.where(before < after, 1.0, 0.0).astype(jnp.bfloat16)
    listed = told[...].reshape(devices, EXTRA, HDIM).astype(jnp.float32)
    for half in range(span_count):
        owner = listed[:, half, :]
        row = listed[:, span_count + half, :]
        mine = jnp.where((owner == me.astype(jnp.float32)) & (lane < select_count), 1.0, 0.0)
        rank = jnp.dot(mine.astype(jnp.bfloat16), earlier, preferred_element_type=jnp.float32)
        table = jnp.where(lane == cap, jnp.sum(mine, axis=1, keepdims=True), 0.0)
        for r in range(cap):
            value = jnp.sum(jnp.where(rank == r, mine * row, 0.0), axis=1, keepdims=True)
            table = jnp.where(lane == r, value, table)
        tab_ref[half] = table.astype(jnp.int32)

    for copy in sent:
        copy.wait_send()


def gather_project(tokens, wq, wk, wv, selected, counts, block_slot, cap, stored):
    token_count, depth = tokens.shape
    rows, width = wq.shape
    span_count, select_count = selected.shape
    devices = lax.axis_size("context")
    columns = lax.axis_size("tensor")
    hbm = pl.BlockSpec(memory_space=pl.ANY)
    vmem = pl.BlockSpec(memory_space=pltpu.VMEM)
    smem = pl.BlockSpec(memory_space=pltpu.SMEM)
    own = jax.ShapeDtypeStruct((token_count, width), jnp.bfloat16)
    two = 2 * HDIM

    def dma(count):
        return [pltpu.SemaphoreType.DMA((count,))] * 2

    return pl.pallas_call(
        functools.partial(project_kernel, span_count, select_count, cap, stored),
        in_specs=[hbm] * 4 + [smem] * 3,
        out_specs=[hbm] + [vmem] * 3,
        out_shape=[
            jax.ShapeDtypeStruct((RING, RING, token_count + EXTRA, width), jnp.bfloat16),
            own,
            own,
            jax.ShapeDtypeStruct((span_count, devices, HDIM), jnp.int32),
        ],
        scratch_shapes=[
            pltpu.VMEM((columns, RING, token_count, depth), jnp.bfloat16),
            pltpu.VMEM((2, RING, rows, two), jnp.bfloat16),
            pltpu.VMEM((2, RING, RING, rows, two), jnp.bfloat16),
            pltpu.VMEM((RING, token_count, two), jnp.float32),
            pltpu.VMEM((2, RING, token_count, two), jnp.bfloat16),
            pltpu.VMEM((RING, token_count, two), jnp.bfloat16),
            pltpu.VMEM((RING, token_count, HDIM), jnp.bfloat16),
            pltpu.VMEM((token_count + EXTRA, HDIM), jnp.bfloat16),
            pltpu.VMEM((RING, RING, EXTRA, HDIM), jnp.bfloat16),
            pltpu.SemaphoreType.DMA((22,)),
        ]
        + dma(36)
        + dma(38)
        + dma(6)
        + dma(80),
        compiler_params=pltpu.CompilerParams(
            collective_id=0, has_side_effects=True, vmem_limit_bytes=40 << 20
        ),
        name="gather_project",
    )(tokens, wq, wk, wv, selected, counts, block_slot)


def owner_kernel(heads, cap, tab_ref, q_ref, k_ref, v_ref, o_ref, st_ref, acc_ref):
    src = pl.program_id(0)
    span_count = o_ref.shape[1]
    span = o_ref.shape[3]
    block = k_ref.shape[1]
    columns = [slice(h * HDIM, (h + 1) * HDIM) for h in range(heads)]

    def scores(half, j):
        n = tab_ref[half, src, cap]
        r0 = tab_ref[half, src, 2 * j]
        r1 = tab_ref[half, src, 2 * j + 1]
        bias1 = jnp.where(2 * j + 1 < n, 0.0, NEG)
        out = []
        for cols in columns:
            q = q_ref[0, half * span : (half + 1) * span, cols]
            k = jnp.concatenate([k_ref[r0, :, cols], k_ref[r1, :, cols]], 0)
            v = jnp.concatenate([v_ref[r0, :, cols], v_ref[r1, :, cols]], 0)
            s = dot_nt(k, q) * SCALE
            out.append((jnp.concatenate([s[:block], s[block:] + bias1], 0), v))
        return out

    for half in range(span_count):
        results = []
        for s, v in scores(half, 0):
            m = jnp.max(s, axis=0, keepdims=True)
            p = jnp.exp2(s - m)
            l = jnp.sum(p, axis=0, keepdims=True)
            results.append((m, l, dot_tn(v, p.astype(jnp.bfloat16))))
        some = tab_ref[half, src, cap] > 0
        for h, (m, l, a) in enumerate(results):
            st_ref[0, half, h : h + 1, :] = jnp.where(some, m, NEG)
            st_ref[0, half, 8 + h : 9 + h, :] = l
            acc_ref[half, columns[h], :] = a
            o_ref[0, half, columns[h], :] = a.astype(jnp.bfloat16)

    for half in range(span_count):
        n = tab_ref[half, src, cap]

        @pl.when(n > 2)
        def _():
            @pl.loop(1, (n + 1) // 2)
            def _(j):
                results = []
                for h, (s, v) in enumerate(scores(half, j)):
                    old = st_ref[0, half, h : h + 1, :]
                    m = jnp.maximum(jnp.max(s, axis=0, keepdims=True), old)
                    decay = jnp.exp2(old - m)
                    p = jnp.exp2(s - m)
                    l = jnp.sum(p, axis=0, keepdims=True)
                    l = l + st_ref[0, half, 8 + h : 9 + h, :] * decay
                    a = dot_tn(v, p.astype(jnp.bfloat16)) + acc_ref[half, columns[h], :] * decay
                    results.append((m, l, a))
                for h, (m, l, a) in enumerate(results):
                    st_ref[0, half, h : h + 1, :] = m
                    st_ref[0, half, 8 + h : 9 + h, :] = l
                    acc_ref[half, columns[h], :] = a

            for h in range(heads):
                o_ref[0, half, columns[h], :] = acc_ref[half, columns[h], :].astype(jnp.bfloat16)


def owner_attention(table, q_all, cache_keys, cache_values, heads, cap):
    tokens, width = q_all.shape[2] - EXTRA, q_all.shape[3]
    span_count, devices = table.shape[:2]
    span = tokens // span_count
    q_all = q_all.reshape(devices, tokens + EXTRA, width)
    whole = pl.BlockSpec(cache_keys.shape, lambda s, *_: (0, 0, 0), pipeline_mode=pl.Buffered(1))
    return pl.pallas_call(
        functools.partial(owner_kernel, heads, cap),
        grid_spec=pltpu.PrefetchScalarGridSpec(
            num_scalar_prefetch=1,
            grid=(devices,),
            in_specs=[
                pl.BlockSpec((1, tokens, width), lambda s, *_: (s, 0, 0)),
                whole,
                whole,
            ],
            out_specs=[
                pl.BlockSpec((1, span_count, width, span), lambda s, *_: (s, 0, 0, 0)),
                pl.BlockSpec((1, span_count, 16, span), lambda s, *_: (s, 0, 0, 0)),
            ],
            scratch_shapes=[pltpu.VMEM((span_count, width, span), jnp.float32)],
        ),
        out_shape=[
            jax.ShapeDtypeStruct((devices, span_count, width, span), jnp.bfloat16),
            jax.ShapeDtypeStruct((devices, span_count, 16, span), jnp.float32),
        ],
    )(table, q_all, cache_keys, cache_values)


def combine_kernel(
    heads,
    o_ref, st_ref, q_ref, k_ref, v_ref,
    out_ref,
    own, query, before, relay, relay_st, got, got_st, mid, mid_st,
    relay2, relay2_st, got2, got2_st, acc, acc_st,
    load_sem, send, recv, send_st, recv_st, psend, precv,
):
    me = lax.axis_index("context")
    zpos, xpos = me // RING, lax.rem(me, RING)
    devices = RING * RING
    behind, ahead = lax.rem(me + devices - 1, devices), lax.rem(me + 1, devices)
    span = o_ref.shape[-1]
    token_count = k_ref.shape[0]
    cut = (heads + 1) // 2 * HDIM
    parts = ((0, cut), (cut, heads * HDIM - cut))
    order = (2, -1, 1, 0)

    def first_at(half, step):
        return wrap((xpos if half == 0 else zpos) + step)

    def second_at(half, step):
        return wrap((zpos if half == 0 else xpos) + step)

    def place(half, step, further):
        a, b = first_at(half, step), second_at(half, further)
        return (b, a, half) if half == 0 else (a, b, half)

    loads = {}
    count = 0
    for kind in (0, 1):
        for further in order:
            step = (1 if further in (2, 1) else -1) if kind == 0 else 0
            for half in (0, 1):
                slot = (half, kind, order.index(further))
                loads[slot] = pltpu.make_async_copy(
                    o_ref.at[place(half, step, further)], own.at[slot], load_sem.at[count]
                )
                loads[slot].start()
                count += 1
    query_load = pltpu.make_async_copy(
        q_ref.at[zpos, xpos, pl.ds(0, token_count)], query, load_sem.at[count]
    )
    query_load.start()

    barrier = pltpu.get_barrier_semaphore()
    for other in (
        context_of(zpos + 1, xpos),
        context_of(zpos - 1, xpos),
        context_of(zpos, xpos + 1),
        context_of(zpos, xpos - 1),
        behind,
        ahead,
    ):
        pl.semaphore_signal(barrier, inc=1, device_id={"context": other}, device_id_type=MESH)
    pl.semaphore_wait(barrier, 6)

    started = []

    def copies(half, index, way, first, src, src_st, dst, dst_st):
        if (half == 0) == first:
            to = {"context": context_of(zpos, xpos + way)}
        else:
            to = {"context": context_of(zpos + way, xpos)}
        base = half * 18
        return (
            remote(src, dst, (send, recv, base), index, to),
            remote(src_st, dst_st, (send_st, recv_st, base), index, to),
        )

    def start(*args):
        for copy in copies(*args):
            copy.start()
            started.append(copy)

    def arrive(half, index, dst, dst_st):
        for copy in copies(half, index, 1, True, dst, dst_st, dst, dst_st):
            copy.wait_recv()

    def merge(out, out_st, sources, head_range):
        results = []
        for h in head_range:
            rows = slice(h * HDIM, (h + 1) * HDIM)
            ms = [st[h : h + 1, :] for _, st in sources]
            m = functools.reduce(jnp.maximum, ms)
            ws = [jnp.exp2(x - m) for x in ms]
            ls = [st[8 + h : 9 + h, :] * w for (_, st), w in zip(sources, ws)]
            terms = [part[rows, :].astype(jnp.float32) * w for (part, _), w in zip(sources, ws)]
            total = functools.reduce(jnp.add, terms).astype(jnp.bfloat16)
            results.append((h, rows, m, functools.reduce(jnp.add, ls), total))
        for h, rows, m, l, total in results:
            out[rows, :] = total
            out_st[h : h + 1, :] = m
            out_st[8 + h : 9 + h, :] = l

    every = range(heads)

    def way_of(further):
        return 1 if further in (2, 1) else -1

    def forward(half, further):
        i, at = order.index(further), place(half, 2, further)
        start(
            half, i, way_of(further), True, o_ref.at[at], st_ref.at[at],
            relay.at[half, i], relay_st.at[half, i],
        )

    def direct(half, further):
        way = -way_of(further)
        i, at, side = order.index(further), place(half, way, further), 0 if way == 1 else 1
        start(
            half, 4 + i, way, True, o_ref.at[at], st_ref.at[at],
            got.at[half, side, i], got_st.at[half, side, i],
        )

    def merged(half, further):
        way = way_of(further)
        i, at, side = order.index(further), place(half, way, further), 0 if way == 1 else 1
        part, st = relay.at[half, i], relay_st.at[half, i]
        arrive(half, i, part, st)
        loads[half, 0, i].wait()
        merge(part, st, [(part, st), (own.at[half, 0, i], st_ref.at[at])], every)
        start(
            half, 8 + i, way, True, part, st, got.at[half, side, i], got_st.at[half, side, i]
        )

    def collect(half, further):
        i = order.index(further)
        side = 0 if way_of(further) == 1 else 1
        arrive(half, 4 + i, got.at[half, 1 - side, i], got_st.at[half, 1 - side, i])
        arrive(half, 8 + i, got.at[half, side, i], got_st.at[half, side, i])
        loads[half, 1, i].wait()
        merge(
            mid.at[half, i], mid_st.at[half, i],
            [(own.at[half, 1, i], st_ref.at[place(half, 0, further)])]
            + [(got.at[half, n, i], got_st.at[half, n, i]) for n in (0, 1)],
            every,
        )

    halves = (0, 1)
    for further in order:
        for half in halves:
            forward(half, further)
    for further in (2, -1):
        for half in halves:
            direct(half, further)

    key = lax.broadcasted_iota(jnp.int32, (span, span), 0)
    row = lax.broadcasted_iota(jnp.int32, (span, span), 1)

    def local(half, keys_of, values_of, bias, first):
        results = []
        for h in every:
            cols = slice(h * HDIM, (h + 1) * HDIM)
            s = dot_nt(keys_of(cols), query[half * span : (half + 1) * span, cols]) * SCALE
            s = jnp.where(key <= row, s, NEG) if bias is None else s + bias
            m = jnp.max(s, axis=0, keepdims=True)
            if not first:
                old = acc_st[half, h : h + 1, :]
                m = jnp.maximum(m, old)
                decay = jnp.exp2(old - m)
            p = jnp.exp2(s - m)
            l = jnp.sum(p, axis=0, keepdims=True)
            a = dot_tn(values_of(cols), p.astype(jnp.bfloat16))
            if not first:
                l = l + acc_st[half, 8 + h : 9 + h, :] * decay
                a = a + acc[half, cols, :] * decay
            results.append((h, cols, m, l, a))
        for h, cols, m, l, a in results:
            acc_st[half, h : h + 1, :] = m
            acc_st[half, 8 + h : 9 + h, :] = l
            acc[half, cols, :] = a

    query_load.wait()
    for half in halves:
        rows = slice(half * span, (half + 1) * span)
        local(half, lambda c, r=rows: k_ref[r, c], lambda c, r=rows: v_ref[r, c], None, True)

    for further in (2, -1):
        for half in halves:
            merged(half, further)
    for further in (1, 0):
        for half in halves:
            direct(half, further)
    prior = []
    for i, ref in enumerate((k_ref, v_ref)):
        prior.append(
            remote(
                ref.at[pl.ds(token_count - span, span), :], before.at[i], (psend, precv, 0), i,
                {"context": ahead},
            )
        )
        prior[-1].start()
    for further in (1, 0):
        for half in halves:
            merged(half, further)
    local(1, lambda c: k_ref[0:span, c], lambda c: v_ref[0:span, c], 0.0, False)

    for half in halves:
        collect(half, 2)
        for side, way in ((0, 1), (1, -1)):
            rows = pl.ds(*parts[side])
            start(
                half, 12 + side, way, False, mid.at[half, 0, rows], mid_st.at[half, 0],
                relay2.at[half, rows], relay2_st.at[half, side],
            )
    for side, way in ((1, -1), (0, 1)):
        for half in halves:
            i = order.index(way)
            collect(half, way)
            other = pl.ds(*parts[1 - side])
            start(
                half, 14 + side, way, False, mid.at[half, i, other], mid_st.at[half, i],
                got2.at[half, side, other], got2_st.at[half, side, 1 - side],
            )
    for half in halves:
        for side, way in ((0, 1), (1, -1)):
            i = order.index(way)
            rows = pl.ds(*parts[side])
            part, st = relay2.at[half], relay2_st.at[half, side]
            arrive(half, 12 + side, relay2.at[half, rows], st)
            merge(
                part, st, [(part, st), (mid.at[half, i], mid_st.at[half, i])],
                range(parts[side][0] // HDIM, sum(parts[side]) // HDIM),
            )
            start(
                half, 16 + side, way, False, relay2.at[half, rows], st,
                got2.at[half, side, rows], got2_st.at[half, side, side],
            )

    for copy in prior:
        copy.wait_recv()
    local(
        0, lambda c: before[0, :, c], lambda c: before[1, :, c], jnp.where(me > 0, 0.0, NEG), False
    )
    last = order.index(0)
    for half in halves:
        collect(half, 0)
    for half in halves:
        for side in (0, 1):
            for index, which in ((14 + side, 1 - side), (16 + side, side)):
                arrive(
                    half, index,
                    got2.at[half, side, pl.ds(*parts[which])], got2_st.at[half, side, which],
                )
        for h in every:
            cols = slice(h * HDIM, (h + 1) * HDIM)
            which = 0 if h * HDIM < cut else 1
            sources = [(mid.at[half, last], mid_st.at[half, last])]
            sources += [(got2.at[half, i], got2_st.at[half, i, which]) for i in (0, 1)]
            old = acc_st[half, h : h + 1, :]
            ms = [st[h : h + 1, :] for _, st in sources]
            m = functools.reduce(jnp.maximum, ms, old)
            decay = jnp.exp2(old - m)
            total = acc_st[half, 8 + h : 9 + h, :] * decay
            a = acc[half, cols, :] * decay
            for (part, st), x in zip(sources, ms):
                w = jnp.exp2(x - m)
                total = total + st[8 + h : 9 + h, :] * w
                a = a + part[cols, :].astype(jnp.float32) * w
            out_ref[half * span : (half + 1) * span, cols] = jnp.transpose(a / total).astype(
                out_ref.dtype
            )

    for copy in started + prior:
        copy.wait_send()


def combine(o, st, q_all, k, v, heads):
    span_count, width, span = o.shape[1:]
    rows = st.shape[2]
    o = o.reshape(RING, RING, span_count, width, span)
    st = st.reshape(RING, RING, span_count, rows, span)
    vmem = pl.BlockSpec(memory_space=pltpu.VMEM)
    hbm = pl.BlockSpec(memory_space=pl.ANY)

    def part(*lead):
        return pltpu.VMEM(lead + (width, span), jnp.bfloat16)

    def stats(*lead):
        return pltpu.VMEM(lead + (rows, span), jnp.float32)

    return pl.pallas_call(
        functools.partial(combine_kernel, heads),
        in_specs=[hbm, vmem, hbm, vmem, vmem],
        out_specs=vmem,
        out_shape=jax.ShapeDtypeStruct(k.shape, jnp.bfloat16),
        scratch_shapes=[
            part(2, 2, RING),
            pltpu.VMEM(k.shape, jnp.bfloat16),
            pltpu.VMEM((2, span, width), jnp.bfloat16),
            part(2, RING),
            stats(2, RING),
            part(2, 2, RING),
            stats(2, 2, RING),
            part(2, RING),
            stats(2, RING),
            part(2),
            stats(2, 2),
            part(2, 2),
            stats(2, 2, 2),
            pltpu.VMEM((2, width, span), jnp.float32),
            stats(2),
            pltpu.SemaphoreType.DMA((17,)),
        ]
        + [pltpu.SemaphoreType.DMA((36,))] * 4
        + [pltpu.SemaphoreType.DMA((2,))] * 2,
        compiler_params=pltpu.CompilerParams(
            collective_id=1, has_side_effects=True, vmem_limit_bytes=40 << 20
        ),
        name="combine",
    )(o, st, q_all, k, v)


def shards(
    tokens,
    query_weight,
    key_weight,
    value_weight,
    cache_keys,
    cache_values,
    selected,
    counts,
    block_slot,
):
    heads = query_weight.shape[1] // HDIM
    span_count, select_count = selected.shape
    devices = lax.axis_size("context")
    cap = max(2, 2 * span_count * select_count // devices)

    stored = cache_keys.shape[0]
    q_all, k, v, table = gather_project(
        tokens, query_weight, key_weight, value_weight, selected, counts, block_slot, cap, stored
    )
    o, st = owner_attention(table, q_all, cache_keys, cache_values, heads, cap)
    return combine(o, st, q_all, k, v, heads)


def solution(mesh):
    placed = (
        P("context", "tensor"),
        P("context", "tensor"),
        P("context", "tensor"),
        P("context", "tensor"),
        P("context", None, "tensor"),
        P("context", None, "tensor"),
        P("context", None),
        P("context"),
        P(),
    )
    return jax.shard_map(
        shards, mesh=mesh, in_specs=placed, out_specs=P("context", "tensor"), check_vma=False
    )
```

time: 185 us -> 193 us (1.043)
  local copies, waits for them, and re-layouts: 1.73 us -> 15.8 us
  Pallas kernels: 179 us -> 176 us
  other arithmetic: 2.23 us -> 0 us
    unnamed x1 -> x25, local copies, waits for them, and re-layouts: 1.73 us -> 15.8 us
    pallas_call x1, Pallas kernels: 109 us -> 107 us  [gather_project(): pl.pallas_call(functools.partial(project_kernel, span_count, select_count...]
where the time goes in v5:
time: 193 us; the launch traced here: 192 us
  Pallas kernels  176 us (91%)
  local copies, waits for them, and re-layouts  15.8 us (8%)
    pallas_call x1, Pallas kernels, gather_project(): pl.pallas_call(functools.partial(project_kernel, span_count, select_count...  107 us
    pallas_call x1, Pallas kernels, combine(): pl.pallas_call(functools.partial(combine_kernel, heads), in_specs=[hbm, v...  47.3 us
    pallas_call x1, Pallas kernels, owner_attention(): pl.pallas_call(functools.partial(owner_kernel, heads, cap), grid_spec=plt...  21.9 us
    unnamed x25, local copies, waits for them, and re-layouts  15.8 us

profile of v5, /device:TPU:0, one launch (start us, length us, event | category | flops | bytes accessed | tf_op | source)
XLA Modules:
  0.0 192.0 jit_solution(17443626091630477198)
XLA Ops:
  0.0 0.0 copy-start.3
  0.0 1.0 copy-done.3
  1.0 0.0 copy-start.4
  1.0 1.0 copy-done.4
  2.0 0.0 copy-start.5
  2.0 1.0 copy-done.5
  3.0 0.0 copy-start.6
  3.0 1.0 copy-done.6
  4.0 0.0 copy-start.9
  4.0 0.7 copy-done.9
  4.7 0.0 copy-start.10
  4.7 0.7 copy-done.10
  5.3 0.0 copy-start.11
  5.3 0.7 copy-done.11
  6.0 107.0 %gather_project.1 = (bf16[4,4,272,640]{3,2,1,0:T(8,128)(2,1)S(1)}, bf16[256,640]{1,0:T(8,128)(2,1)S(1)}, bf16[256,640]{1,0:T(8,128)(2,1)S(1)}, s32[2,16,128]{2,1,0:T(8,128)S(1)}) custom-call(bf16[256,640]{1,0:T(8,128)(2,1)S(1)} %copy-done.6, bf16[320,640]{1,0:T(8,128)(2,1)S(1)} %copy-done.3, bf16[320,640]{1,0:T(8,128)(2,1)S(1)} %copy-done.4, ...), custom_call_target="tpu_custom_call" | custom-call | tf_op jit(solution)/shard_map/gather_project/pallas_call | solution.py:486
  113.0 0.0 copy-start
  113.0 2.4 %copy-done = bf16[4,4,272,640]{3,2,1,0:T(8,128)(2,1)} copy-done((bf16[4,4,272,640]{3,2,1,0:T(8,128)(2,1)}, bf16[4,4,272,640]{3,2,1,0:T(8,128)(2,1)S(1)}, u32[]{:S(2)}) %copy-start) | copy-done | bytes 5570584
  115.4 0.0 copy-start.8
  115.5 0.6 copy-done.8
  116.1 21.9 %shard_map.91 = (bf16[16,2,640,128]{3,2,1,0:T(8,128)(2,1)}, f32[16,2,16,128]{3,2,1,0:T(8,128)}) custom-call(s32[2,16,128]{2,1,0:T(8,128)} %copy-done.8, bf16[16,272,640]{2,1,0:T(8,128)(2,1)} %bitcast.3, bf16[32,64,640]{2,1,0:T(8,128)(2,1)} %k_ref.1, bf16[32,64,640]{2,1,0:T(8,128)(2,1)} %v_ref.1), custom_call_target="tpu_custom_call" | custom-call | tf_op jit(solution)/shard_map/pallas_call | solution.py:586
  138.0 0.0 copy-start.1
  138.0 2.6 %copy-done.1 = bf16[4,4,272,640]{3,2,1,0:T(8,128)(2,1)S(1)} copy-done((bf16[4,4,272,640]{3,2,1,0:T(8,128)(2,1)S(1)}, bf16[4,4,272,640]{3,2,1,0:T(8,128)(2,1)}, u32[]{:S(2)}) %copy-start.1) | copy-done | bytes 5570584
  140.6 0.0 copy-start.2
  140.6 2.5 %copy-done.2 = bf16[16,2,640,128]{3,2,1,0:T(8,128)(2,1)S(1)} copy-done((bf16[16,2,640,128]{3,2,1,0:T(8,128)(2,1)S(1)}, bf16[16,2,640,128]{3,2,1,0:T(8,128)(2,1)}, u32[]{:S(2)}) %copy-start.2) | copy-done | bytes 5242904
  143.0 0.0 copy-start.7
  143.1 0.9 copy-done.7
  144.0 47.3 %combine.1 = bf16[256,640]{1,0:T(8,128)(2,1)S(1)} custom-call(bf16[4,4,2,640,128]{4,3,2,1,0:T(8,128)(2,1)S(1)} %bitcast.4, f32[4,4,2,16,128]{4,3,2,1,0:T(8,128)S(1)} %bitcast.5, bf16[4,4,272,640]{3,2,1,0:T(8,128)(2,1)S(1)} %copy-done.1, bf16[256,640]{1,0:T(8,128)(2,1)S(1)} %get-tuple-element.15.k_ref, bf16[256,640]{1,0:T(8,128)(2,1)S(1)} %get-tuple-element.16.v_ref), custom_call_target="tpu_custom_call" | custom-call | tf_op jit(solution)/shard_map/combine/pallas_call | solution.py:891
  191.3 0.7 copy.11
Async XLA Ops:
  0.0 1.0 copy-start.3
  1.0 1.0 copy-start.4
  2.0 1.0 copy-start.5
  3.0 1.0 copy-start.6
  4.0 0.7 copy-start.9
  4.7 0.7 copy-start.10
  5.3 0.7 copy-start.11
  113.0 2.4 %copy-start = (bf16[4,4,272,640]{3,2,1,0:T(8,128)(2,1)}, bf16[4,4,272,640]{3,2,1,0:T(8,128)(2,1)S(1)}, u32[]{:S(2)}) copy-start(bf16[4,4,272,640]{3,2,1,0:T(8,128)(2,1)S(1)} %get-tuple-element.12.q_ref) | copy-start | bytes 16711684
  115.4 0.6 copy-start.8
  138.0 2.6 %copy-start.1 = (bf16[4,4,272,640]{3,2,1,0:T(8,128)(2,1)S(1)}, bf16[4,4,272,640]{3,2,1,0:T(8,128)(2,1)}, u32[]{:S(2)}) copy-start(bf16[4,4,272,640]{3,2,1,0:T(8,128)(2,1)} %copy-done) | copy-start | bytes 16711684
  140.6 2.5 %copy-start.2 = (bf16[16,2,640,128]{3,2,1,0:T(8,128)(2,1)S(1)}, bf16[16,2,640,128]{3,2,1,0:T(8,128)(2,1)}, u32[]{:S(2)}) copy-start(bf16[16,2,640,128]{3,2,1,0:T(8,128)(2,1)} %get-tuple-element.13) | copy-start | bytes 15728644
  143.0 0.9 copy-start.7

commit v6 on v5

--- a/solution.py
+++ b/solution.py
@@ -245,6 +245,39 @@
         copy.start()
         copy.wait()
 
+    def compute(part, step):
+        for side in (0, 1):
+            t = wrap(ypos + step) * 2 + side
+            piece = w[part, wrap(ypos + step), 2 * side : 2 * side + 2].reshape(depth, w.shape[4])
+
+            @pl.loop(0, RING)
+            def _(z):
+                new = jnp.dot(tok[t, z], piece, preferred_element_type=jnp.float32)
+                if step == 0 and side == 0:
+                    acc[z] = new
+                else:
+                    acc[z] += new
+
+    def give_back(part, buf, columns, base):
+        buf[zpos] = acc[zpos, :, columns].astype(jnp.bfloat16)
+        for i, step in enumerate(OFFSETS[1:]):
+            copy = remote(
+                done.at[part, wrap(zpos + step), :, columns], buf.at[zpos],
+                (bsend, brecv, base), i, at_z(step),
+            )
+            copy.start()
+            sent.append(copy)
+
+    def take_back(buf, base):
+        for i, step in enumerate(OFFSETS[1:]):
+            ref = buf.at[wrap(zpos - step)]
+            remote(ref, ref, (bsend, brecv, base), i, at_z(step)).wait_recv()
+
+    def finish(part):
+        @pl.loop(0, RING)
+        def _(z):
+            done[part, z] = acc[z].astype(jnp.bfloat16)
+
     token_load.wait()
     ztok.whole()
     ytok[0].whole()
@@ -255,6 +288,22 @@
     exchange(0, -1)
     keep(1)
     xw[1, 0].whole()
+
+    lane = lax.broadcasted_iota(jnp.int32, (EXTRA, HDIM), 1)
+    line = lax.broadcasted_iota(jnp.int32, (EXTRA, HDIM), 0)
+    chosen = jnp.zeros((EXTRA, HDIM), jnp.int32)
+    for half in range(span_count):
+
+        def note(j, chosen, half=half):
+            slot = slot_ref[jnp.maximum(sel_ref[half, j], 0)]
+            owner = jnp.where(j < count_ref[half], slot // stored, -1)
+            value = jnp.where(line == half, owner, slot % stored)
+            here = (lane == j) & ((line == half) | (line == span_count + half))
+            return jnp.where(here, value, chosen)
+
+        chosen = lax.fori_loop(0, select_count, note, chosen)
+    small[token_count:, :] = chosen.astype(jnp.float32).astype(jnp.bfloat16)
+
     xw[0, 0].onward()
     ztok.onward()
     for o in (-1, 1):
@@ -285,90 +334,48 @@
     for step in (1, -1):
         exchange(1, step, receive=True)
         xw[1, -step].whole()
-    ytok[0].opposite()
-    share(2, 0)
     xw[0, 2].onward()
     exchange(1, 2, receive=True)
     xw[1, 2].whole()
+    for o in (-1, 1):
+        xw[1, o].onward()
+    ytok[0].opposite()
+    share(2, 0)
+
+    def shared(step):
+        for o in OFFSETS:
+            share(step, o, receive=True)
+
+    for o in OFFSETS:
+        xw[0, o].opposite()
+    shared(0)
+    compute(0, 0)
     ytok[2].onward()
     share(-1, 2)
     share(1, 2)
-    for o in (-1, 1, 2):
-        xw[1, o].onward()
-    for o in (-1, 1):
-        ytok[o].opposite()
-        share(2, o)
-
-    def compute(part, step):
-        for side in (0, 1):
-            t = wrap(ypos + step) * 2 + side
-            piece = w[part, wrap(ypos + step), 2 * side : 2 * side + 2].reshape(depth, w.shape[4])
-
-            @pl.loop(0, RING)
-            def _(z):
-                new = jnp.dot(tok[t, z], piece, preferred_element_type=jnp.float32)
-                if step == 0 and side == 0:
-                    acc[z] = new
-                else:
-                    acc[z] += new
-
-    def give_back(part, buf, columns, base):
-        buf[zpos] = acc[zpos, :, columns].astype(jnp.bfloat16)
-        for i, step in enumerate(OFFSETS[1:]):
-            copy = remote(
-                done.at[part, wrap(zpos + step), :, columns], buf.at[zpos],
-                (bsend, brecv, base), i, at_z(step),
-            )
-            copy.start()
-            sent.append(copy)
-
-    def take_back(buf, base):
-        for i, step in enumerate(OFFSETS[1:]):
-            ref = buf.at[wrap(zpos - step)]
-            remote(ref, ref, (bsend, brecv, base), i, at_z(step)).wait_recv()
-
-    def finish(part):
-        @pl.loop(0, RING)
-        def _(z):
-            done[part, z] = acc[z].astype(jnp.bfloat16)
-
-    lane = lax.broadcasted_iota(jnp.int32, (EXTRA, HDIM), 1)
-    line = lax.broadcasted_iota(jnp.int32, (EXTRA, HDIM), 0)
-    chosen = jnp.zeros((EXTRA, HDIM), jnp.int32)
-    for half in range(span_count):
-
-        def note(j, chosen, half=half):
-            slot = slot_ref[jnp.maximum(sel_ref[half, j], 0)]
-            owner = jnp.where(j < count_ref[half], slot // stored, -1)
-            value = jnp.where(line == half, owner, slot % stored)
-            here = (lane == j) & ((line == half) | (line == span_count + half))
-            return jnp.where(here, value, chosen)
-
-        chosen = lax.fori_loop(0, select_count, note, chosen)
-    small[token_count:, :] = chosen.astype(jnp.float32).astype(jnp.bfloat16)
-
-    for o in OFFSETS:
-        xw[0, o].opposite()
-    for step in OFFSETS[:3]:
-        for o in OFFSETS:
-            share(step, o, receive=True)
-        compute(0, step)
+    xw[1, 2].onward()
+    shared(-1)
+    compute(0, -1)
+    ytok[-1].opposite()
+    share(2, -1)
+    shared(1)
+    compute(0, 1)
+    ytok[1].opposite()
+    share(2, 1)
     ytok[2].opposite()
     share(2, 2)
-    for o in OFFSETS:
-        share(2, o, receive=True)
+    shared(2)
     compute(0, 2)
     finish(0)
 
-    groups = RING // 2
+    groups = (pl.ds(0, 1), pl.ds(1, RING - 1))
 
     def head_view(z, x, half, part):
-        low, size = ((0, groups), (0, groups // 2), (groups // 2, groups // 2))[part]
         head = pl.ds(pl.multiple_of(z * HDIM, HDIM), HDIM)
-        return q_ref.at[pl.ds(half * groups + low, size), x, pl.ds(0, token_count), head]
+        return q_ref.at[groups[half], x, cut(token_count)[part], head]
 
     def head_own(half):
-        return done.at[0, pl.ds(half * groups, groups), :, pl.ds(0, HDIM)]
+        return done.at[0, groups[half], :, pl.ds(0, HDIM)]
 
     heads = context_gather(head_view, head_own, (qsend, qrecv, 0), zpos, xpos, sent)
 
@@ -391,8 +398,8 @@
 
     last = context_gather(last_view, last_own, (qsend, qrecv, 40), zpos, xpos, sent)
 
+    give_back(0, fifth, slice(HDIM, 2 * HDIM), 0)
     heads[0]()
-    give_back(0, fifth, slice(HDIM, 2 * HDIM), 0)
     keeps = [
         pltpu.make_async_copy(
             done.at[0, :, :, pl.ds(0, HDIM)],
@@ -417,14 +424,14 @@
     keeps[1].start()
     heads[1]()
     compute(1, -1)
+    compute(1, 1)
     heads[2]()
     last[1]()
-    compute(1, 1)
-    heads[3]()
-    last[2]()
     compute(1, 2)
     finish(1)
     give_back(1, back, slice(0, 2 * HDIM), 3)
+    heads[3]()
+    last[2]()
     heads[4]()
     last[3]()
     last[4]()
@@ -510,7 +517,7 @@
         + dma(6)
         + dma(80),
         compiler_params=pltpu.CompilerParams(
-            collective_id=0, has_side_effects=True, vmem_limit_bytes=40 << 20
+            collective_id=0, has_side_effects=True, vmem_limit_bytes=60 << 20
         ),
         name="gather_project",
     )(tokens, wq, wk, wv, selected, counts, block_slot)
@@ -634,12 +641,15 @@
         a, b = first_at(half, step), second_at(half, further)
         return (b, a, half) if half == 0 else (a, b, half)
 
+    def way_of(half, further):
+        return 1 if further == 2 or (further == 1 and half == 1) else -1
+
     loads = {}
     count = 0
     for kind in (0, 1):
         for further in order:
-            step = (1 if further in (2, 1) else -1) if kind == 0 else 0
             for half in (0, 1):
+                step = way_of(half, further) if kind == 0 else 0
                 slot = (half, kind, order.index(further))
                 loads[slot] = pltpu.make_async_copy(
                     o_ref.at[place(half, step, further)], own.at[slot], load_sem.at[count]
@@ -703,18 +713,15 @@
 
     every = range(heads)
 
-    def way_of(further):
-        return 1 if further in (2, 1) else -1
-
     def forward(half, further):
         i, at = order.index(further), place(half, 2, further)
         start(
-            half, i, way_of(further), True, o_ref.at[at], st_ref.at[at],
+            half, i, way_of(half, further), True, o_ref.at[at], st_ref.at[at],
             relay.at[half, i], relay_st.at[half, i],
         )
 
     def direct(half, further):
-        way = -way_of(further)
+        way = -way_of(half, further)
         i, at, side = order.index(further), place(half, way, further), 0 if way == 1 else 1
         start(
             half, 4 + i, way, True, o_ref.at[at], st_ref.at[at],
@@ -722,7 +729,7 @@
         )
 
     def merged(half, further):
-        way = way_of(further)
+        way = way_of(half, further)
         i, at, side = order.index(further), place(half, way, further), 0 if way == 1 else 1
         part, st = relay.at[half, i], relay_st.at[half, i]
         arrive(half, i, part, st)
@@ -734,7 +741,7 @@
 
     def collect(half, further):
         i = order.index(further)
-        side = 0 if way_of(further) == 1 else 1
+        side = 0 if way_of(half, further) == 1 else 1
         arrive(half, 4 + i, got.at[half, 1 - side, i], got_st.at[half, 1 - side, i])
         arrive(half, 8 + i, got.at[half, side, i], got_st.at[half, side, i])
         loads[half, 1, i].wait()
@@ -914,7 +921,7 @@
         + [pltpu.SemaphoreType.DMA((36,))] * 4
         + [pltpu.SemaphoreType.DMA((2,))] * 2,
         compiler_params=pltpu.CompilerParams(
-            collective_id=1, has_side_effects=True, vmem_limit_bytes=40 << 20
+            collective_id=1, has_side_effects=True, vmem_limit_bytes=60 << 20
         ),
         name="combine",
     )(o, st, q_all, k, v)

time: 193 us -> 173 us (0.90)
  local copies, waits for them, and re-layouts: 15.8 us -> 1.73 us
  Pallas kernels: 176 us -> 172 us
    unnamed x25 -> x1, local copies, waits for them, and re-layouts: 15.8 us -> 1.73 us
    pallas_call x1, Pallas kernels: 107 us -> 104 us  [gather_project(): pl.pallas_call(functools.partial(project_kernel, span_count, select_count...]
    pallas_call x1, Pallas kernels: 47.3 us -> 45.2 us  [combine(): pl.pallas_call(functools.partial(combine_kernel, heads), in_specs=[hbm, v...]
where the time goes in v6:
time: 173 us; the launch traced here: 174 us
  Pallas kernels  172 us (99%)
  local copies, waits for them, and re-layouts  1.73 us (1%)
    pallas_call x1, Pallas kernels, gather_project(): pl.pallas_call(functools.partial(project_kernel, span_count, select_count...  104 us
    pallas_call x1, Pallas kernels, combine(): pl.pallas_call(functools.partial(combine_kernel, heads), in_specs=[hbm, v...  45.2 us
    pallas_call x1, Pallas kernels, owner_attention(): pl.pallas_call(functools.partial(owner_kernel, heads, cap), grid_spec=plt...  22.5 us

profile of v6, /device:TPU:0, one launch (start us, length us, event | category | flops | bytes accessed | tf_op | source)
XLA Modules:
  0.0 173.7 jit_solution(3601397952952787169)
XLA Ops:
  0.0 104.2 %gather_project.1 = (bf16[4,4,272,640]{3,2,1,0:T(8,128)(2,1)}, bf16[256,640]{1,0:T(8,128)(2,1)}, bf16[256,640]{1,0:T(8,128)(2,1)}, s32[2,16,128]{2,1,0:T(8,128)}) custom-call(bf16[256,640]{1,0:T(8,128)(2,1)} %tok_ref.1, bf16[320,640]{1,0:T(8,128)(2,1)} %wq_ref.1, bf16[320,640]{1,0:T(8,128)(2,1)} %wk_ref.1, bf16[320,640]{1,0:T(8,128)(2,1)} %wv_ref.1, ...), custom_call_target="tpu_custom_call" | custom-call | tf_op jit(solution)/shard_map/gather_project/pallas_call | solution.py:493
  104.2 22.5 %shard_map.91 = (bf16[16,2,640,128]{3,2,1,0:T(8,128)(2,1)}, f32[16,2,16,128]{3,2,1,0:T(8,128)}) custom-call(s32[2,16,128]{2,1,0:T(8,128)} %get-tuple-element.11.tab_ref, bf16[16,272,640]{2,1,0:T(8,128)(2,1)} %bitcast.3, bf16[32,64,640]{2,1,0:T(8,128)(2,1)} %k_ref.1, bf16[32,64,640]{2,1,0:T(8,128)(2,1)} %v_ref.1), custom_call_target="tpu_custom_call" | custom-call | tf_op jit(solution)/shard_map/pallas_call | solution.py:593
  126.7 45.2 %combine.1 = bf16[256,640]{1,0:T(8,128)(2,1)} custom-call(bf16[4,4,2,640,128]{4,3,2,1,0:T(8,128)(2,1)} %bitcast.4, f32[4,4,2,16,128]{4,3,2,1,0:T(8,128)} %bitcast.5, bf16[4,4,272,640]{3,2,1,0:T(8,128)(2,1)} %get-tuple-element.12.q_ref, bf16[256,640]{1,0:T(8,128)(2,1)} %get-tuple-element.15.k_ref, bf16[256,640]{1,0:T(8,128)(2,1)} %get-tuple-element.16.v_ref), custom_call_target="tpu_custom_call" | custom-call | tf_op jit(solution)/shard_map/combine/pallas_call | solution.py:898
  172.0 1.7 copy.11

commit v7 on v6

--- a/solution.py
+++ b/solution.py
@@ -11,6 +11,7 @@
 NEG = -1e30
 MESH = pl.DeviceIdType.MESH
 EXTRA = 16
+GROUP = 2
 SCALE = HDIM ** (-0.5) * 1.4426950408889634
 
 
@@ -524,64 +525,67 @@
 
 
 def owner_kernel(heads, cap, tab_ref, q_ref, k_ref, v_ref, o_ref, st_ref, acc_ref):
-    src = pl.program_id(0)
-    span_count = o_ref.shape[1]
-    span = o_ref.shape[3]
+    group, span_count, span = o_ref.shape[0], o_ref.shape[1], o_ref.shape[3]
+    first = pl.program_id(0) * group
     block = k_ref.shape[1]
     columns = [slice(h * HDIM, (h + 1) * HDIM) for h in range(heads)]
 
-    def scores(half, j):
-        n = tab_ref[half, src, cap]
-        r0 = tab_ref[half, src, 2 * j]
-        r1 = tab_ref[half, src, 2 * j + 1]
-        bias1 = jnp.where(2 * j + 1 < n, 0.0, NEG)
-        out = []
-        for cols in columns:
-            q = q_ref[0, half * span : (half + 1) * span, cols]
-            k = jnp.concatenate([k_ref[r0, :, cols], k_ref[r1, :, cols]], 0)
-            v = jnp.concatenate([v_ref[r0, :, cols], v_ref[r1, :, cols]], 0)
-            s = dot_nt(k, q) * SCALE
-            out.append((jnp.concatenate([s[:block], s[block:] + bias1], 0), v))
-        return out
-
-    for half in range(span_count):
-        results = []
-        for s, v in scores(half, 0):
-            m = jnp.max(s, axis=0, keepdims=True)
-            p = jnp.exp2(s - m)
-            l = jnp.sum(p, axis=0, keepdims=True)
-            results.append((m, l, dot_tn(v, p.astype(jnp.bfloat16))))
-        some = tab_ref[half, src, cap] > 0
-        for h, (m, l, a) in enumerate(results):
-            st_ref[0, half, h : h + 1, :] = jnp.where(some, m, NEG)
-            st_ref[0, half, 8 + h : 9 + h, :] = l
-            acc_ref[half, columns[h], :] = a
-            o_ref[0, half, columns[h], :] = a.astype(jnp.bfloat16)
-
-    for half in range(span_count):
-        n = tab_ref[half, src, cap]
+    def score(i, half, h, j):
+        r0 = tab_ref[half, first + i, 2 * j]
+        r1 = tab_ref[half, first + i, 2 * j + 1]
+        bias = jnp.where(2 * j + 1 < tab_ref[half, first + i, cap], 0.0, NEG)
+        cols = columns[h]
+        q = q_ref[i, half * span : (half + 1) * span, cols]
+        k = jnp.concatenate([k_ref[r0, :, cols], k_ref[r1, :, cols]], 0)
+        v = jnp.concatenate([v_ref[r0, :, cols], v_ref[r1, :, cols]], 0)
+        s = dot_nt(k, q) * SCALE
+        return jnp.concatenate([s[:block], s[block:] + bias], 0), v
+
+    def put(i, half, h, m, l, a):
+        st_ref[i, half, h : h + 1, :] = m
+        st_ref[i, half, 8 + h : 9 + h, :] = l
+        acc_ref[i, half, columns[h], :] = a
+        o_ref[i, half, columns[h], :] = a.astype(jnp.bfloat16)
+
+    places = [(i, half) for i in range(group) for half in range(span_count)]
+    def soften(i, half, h, s, v):
+        m = jnp.max(s, axis=0, keepdims=True)
+        p = jnp.exp2(s - m)
+        l = jnp.sum(p, axis=0, keepdims=True)
+        m = jnp.where(tab_ref[half, first + i, cap] > 0, m, NEG)
+        return i, half, h, m, l, p.astype(jnp.bfloat16), v
+
+    def weigh(i, half, h, m, l, p, v):
+        return i, half, h, m, l, dot_tn(v, p)
+
+    made = [[(i, half, h, *score(i, half, h, 0)) for h in range(heads)] for i, half in places]
+    results = []
+    for tiles in made:
+        soft = [soften(*tile) for tile in tiles]
+        results += [weigh(*tile) for tile in soft]
+    for result in results:
+        put(*result)
+
+    for i, half in places:
+        n = tab_ref[half, first + i, cap]
 
         @pl.when(n > 2)
-        def _():
+        def _(i=i, half=half, n=n):
             @pl.loop(1, (n + 1) // 2)
             def _(j):
                 results = []
-                for h, (s, v) in enumerate(scores(half, j)):
-                    old = st_ref[0, half, h : h + 1, :]
+                for h, (s, v) in enumerate([score(i, half, h, j) for h in range(heads)]):
+                    old = st_ref[i, half, h : h + 1, :]
                     m = jnp.maximum(jnp.max(s, axis=0, keepdims=True), old)
                     decay = jnp.exp2(old - m)
                     p = jnp.exp2(s - m)
                     l = jnp.sum(p, axis=0, keepdims=True)
-                    l = l + st_ref[0, half, 8 + h : 9 + h, :] * decay
-                    a = dot_tn(v, p.astype(jnp.bfloat16)) + acc_ref[half, columns[h], :] * decay
-                    results.append((m, l, a))
-                for h, (m, l, a) in enumerate(results):
-                    st_ref[0, half, h : h + 1, :] = m
-                    st_ref[0, half, 8 + h : 9 + h, :] = l
-                    acc_ref[half, columns[h], :] = a
-
-            for h in range(heads):
-                o_ref[0, half, columns[h], :] = acc_ref[half, columns[h], :].astype(jnp.bfloat16)
+                    l = l + st_ref[i, half, 8 + h : 9 + h, :] * decay
+                    a = dot_tn(v, p.astype(jnp.bfloat16))
+                    a = a + acc_ref[i, half, columns[h], :] * decay
+                    results.append((i, half, h, m, l, a))
+                for result in results:
+                    put(*result)
 
 
 def owner_attention(table, q_all, cache_keys, cache_values, heads, cap):
@@ -594,22 +598,23 @@
         functools.partial(owner_kernel, heads, cap),
         grid_spec=pltpu.PrefetchScalarGridSpec(
             num_scalar_prefetch=1,
-            grid=(devices,),
+            grid=(devices // GROUP,),
             in_specs=[
-                pl.BlockSpec((1, tokens, width), lambda s, *_: (s, 0, 0)),
+                pl.BlockSpec((GROUP, tokens, width), lambda s, *_: (s, 0, 0)),
                 whole,
                 whole,
             ],
             out_specs=[
-                pl.BlockSpec((1, span_count, width, span), lambda s, *_: (s, 0, 0, 0)),
-                pl.BlockSpec((1, span_count, 16, span), lambda s, *_: (s, 0, 0, 0)),
+                pl.BlockSpec((GROUP, span_count, width, span), lambda s, *_: (s, 0, 0, 0)),
+                pl.BlockSpec((GROUP, span_count, 16, span), lambda s, *_: (s, 0, 0, 0)),
             ],
-            scratch_shapes=[pltpu.VMEM((span_count, width, span), jnp.float32)],
+            scratch_shapes=[pltpu.VMEM((GROUP, span_count, width, span), jnp.float32)],
         ),
         out_shape=[
             jax.ShapeDtypeStruct((devices, span_count, width, span), jnp.bfloat16),
             jax.ShapeDtypeStruct((devices, span_count, 16, span), jnp.float32),
         ],
+        name="owner_attention",
     )(table, q_all, cache_keys, cache_values)
 
 

time: 173 us -> 167 us (0.965); the launches traced: 174 us -> 165 us
  Pallas kernels: 172 us -> 163 us
    pallas_call x1, Pallas kernels: 22.5 us -> 15.9 us  [owner_attention(): pl.pallas_call(functools.partial(owner_kernel, heads, cap), grid_spec=plt...]
    pallas_call x1, Pallas kernels: 45.2 us -> 42.8 us  [combine(): pl.pallas_call(functools.partial(combine_kernel, heads), in_specs=[hbm, v...]
where the time goes in v7:
time: 167 us; the launch traced here: 165 us
  Pallas kernels  163 us (98%)
  local copies, waits for them, and re-layouts  1.73 us (1%)
    pallas_call x1, Pallas kernels, gather_project(): pl.pallas_call(functools.partial(project_kernel, span_count, select_count...  104 us
    pallas_call x1, Pallas kernels, combine(): pl.pallas_call(functools.partial(combine_kernel, heads), in_specs=[hbm, v...  42.8 us
    pallas_call x1, Pallas kernels, owner_attention(): pl.pallas_call(functools.partial(owner_kernel, heads, cap), grid_spec=plt...  15.9 us

profile of v7, /device:TPU:0, one launch (start us, length us, event | category | flops | bytes accessed | tf_op | source)
XLA Modules:
  0.0 164.7 jit_solution(17422765950422542127)
XLA Ops:
  0.0 104.2 %gather_project.1 = (bf16[4,4,272,640]{3,2,1,0:T(8,128)(2,1)}, bf16[256,640]{1,0:T(8,128)(2,1)}, bf16[256,640]{1,0:T(8,128)(2,1)}, s32[2,16,128]{2,1,0:T(8,128)}) custom-call(bf16[256,640]{1,0:T(8,128)(2,1)} %tok_ref.1, bf16[320,640]{1,0:T(8,128)(2,1)} %wq_ref.1, bf16[320,640]{1,0:T(8,128)(2,1)} %wk_ref.1, bf16[320,640]{1,0:T(8,128)(2,1)} %wv_ref.1, ...), custom_call_target="tpu_custom_call" | custom-call | tf_op jit(solution)/shard_map/gather_project/pallas_call | solution.py:494
  104.2 15.9 %owner_attention.1 = (bf16[16,2,640,128]{3,2,1,0:T(8,128)(2,1)}, f32[16,2,16,128]{3,2,1,0:T(8,128)}) custom-call(s32[2,16,128]{2,1,0:T(8,128)} %get-tuple-element.11.tab_ref, bf16[16,272,640]{2,1,0:T(8,128)(2,1)} %bitcast.3, bf16[32,64,640]{2,1,0:T(8,128)(2,1)} %k_ref.1, bf16[32,64,640]{2,1,0:T(8,128)(2,1)} %v_ref.1), custom_call_target="tpu_custom_call" | custom-call | tf_op jit(solution)/shard_map/owner_attention/pallas_call | solution.py:597
  120.2 42.8 %combine.1 = bf16[256,640]{1,0:T(8,128)(2,1)} custom-call(bf16[4,4,2,640,128]{4,3,2,1,0:T(8,128)(2,1)} %bitcast.4, f32[4,4,2,16,128]{4,3,2,1,0:T(8,128)} %bitcast.5, bf16[4,4,272,640]{3,2,1,0:T(8,128)(2,1)} %get-tuple-element.12.q_ref, bf16[256,640]{1,0:T(8,128)(2,1)} %get-tuple-element.15.k_ref, bf16[256,640]{1,0:T(8,128)(2,1)} %get-tuple-element.16.v_ref), custom_call_target="tpu_custom_call" | custom-call | tf_op jit(solution)/shard_map/combine/pallas_call | solution.py:903
  163.0 1.7 %copy.11 = bf16[256,640]{1,0:T(8,128)(2,1)} copy(bf16[256,640]{1,0:T(8,128)(2,1)} %combine.1) | data formatting | bytes 655360

commit v8 on v7

--- a/solution.py
+++ b/solution.py
@@ -36,38 +36,30 @@
 
 
 class Ring:
-    def __init__(self, view, to, sems, sent, own=None):
-        self.view, self.to, self.sems, self.sent, self.own = view, to, sems, sent, own
-        self.waited = set()
+    def __init__(self, view, to, sems, own=None):
+        self.view, self.to, self.sems, self.own = view, to, sems, own
 
     def copy(self, index, step):
         ref = self.view(step, max(0, index - 1))
         src = self.own if step == 0 and self.own is not None else ref
-        return remote(src, ref, self.sems, index, self.to(1 if index % 2 == 0 else -1))
+        return remote(src, ref, self.sems, min(index, 2), self.to(1 if index % 2 == 0 else -1))
 
     def start(self, index):
-        copy = self.copy(index, (0, 0, -1, 1)[index])
-        copy.start()
-        self.sent.append(copy)
-
-    def arrive(self, index):
-        if index not in self.waited:
-            self.waited.add(index)
-            self.copy(index, (-1, 1, 2, 2)[index]).wait_recv()
+        self.copy(index, (0, 0, -1, 1)[index]).start()
 
     def whole(self):
         self.start(0)
         self.start(1)
 
     def onward(self):
-        self.arrive(0)
+        self.copy(0, -1).wait_recv()
         self.start(2)
-        self.arrive(1)
+        self.copy(1, 1).wait_recv()
         self.start(3)
 
     def opposite(self):
-        self.arrive(2)
-        self.arrive(3)
+        ref = self.view(2, 0)
+        remote(ref, ref, self.sems, 2, self.to(1)).wait_recv()
 
 
 def remote(src, dst, sems, index, to):
@@ -75,14 +67,14 @@
     return pltpu.make_async_remote_copy(
         src_ref=src,
         dst_ref=dst,
-        send_sem=send.at[base + index],
+        send_sem=send,
         recv_sem=recv.at[base + index],
         device_id=to,
         device_id_type=MESH,
     )
 
 
-def context_gather(view, own, sems, zpos, xpos, sent):
+def context_gather(view, own, sems, zpos, xpos, halves=(0, 1)):
     rings = {}
 
     def make(half, phase):
@@ -99,41 +91,41 @@
 
         send, recv, base = sems
         source = own(half) if first == 0 else None
-        return Ring(piece, to, (send, recv, base + half * 20 + phase * 4), sent, source)
-
-    for half in (0, 1):
+        return Ring(piece, to, (send, recv, base + halves.index(half) * 15 + phase * 3), source)
+
+    for half in halves:
         for phase in range(5):
             rings[half, phase] = make(half, phase)
 
     def own():
-        for half in (0, 1):
+        for half in halves:
             rings[half, 0].whole()
             rings[half, 1].whole()
 
     def neighbours():
-        for half in (0, 1):
+        for half in halves:
             rings[half, 0].onward()
             rings[half, 2].whole()
             rings[half, 3].whole()
-        for half in (0, 1):
+        for half in halves:
             rings[half, 1].onward()
 
     def far():
-        for half in (0, 1):
+        for half in halves:
             rings[half, 0].opposite()
             rings[half, 4].whole()
 
     def corners():
-        for half in (0, 1):
+        for half in halves:
             rings[half, 2].onward()
             rings[half, 3].onward()
 
     def last():
-        for half in (0, 1):
+        for half in halves:
             rings[half, 4].onward()
 
     def rest():
-        for half in (0, 1):
+        for half in halves:
             for phase in (1, 2, 3, 4):
                 rings[half, phase].opposite()
 
@@ -145,7 +137,7 @@
     tok_ref, wq_ref, wk_ref, wv_ref, sel_ref, count_ref, slot_ref,
     q_ref, k_ref, v_ref, tab_ref,
     tok, stage, w, acc, done, back, fifth, small, told,
-    load_sem, tsend, trecv, wsend, wrecv, bsend, brecv, qsend, qrecv,
+    load_sem, send, trecv, wrecv, brecv, qrecv,
 ):
     me = lax.axis_index("context")
     zpos, xpos = me // RING, lax.rem(me, RING)
@@ -153,11 +145,9 @@
     ypos, core = col // 2, lax.rem(col, 2)
     token_count, depth = tok.shape[2], tok.shape[3]
     rows = w.shape[3]
-    sent = []
 
     token_load = pltpu.make_async_copy(tok_ref, tok.at[col, zpos], load_sem.at[0])
     token_load.start()
-    loads = ([], [])
     for part in (0, 1):
         for to in range(RING):
             left = (wq_ref, wk_ref, wv_ref, wq_ref)[to]
@@ -166,10 +156,9 @@
                 load = pltpu.make_async_copy(
                     ref.at[:, pl.ds(head * HDIM, HDIM)],
                     stage.at[part, to, :, pl.ds(i * HDIM, HDIM)],
-                    load_sem.at[2 + part * 8 + to * 2 + i],
+                    load_sem.at[2 + part],
                 )
                 load.start()
-                loads[part].append(load)
 
     def at_x(way):
         return {"context": context_of(zpos, xpos + way)}
@@ -192,64 +181,84 @@
 
     ztok = Ring(
         lambda step, part: tok.at[col, wrap(zpos + step), cut(token_count)[part]],
-        at_z, (tsend, trecv, 0), sent,
+        at_z, (send.at[0], trecv, 0),
     )
     ytok = {
         o: Ring(
             lambda step, part, o=o: tok.at[
                 wrap(ypos + step) * 2 + core, wrap(zpos + o), cut(token_count)[part]
             ],
-            at_y, (tsend, trecv, 4 + 4 * i), sent,
+            at_y, (send.at[0], trecv, 3 + 3 * i),
         )
         for i, o in enumerate(OFFSETS)
     }
 
-    def share(step, o, receive=False):
-        side = 1 - core if receive else core
-        ref = tok.at[wrap(ypos + step) * 2 + side, wrap(zpos + o)]
-        index = 20 + OFFSETS.index(step) * 4 + OFFSETS.index(o)
-        copy = remote(ref, ref, (tsend, trecv, 0), index, mate)
-        if receive:
-            copy.wait_recv()
-        else:
-            copy.start()
-            sent.append(copy)
+    def share(step, o):
+        ref = tok.at[wrap(ypos + step) * 2 + core, wrap(zpos + o)]
+        remote(ref, ref, (send.at[1], trecv, 15), OFFSETS.index(o), mate).start()
+
+    def shared(o):
+        ref = tok.at[pl.ds(0, RING), 0]
+        remote(ref, ref, (send.at[1], trecv, 15), OFFSETS.index(o), mate).wait_recv()
 
     def exchange(part, step, receive=False):
         index = part * 3 + OFFSETS.index(step) - 1
         src = stage.at[part, wrap(zpos + step)]
         if receive:
             dst = w.at[part, wrap(zpos - step), xpos]
-            remote(src, dst, (wsend, wrecv, 0), index, at_z(step)).wait_recv()
+            remote(src, dst, (send.at[2], wrecv, 0), index, at_z(step)).wait_recv()
         else:
-            copy = remote(src, w.at[part, zpos, xpos], (wsend, wrecv, 0), index, at_z(step))
-            copy.start()
-            sent.append(copy)
+            dst = w.at[part, zpos, xpos]
+            remote(src, dst, (send.at[2], wrecv, 0), index, at_z(step)).start()
 
     xw = {
         (part, o): Ring(
             lambda step, piece, part=part, o=o: w.at[
                 part, wrap(zpos + o), wrap(xpos + step), cut(rows)[piece]
             ],
-            at_x, (wsend, wrecv, 6 + part * 16 + 4 * i), sent,
+            at_x, (send.at[3], wrecv, 6 + part * 12 + 3 * i),
         )
         for part in (0, 1)
         for i, o in enumerate(OFFSETS)
     }
 
     def keep(part):
-        for load in loads[part]:
-            load.wait()
+        whole = stage.at[part]
+        pltpu.make_async_copy(whole, whole, load_sem.at[2 + part]).wait()
         copy = pltpu.make_async_copy(
-            stage.at[part, zpos], w.at[part, zpos, xpos], load_sem.at[18 + part]
+            stage.at[part, zpos], w.at[part, zpos, xpos], load_sem.at[4 + part]
         )
         copy.start()
         copy.wait()
 
-    def compute(part, step):
+    def queries(o):
+        z = wrap(zpos + o)
+
+        @pl.loop(0, tok.shape[0])
+        def _(t):
+            piece = w[0, t // 2, pl.ds(lax.rem(t, 2) * 2, 2)].reshape(depth, w.shape[4])
+            new = jnp.dot(tok[t, z], piece, preferred_element_type=jnp.float32)
+
+            @pl.when(t == 0)
+            def _():
+                acc[z] = new
+
+            @pl.when(t > 0)
+            def _():
+                acc[z] += new
+
+        done[0, z] = acc[z].astype(jnp.bfloat16)
+        last_head = slice(HDIM, 2 * HDIM)
+        if o == 0:
+            fifth[zpos] = acc[z, :, last_head].astype(jnp.bfloat16)
+        else:
+            src = done.at[0, z, :, last_head]
+            remote(src, fifth.at[zpos], (send.at[4], brecv, 0), 0, at_z(o)).start()
+
+    def compute(step):
         for side in (0, 1):
             t = wrap(ypos + step) * 2 + side
-            piece = w[part, wrap(ypos + step), 2 * side : 2 * side + 2].reshape(depth, w.shape[4])
+            piece = w[1, wrap(ypos + step), 2 * side : 2 * side + 2].reshape(depth, w.shape[4])
 
             @pl.loop(0, RING)
             def _(z):
@@ -259,126 +268,34 @@
                 else:
                     acc[z] += new
 
-    def give_back(part, buf, columns, base):
-        buf[zpos] = acc[zpos, :, columns].astype(jnp.bfloat16)
-        for i, step in enumerate(OFFSETS[1:]):
-            copy = remote(
-                done.at[part, wrap(zpos + step), :, columns], buf.at[zpos],
-                (bsend, brecv, base), i, at_z(step),
-            )
-            copy.start()
-            sent.append(copy)
-
-    def take_back(buf, base):
-        for i, step in enumerate(OFFSETS[1:]):
-            ref = buf.at[wrap(zpos - step)]
-            remote(ref, ref, (bsend, brecv, base), i, at_z(step)).wait_recv()
-
-    def finish(part):
+    def give_back():
         @pl.loop(0, RING)
         def _(z):
-            done[part, z] = acc[z].astype(jnp.bfloat16)
-
-    token_load.wait()
-    ztok.whole()
-    ytok[0].whole()
-    share(0, 0)
-    keep(0)
-    xw[0, 0].whole()
-    exchange(0, 1)
-    exchange(0, -1)
-    keep(1)
-    xw[1, 0].whole()
-
-    lane = lax.broadcasted_iota(jnp.int32, (EXTRA, HDIM), 1)
-    line = lax.broadcasted_iota(jnp.int32, (EXTRA, HDIM), 0)
-    chosen = jnp.zeros((EXTRA, HDIM), jnp.int32)
-    for half in range(span_count):
-
-        def note(j, chosen, half=half):
-            slot = slot_ref[jnp.maximum(sel_ref[half, j], 0)]
-            owner = jnp.where(j < count_ref[half], slot // stored, -1)
-            value = jnp.where(line == half, owner, slot % stored)
-            here = (lane == j) & ((line == half) | (line == span_count + half))
-            return jnp.where(here, value, chosen)
-
-        chosen = lax.fori_loop(0, select_count, note, chosen)
-    small[token_count:, :] = chosen.astype(jnp.float32).astype(jnp.bfloat16)
-
-    xw[0, 0].onward()
-    ztok.onward()
-    for o in (-1, 1):
-        ytok[o].whole()
-        share(0, o)
-    ytok[0].onward()
-    exchange(0, 2)
-    exchange(1, 1)
-    exchange(1, -1)
-    exchange(1, 2)
-    share(-1, 0)
-    share(1, 0)
-    for step in (1, -1):
-        exchange(0, step, receive=True)
-        xw[0, -step].whole()
-    xw[1, 0].onward()
-    ztok.opposite()
-    ytok[2].whole()
-    share(0, 2)
-    exchange(0, 2, receive=True)
-    xw[0, 2].whole()
-    for o in (-1, 1):
-        ytok[o].onward()
-        share(-1, o)
-        share(1, o)
-    xw[0, -1].onward()
-    xw[0, 1].onward()
-    for step in (1, -1):
-        exchange(1, step, receive=True)
-        xw[1, -step].whole()
-    xw[0, 2].onward()
-    exchange(1, 2, receive=True)
-    xw[1, 2].whole()
-    for o in (-1, 1):
-        xw[1, o].onward()
-    ytok[0].opposite()
-    share(2, 0)
-
-    def shared(step):
-        for o in OFFSETS:
-            share(step, o, receive=True)
-
-    for o in OFFSETS:
-        xw[0, o].opposite()
-    shared(0)
-    compute(0, 0)
-    ytok[2].onward()
-    share(-1, 2)
-    share(1, 2)
-    xw[1, 2].onward()
-    shared(-1)
-    compute(0, -1)
-    ytok[-1].opposite()
-    share(2, -1)
-    shared(1)
-    compute(0, 1)
-    ytok[1].opposite()
-    share(2, 1)
-    ytok[2].opposite()
-    share(2, 2)
-    shared(2)
-    compute(0, 2)
-    finish(0)
-
-    groups = (pl.ds(0, 1), pl.ds(1, RING - 1))
-
-    def head_view(z, x, half, part):
-        head = pl.ds(pl.multiple_of(z * HDIM, HDIM), HDIM)
-        return q_ref.at[groups[half], x, cut(token_count)[part], head]
-
-    def head_own(half):
-        return done.at[0, groups[half], :, pl.ds(0, HDIM)]
-
-    heads = context_gather(head_view, head_own, (qsend, qrecv, 0), zpos, xpos, sent)
+            done[1, z] = acc[z].astype(jnp.bfloat16)
+
+        back[zpos] = acc[zpos].astype(jnp.bfloat16)
+        for step in OFFSETS[1:]:
+            src = done.at[1, wrap(zpos + step)]
+            remote(src, back.at[zpos], (send.at[5], brecv, 1), 0, at_z(step)).start()
+
+    def take_back(buf, index):
+        ref = buf.at[pl.ds(0, RING - 1)]
+        remote(ref, ref, (send.at[4], brecv, index), 0, at_z(1)).wait_recv()
+
+    def heads_of(o):
+        def view(z, x, half, part):
+            head = pl.ds(pl.multiple_of(z * HDIM, HDIM), HDIM)
+            return q_ref.at[wrap(z + o), x, cut(token_count)[part], head]
+
+        def own(half):
+            return done.at[0, wrap(zpos + o), :, pl.ds(0, HDIM)]
+
+        i = OFFSETS.index(o)
+        return context_gather(
+            view, own, (send.at[6], qrecv, 30 + 15 * i), zpos, xpos, ((0,), (1,))[i % 2]
+        )
+
+    heads = {o: heads_of(o) for o in OFFSETS}
 
     half_rows = token_count // 2
     quarter = half_rows // 2
@@ -397,10 +314,99 @@
     def last_own(half):
         return small.at[pl.ds(*ranges[half][0]), :]
 
-    last = context_gather(last_view, last_own, (qsend, qrecv, 40), zpos, xpos, sent)
-
-    give_back(0, fifth, slice(HDIM, 2 * HDIM), 0)
-    heads[0]()
+    last = context_gather(last_view, last_own, (send.at[7], qrecv, 0), zpos, xpos)
+
+    token_load.wait()
+    ztok.whole()
+    ytok[0].whole()
+    share(0, 0)
+    keep(0)
+    xw[0, 0].whole()
+    exchange(0, 1)
+    exchange(0, -1)
+    keep(1)
+
+    lane = lax.broadcasted_iota(jnp.int32, (EXTRA, HDIM), 1)
+    line = lax.broadcasted_iota(jnp.int32, (EXTRA, HDIM), 0)
+    chosen = jnp.zeros((EXTRA, HDIM), jnp.int32)
+    for half in range(span_count):
+
+        def note(j, chosen, half=half):
+            slot = slot_ref[jnp.maximum(sel_ref[half, j], 0)]
+            owner = jnp.where(j < count_ref[half], slot // stored, -1)
+            value = jnp.where(line == half, owner, slot % stored)
+            here = (lane == j) & ((line == half) | (line == span_count + half))
+            return jnp.where(here, value, chosen)
+
+        chosen = lax.fori_loop(0, select_count, note, chosen)
+    small[token_count:, :] = chosen.astype(jnp.float32).astype(jnp.bfloat16)
+
+    xw[0, 0].onward()
+    ztok.onward()
+    ytok[0].onward()
+    for o in (-1, 1):
+        ytok[o].whole()
+        share(0, o)
+    exchange(0, 2)
+    xw[1, 0].whole()
+    exchange(1, 1)
+    exchange(1, -1)
+    exchange(1, 2)
+    share(-1, 0)
+    share(1, 0)
+    for step in (1, -1):
+        exchange(0, step, receive=True)
+        xw[0, -step].whole()
+    ztok.opposite()
+    ytok[2].whole()
+    share(0, 2)
+    exchange(0, 2, receive=True)
+    xw[0, 2].whole()
+    ytok[-1].onward()
+    share(-1, -1)
+    share(1, -1)
+    ytok[0].opposite()
+    share(2, 0)
+    xw[0, -1].onward()
+    xw[0, 1].onward()
+    xw[1, 0].onward()
+    ytok[1].onward()
+    share(-1, 1)
+    share(1, 1)
+    xw[0, 2].onward()
+    for step in (1, -1):
+        exchange(1, step, receive=True)
+        xw[1, -step].whole()
+    exchange(1, 2, receive=True)
+    xw[1, 2].whole()
+    for o in OFFSETS:
+        xw[0, o].opposite()
+    shared(0)
+    queries(0)
+    heads[0][0]()
+    ytok[-1].opposite()
+    share(2, -1)
+    xw[1, -1].onward()
+    xw[1, 1].onward()
+    ytok[2].onward()
+    share(-1, 2)
+    share(1, 2)
+    shared(-1)
+    queries(-1)
+    heads[-1][0]()
+    ytok[1].opposite()
+    share(2, 1)
+    xw[1, 2].onward()
+    heads[0][1]()
+    shared(1)
+    queries(1)
+    heads[1][0]()
+    ytok[2].opposite()
+    share(2, 2)
+    heads[-1][1]()
+    shared(2)
+    queries(2)
+    heads[2][0]()
     keeps = [
         pltpu.make_async_copy(
             done.at[0, :, :, pl.ds(0, HDIM)],
@@ -411,42 +417,52 @@
         )
     ]
     keeps[0].start()
-    for o in OFFSETS:
-        xw[1, o].opposite()
-    compute(1, 0)
+    heads[0][2]()
+    heads[1][1]()
     take_back(fifth, 0)
     small[0:token_count, :] = fifth[0]
     last[0]()
     keeps.append(
         pltpu.make_async_copy(
-            small, q_ref.at[zpos, xpos, :, pl.ds(RING * HDIM, HDIM)], load_sem.at[20]
+            small, q_ref.at[zpos, xpos, :, pl.ds(RING * HDIM, HDIM)], load_sem.at[6]
         )
     )
     keeps[1].start()
-    heads[1]()
-    compute(1, -1)
-    compute(1, 1)
-    heads[2]()
+    for o in OFFSETS:
+        xw[1, o].opposite()
+    compute(0)
+    heads[-1][2]()
+    heads[0][3]()
+    heads[2][1]()
+    compute(-1)
     last[1]()
-    compute(1, 2)
-    finish(1)
-    give_back(1, back, slice(0, 2 * HDIM), 3)
-    heads[3]()
+    heads[1][2]()
+    heads[-1][3]()
+    heads[0][4]()
+    compute(1)
+    heads[2][2]()
+    heads[1][3]()
     last[2]()
-    heads[4]()
+    compute(2)
+    give_back()
+    heads[-1][4]()
+    heads[2][3]()
     last[3]()
+    heads[1][4]()
+    heads[2][4]()
     last[4]()
     for keep_copy in keeps:
         keep_copy.wait()
-    heads[5]()
+    for o in OFFSETS:
+        heads[o][5]()
     last[5]()
     look = pltpu.make_async_copy(
         q_ref.at[:, :, pl.ds(token_count, EXTRA), pl.ds(RING * HDIM, HDIM)],
         told,
-        load_sem.at[21],
+        load_sem.at[7],
     )
     look.start()
-    take_back(back, 3)
+    take_back(back, 1)
     for head in range(RING):
         cols = slice(head * HDIM, (head + 1) * HDIM)
         k_ref[:, cols] = back[head, :, 0:HDIM]
@@ -472,8 +488,19 @@
             table = jnp.where(lane == r, value, table)
         tab_ref[half] = table.astype(jnp.int32)
 
-    for copy in sent:
-        copy.wait_send()
+    for index, ref in enumerate(
+        (
+            tok.at[pl.ds(0, 5), pl.ds(0, 3)],
+            tok.at[pl.ds(0, 4)],
+            w.at[pl.ds(0, 2), pl.ds(0, 3), 0],
+            w.at[pl.ds(0, 2), pl.ds(0, 3)],
+            fifth.at[pl.ds(0, 3)],
+            back.at[pl.ds(0, 3)],
+            q_ref.at[:, pl.ds(0, 3), pl.ds(0, token_count), :],
+            q_ref.at[0, pl.ds(0, 3)],
+        )
+    ):
+        remote(ref, ref, (send.at[index], brecv, 0), 0, at_z(1)).wait_send()
 
 
 def gather_project(tokens, wq, wk, wv, selected, counts, block_slot, cap, stored):
@@ -487,9 +514,6 @@
     smem = pl.BlockSpec(memory_space=pltpu.SMEM)
     own = jax.ShapeDtypeStruct((token_count, width), jnp.bfloat16)
     two = 2 * HDIM
-
-    def dma(count):
-        return [pltpu.SemaphoreType.DMA((count,))] * 2
 
     return pl.pallas_call(
         functools.partial(project_kernel, span_count, select_count, cap, stored),
@@ -511,12 +535,8 @@
             pltpu.VMEM((RING, token_count, HDIM), jnp.bfloat16),
             pltpu.VMEM((token_count + EXTRA, HDIM), jnp.bfloat16),
             pltpu.VMEM((RING, RING, EXTRA, HDIM), jnp.bfloat16),
-            pltpu.SemaphoreType.DMA((22,)),
         ]
-        + dma(36)
-        + dma(38)
-        + dma(6)
-        + dma(80),
+        + [pltpu.SemaphoreType.DMA((count,)) for count in (8, 8, 19, 30, 2, 90)],
         compiler_params=pltpu.CompilerParams(
             collective_id=0, has_side_effects=True, vmem_limit_bytes=60 << 20
         ),
@@ -624,7 +644,7 @@
     out_ref,
     own, query, before, relay, relay_st, got, got_st, mid, mid_st,
     relay2, relay2_st, got2, got2_st, acc, acc_st,
-    load_sem, send, recv, send_st, recv_st, psend, precv,
+    load_sem, send, recv, recv_st, precv,
 ):
     me = lax.axis_index("context")
     zpos, xpos = me // RING, lax.rem(me, RING)
@@ -649,21 +669,16 @@
     def way_of(half, further):
         return 1 if further == 2 or (further == 1 and half == 1) else -1
 
-    loads = {}
-    count = 0
+    def load(ref, dst, index):
+        return pltpu.make_async_copy(ref, dst, load_sem.at[index])
+
     for kind in (0, 1):
         for further in order:
             for half in (0, 1):
                 step = way_of(half, further) if kind == 0 else 0
                 slot = (half, kind, order.index(further))
-                loads[slot] = pltpu.make_async_copy(
-                    o_ref.at[place(half, step, further)], own.at[slot], load_sem.at[count]
-                )
-                loads[slot].start()
-                count += 1
-    query_load = pltpu.make_async_copy(
-        q_ref.at[zpos, xpos, pl.ds(0, token_count)], query, load_sem.at[count]
-    )
+                load(o_ref.at[place(half, step, further)], own.at[slot], 0).start()
+    query_load = load(q_ref.at[zpos, xpos, pl.ds(0, token_count)], query, 1)
     query_load.start()
 
     barrier = pltpu.get_barrier_semaphore()
@@ -678,26 +693,24 @@
         pl.semaphore_signal(barrier, inc=1, device_id={"context": other}, device_id_type=MESH)
     pl.semaphore_wait(barrier, 6)
 
-    started = []
-
-    def copies(half, index, way, first, src, src_st, dst, dst_st):
+    def copies(half, index, way, src, src_st, dst, dst_st):
+        first = index < 8
         if (half == 0) == first:
             to = {"context": context_of(zpos, xpos + way)}
         else:
             to = {"context": context_of(zpos + way, xpos)}
-        base = half * 18
+        kind = 0 if first else 2
         return (
-            remote(src, dst, (send, recv, base), index, to),
-            remote(src_st, dst_st, (send_st, recv_st, base), index, to),
+            remote(src, dst, (send.at[kind], recv, half * 11), index, to),
+            remote(src_st, dst_st, (send.at[kind + 1], recv_st, half * 11), index, to),
         )
 
     def start(*args):
         for copy in copies(*args):
             copy.start()
-            started.append(copy)
 
     def arrive(half, index, dst, dst_st):
-        for copy in copies(half, index, 1, True, dst, dst_st, dst, dst_st):
+        for copy in copies(half, index, 1, dst, dst_st, dst, dst_st):
             copy.wait_recv()
 
     def merge(out, out_st, sources, head_range):
@@ -721,7 +734,7 @@
     def forward(half, further):
         i, at = order.index(further), place(half, 2, further)
         start(
-            half, i, way_of(half, further), True, o_ref.at[at], st_ref.at[at],
+            half, i, way_of(half, further), o_ref.at[at], st_ref.at[at],
             relay.at[half, i], relay_st.at[half, i],
         )
 
@@ -729,7 +742,7 @@
         way = -way_of(half, further)
         i, at, side = order.index(further), place(half, way, further), 0 if way == 1 else 1
         start(
-            half, 4 + i, way, True, o_ref.at[at], st_ref.at[at],
+            half, 4 + i, way, o_ref.at[at], st_ref.at[at],
             got.at[half, side, i], got_st.at[half, side, i],
         )
 
@@ -738,18 +751,15 @@
         i, at, side = order.index(further), place(half, way, further), 0 if way == 1 else 1
         part, st = relay.at[half, i], relay_st.at[half, i]
         arrive(half, i, part, st)
-        loads[half, 0, i].wait()
         merge(part, st, [(part, st), (own.at[half, 0, i], st_ref.at[at])], every)
         start(
-            half, 8 + i, way, True, part, st, got.at[half, side, i], got_st.at[half, side, i]
+            half, 4 + i, way, part, st, got.at[half, side, i], got_st.at[half, side, i]
         )
 
     def collect(half, further):
         i = order.index(further)
-        side = 0 if way_of(half, further) == 1 else 1
-        arrive(half, 4 + i, got.at[half, 1 - side, i], got_st.at[half, 1 - side, i])
-        arrive(half, 8 + i, got.at[half, side, i], got_st.at[half, side, i])
-        loads[half, 1, i].wait()
+        both = pl.ds(0, 2)
+        arrive(half, 4 + i, got.at[half, both, i], got_st.at[half, both, i])
         merge(
             mid.at[half, i], mid_st.at[half, i],
             [(own.at[half, 1, i], st_ref.at[place(half, 0, further)])]
@@ -792,6 +802,7 @@
             acc[half, cols, :] = a
 
     query_load.wait()
+    load(own, own, 0).wait()
     for half in halves:
         rows = slice(half * span, (half + 1) * span)
         local(half, lambda c, r=rows: k_ref[r, c], lambda c, r=rows: v_ref[r, c], None, True)
@@ -802,15 +813,9 @@
     for further in (1, 0):
         for half in halves:
             direct(half, further)
-    prior = []
     for i, ref in enumerate((k_ref, v_ref)):
-        prior.append(
-            remote(
-                ref.at[pl.ds(token_count - span, span), :], before.at[i], (psend, precv, 0), i,
-                {"context": ahead},
-            )
-        )
-        prior[-1].start()
+        last_rows = ref.at[pl.ds(token_count - span, span), :]
+        remote(last_rows, before.at[i], (send.at[4], precv, 0), 0, {"context": ahead}).start()
     for further in (1, 0):
         for half in halves:
             merged(half, further)
@@ -821,7 +826,7 @@
         for side, way in ((0, 1), (1, -1)):
             rows = pl.ds(*parts[side])
             start(
-                half, 12 + side, way, False, mid.at[half, 0, rows], mid_st.at[half, 0],
+                half, 8 + side, way, mid.at[half, 0, rows], mid_st.at[half, 0],
                 relay2.at[half, rows], relay2_st.at[half, side],
             )
     for side, way in ((1, -1), (0, 1)):
@@ -830,7 +835,7 @@
             collect(half, way)
             other = pl.ds(*parts[1 - side])
             start(
-                half, 14 + side, way, False, mid.at[half, i, other], mid_st.at[half, i],
+                half, 10, way, mid.at[half, i, other], mid_st.at[half, i],
                 got2.at[half, side, other], got2_st.at[half, side, 1 - side],
             )
     for half in halves:
@@ -838,18 +843,17 @@
             i = order.index(way)
             rows = pl.ds(*parts[side])
             part, st = relay2.at[half], relay2_st.at[half, side]
-            arrive(half, 12 + side, relay2.at[half, rows], st)
+            arrive(half, 8 + side, relay2.at[half, rows], st)
             merge(
                 part, st, [(part, st), (mid.at[half, i], mid_st.at[half, i])],
                 range(parts[side][0] // HDIM, sum(parts[side]) // HDIM),
             )
             start(
-                half, 16 + side, way, False, relay2.at[half, rows], st,
+                half, 10, way, relay2.at[half, rows], st,
                 got2.at[half, side, rows], got2_st.at[half, side, side],
             )
 
-    for copy in prior:
-        copy.wait_recv()
+    remote(before, before, (send.at[4], precv, 0), 0, {"context": ahead}).wait_recv()
     local(
         0, lambda c: before[0, :, c], lambda c: before[1, :, c], jnp.where(me > 0, 0.0, NEG), False
     )
@@ -857,12 +861,7 @@
     for half in halves:
         collect(half, 0)
     for half in halves:
-        for side in (0, 1):
-            for index, which in ((14 + side, 1 - side), (16 + side, side)):
-                arrive(
-                    half, index,
-                    got2.at[half, side, pl.ds(*parts[which])], got2_st.at[half, side, which],
-                )
+        arrive(half, 10, got2.at[half], got2_st.at[half])
         for h in every:
             cols = slice(h * HDIM, (h + 1) * HDIM)
             which = 0 if h * HDIM < cut else 1
@@ -882,8 +881,16 @@
                 out_ref.dtype
             )
 
-    for copy in started + prior:
-        copy.wait_send()
+    for index, ref in enumerate(
+        (
+            o_ref.at[pl.ds(0, 3)],
+            st_ref.at[pl.ds(0, 3)],
+            o_ref.at[pl.ds(0, 3), 0],
+            st_ref.at[pl.ds(0, 3), pl.ds(0, 2)],
+            before,
+        )
+    ):
+        remote(ref, ref, (send.at[index], precv, 0), 0, {"context": ahead}).wait_send()
 
 
 def combine(o, st, q_all, k, v, heads):
@@ -921,10 +928,8 @@
             stats(2, 2, 2),
             pltpu.VMEM((2, width, span), jnp.float32),
             stats(2),
-            pltpu.SemaphoreType.DMA((17,)),
         ]
-        + [pltpu.SemaphoreType.DMA((36,))] * 4
-        + [pltpu.SemaphoreType.DMA((2,))] * 2,
+        + [pltpu.SemaphoreType.DMA((count,)) for count in (2, 5, 22, 22, 1)],
         compiler_params=pltpu.CompilerParams(
             collective_id=1, has_side_effects=True, vmem_limit_bytes=60 << 20
         ),

time: 167 us -> 154 us (0.922); the launches traced: 165 us -> 154 us
  Pallas kernels: 163 us -> 152 us
    pallas_call x1, Pallas kernels: 104 us -> 92.8 us  [gather_project(): pl.pallas_call(functools.partial(project_kernel, span_count, select_count...]
where the time goes in v8:
time: 154 us
  Pallas kernels  152 us (99%)
  local copies, waits for them, and re-layouts  1.73 us (1%)
    pallas_call x1, Pallas kernels, gather_project(): pl.pallas_call(functools.partial(project_kernel, span_count, select_count...  92.8 us
    pallas_call x1, Pallas kernels, combine(): pl.pallas_call(functools.partial(combine_kernel, heads), in_specs=[hbm, v...  44.2 us
    pallas_call x1, Pallas kernels, owner_attention(): pl.pallas_call(functools.partial(owner_kernel, heads, cap), grid_spec=plt...  14.8 us

profile of v8, /device:TPU:0, one launch (start us, length us, event | category | flops | bytes accessed | tf_op | source)
XLA Modules:
  0.0 153.5 jit_solution(5131666856308433987)
XLA Ops:
  0.0 92.8 %gather_project.1 = (bf16[4,4,272,640]{3,2,1,0:T(8,128)(2,1)}, bf16[256,640]{1,0:T(8,128)(2,1)}, bf16[256,640]{1,0:T(8,128)(2,1)}, s32[2,16,128]{2,1,0:T(8,128)}) custom-call(bf16[256,640]{1,0:T(8,128)(2,1)} %tok_ref.1, bf16[320,640]{1,0:T(8,128)(2,1)} %wq_ref.1, bf16[320,640]{1,0:T(8,128)(2,1)} %wk_ref.1, bf16[320,640]{1,0:T(8,128)(2,1)} %wv_ref.1, ...), custom_call_target="tpu_custom_call" | custom-call | tf_op jit(solution)/shard_map/gather_project/pallas_call | solution.py:518
  92.8 14.8 %owner_attention.1 = (bf16[16,2,640,128]{3,2,1,0:T(8,128)(2,1)}, f32[16,2,16,128]{3,2,1,0:T(8,128)}) custom-call(s32[2,16,128]{2,1,0:T(8,128)} %get-tuple-element.11.tab_ref, bf16[16,272,640]{2,1,0:T(8,128)(2,1)} %bitcast.3, bf16[32,64,640]{2,1,0:T(8,128)(2,1)} %k_ref.1, bf16[32,64,640]{2,1,0:T(8,128)(2,1)} %v_ref.1), custom_call_target="tpu_custom_call" | custom-call | tf_op jit(solution)/shard_map/owner_attention/pallas_call | solution.py:617
  107.6 44.2 %combine.1 = bf16[256,640]{1,0:T(8,128)(2,1)} custom-call(bf16[4,4,2,640,128]{4,3,2,1,0:T(8,128)(2,1)} %bitcast.4, f32[4,4,2,16,128]{4,3,2,1,0:T(8,128)} %bitcast.5, bf16[4,4,272,640]{3,2,1,0:T(8,128)(2,1)} %get-tuple-element.12.q_ref, bf16[256,640]{1,0:T(8,128)(2,1)} %get-tuple-element.15.k_ref, bf16[256,640]{1,0:T(8,128)(2,1)} %get-tuple-element.16.v_ref), custom_call_target="tpu_custom_call" | custom-call | tf_op jit(solution)/shard_map/combine/pallas_call | solution.py:910
  151.8 1.7 %copy.11 = bf16[256,640]{1,0:T(8,128)(2,1)} copy(bf16[256,640]{1,0:T(8,128)(2,1)} %combine.1) | data formatting | bytes 655360

commit v9 on v8

--- a/solution.py
+++ b/solution.py
@@ -282,20 +282,24 @@
         ref = buf.at[pl.ds(0, RING - 1)]
         remote(ref, ref, (send.at[4], brecv, index), 0, at_z(1)).wait_recv()
 
-    def heads_of(o):
+    def heads_of(o, base, halves):
+        size = token_count // len(halves)
+
         def view(z, x, half, part):
             head = pl.ds(pl.multiple_of(z * HDIM, HDIM), HDIM)
-            return q_ref.at[wrap(z + o), x, cut(token_count)[part], head]
+            low = (half * size, half * size, half * size + size // 2)[part]
+            rows = pl.ds(low, size if part == 0 else size // 2)
+            return q_ref.at[wrap(z + o), x, rows, head]
 
         def own(half):
-            return done.at[0, wrap(zpos + o), :, pl.ds(0, HDIM)]
-
-        i = OFFSETS.index(o)
-        return context_gather(
-            view, own, (send.at[6], qrecv, 30 + 15 * i), zpos, xpos, ((0,), (1,))[i % 2]
-        )
-
-    heads = {o: heads_of(o) for o in OFFSETS}
+            return done.at[0, wrap(zpos + o), pl.ds(half * size, size), pl.ds(0, HDIM)]
+
+        return context_gather(view, own, (send.at[6], qrecv, base), zpos, xpos, halves)
+
+    heads = {
+        o: heads_of(o, *rest)
+        for o, *rest in ((0, 30, (0,)), (-1, 45, (0,)), (1, 60, (0, 1)), (2, 90, (0, 1)))
+    }
 
     half_rows = token_count // 2
     quarter = half_rows // 2
@@ -473,6 +477,7 @@
 
     devices = RING * RING
     lane = lax.broadcasted_iota(jnp.int32, (devices, HDIM), 1)
+    source = lax.broadcasted_iota(jnp.int32, (devices, HDIM), 0)
     before = lax.broadcasted_iota(jnp.int32, (HDIM, HDIM), 0)
     after = lax.broadcasted_iota(jnp.int32, (HDIM, HDIM), 1)
     earlier = jnp.where(before < after, 1.0, 0.0).astype(jnp.bfloat16)
@@ -486,6 +491,8 @@
         for r in range(cap):
             value = jnp.sum(jnp.where(rank == r, mine * row, 0.0), axis=1, keepdims=True)
             table = jnp.where(lane == r, value, table)
+        if half == 0:
+            table = jnp.where((lane == cap + 1) & (source == me + 1), 1.0, table)
         tab_ref[half] = table.astype(jnp.int32)
 
     for index, ref in enumerate(
@@ -536,7 +543,7 @@
             pltpu.VMEM((token_count + EXTRA, HDIM), jnp.bfloat16),
             pltpu.VMEM((RING, RING, EXTRA, HDIM), jnp.bfloat16),
         ]
-        + [pltpu.SemaphoreType.DMA((count,)) for count in (8, 8, 19, 30, 2, 90)],
+        + [pltpu.SemaphoreType.DMA((count,)) for count in (8, 8, 19, 30, 2, 120)],
         compiler_params=pltpu.CompilerParams(
             collective_id=0, has_side_effects=True, vmem_limit_bytes=60 << 20
         ),
@@ -544,7 +551,9 @@
     )(tokens, wq, wk, wv, selected, counts, block_slot)
 
 
-def owner_kernel(heads, cap, tab_ref, q_ref, k_ref, v_ref, o_ref, st_ref, acc_ref):
+def owner_kernel(
+    heads, cap, tab_ref, q_ref, k_ref, v_ref, pk_ref, pv_ref, o_ref, st_ref, acc_ref
+):
     group, span_count, span = o_ref.shape[0], o_ref.shape[1], o_ref.shape[3]
     first = pl.program_id(0) * group
     block = k_ref.shape[1]
@@ -586,6 +595,21 @@
     for result in results:
         put(*result)
 
+    def more(i, half, tiles):
+        results = []
+        for h, (s, v) in enumerate(tiles):
+            old = st_ref[i, half, h : h + 1, :]
+            m = jnp.maximum(jnp.max(s, axis=0, keepdims=True), old)
+            decay = jnp.exp2(old - m)
+            p = jnp.exp2(s - m)
+            l = jnp.sum(p, axis=0, keepdims=True)
+            l = l + st_ref[i, half, 8 + h : 9 + h, :] * decay
+            a = dot_tn(v, p.astype(jnp.bfloat16))
+            a = a + acc_ref[i, half, columns[h], :] * decay
+            results.append((i, half, h, m, l, a))
+        for result in results:
+            put(*result)
+
     for i, half in places:
         n = tab_ref[half, first + i, cap]
 
@@ -593,26 +617,25 @@
         def _(i=i, half=half, n=n):
             @pl.loop(1, (n + 1) // 2)
             def _(j):
-                results = []
-                for h, (s, v) in enumerate([score(i, half, h, j) for h in range(heads)]):
-                    old = st_ref[i, half, h : h + 1, :]
-                    m = jnp.maximum(jnp.max(s, axis=0, keepdims=True), old)
-                    decay = jnp.exp2(old - m)
-                    p = jnp.exp2(s - m)
-                    l = jnp.sum(p, axis=0, keepdims=True)
-                    l = l + st_ref[i, half, 8 + h : 9 + h, :] * decay
-                    a = dot_tn(v, p.astype(jnp.bfloat16))
-                    a = a + acc_ref[i, half, columns[h], :] * decay
-                    results.append((i, half, h, m, l, a))
-                for result in results:
-                    put(*result)
-
-
-def owner_attention(table, q_all, cache_keys, cache_values, heads, cap):
+                more(i, half, [score(i, half, h, j) for h in range(heads)])
+
+    for i in range(group):
+
+        @pl.when(tab_ref[0, first + i, cap + 1] > 0)
+        def _(i=i):
+            tiles = [
+                (dot_nt(pk_ref[:, cols], q_ref[i, 0:span, cols]) * SCALE, pv_ref[:, cols])
+                for cols in columns
+            ]
+            more(i, 0, tiles)
+
+
+def owner_attention(table, q_all, cache_keys, cache_values, k, v, heads, cap):
     tokens, width = q_all.shape[2] - EXTRA, q_all.shape[3]
     span_count, devices = table.shape[:2]
     span = tokens // span_count
     q_all = q_all.reshape(devices, tokens + EXTRA, width)
+    newest = pl.BlockSpec((span, width), lambda s, *_: (span_count - 1, 0))
     whole = pl.BlockSpec(cache_keys.shape, lambda s, *_: (0, 0, 0), pipeline_mode=pl.Buffered(1))
     return pl.pallas_call(
         functools.partial(owner_kernel, heads, cap),
@@ -623,6 +646,8 @@
                 pl.BlockSpec((GROUP, tokens, width), lambda s, *_: (s, 0, 0)),
                 whole,
                 whole,
+                newest,
+                newest,
             ],
             out_specs=[
                 pl.BlockSpec((GROUP, span_count, width, span), lambda s, *_: (s, 0, 0, 0)),
@@ -635,21 +660,19 @@
             jax.ShapeDtypeStruct((devices, span_count, 16, span), jnp.float32),
         ],
         name="owner_attention",
-    )(table, q_all, cache_keys, cache_values)
+    )(table, q_all, cache_keys, cache_values, k, v)
 
 
 def combine_kernel(
     heads,
     o_ref, st_ref, q_ref, k_ref, v_ref,
     out_ref,
-    own, query, before, relay, relay_st, got, got_st, mid, mid_st,
+    own, query, relay, relay_st, got, got_st, mid, mid_st,
     relay2, relay2_st, got2, got2_st, acc, acc_st,
-    load_sem, send, recv, recv_st, precv,
+    load_sem, send, recv, recv_st,
 ):
     me = lax.axis_index("context")
     zpos, xpos = me // RING, lax.rem(me, RING)
-    devices = RING * RING
-    behind, ahead = lax.rem(me + devices - 1, devices), lax.rem(me + 1, devices)
     span = o_ref.shape[-1]
     token_count = k_ref.shape[0]
     cut = (heads + 1) // 2 * HDIM
@@ -666,8 +689,8 @@
         a, b = first_at(half, step), second_at(half, further)
         return (b, a, half) if half == 0 else (a, b, half)
 
-    def way_of(half, further):
-        return 1 if further == 2 or (further == 1 and half == 1) else -1
+    def way_of(further):
+        return 1 if further in (2, 1) else -1
 
     def load(ref, dst, index):
         return pltpu.make_async_copy(ref, dst, load_sem.at[index])
@@ -675,7 +698,7 @@
     for kind in (0, 1):
         for further in order:
             for half in (0, 1):
-                step = way_of(half, further) if kind == 0 else 0
+                step = way_of(further) if kind == 0 else 0
                 slot = (half, kind, order.index(further))
                 load(o_ref.at[place(half, step, further)], own.at[slot], 0).start()
     query_load = load(q_ref.at[zpos, xpos, pl.ds(0, token_count)], query, 1)
@@ -687,11 +710,9 @@
         context_of(zpos - 1, xpos),
         context_of(zpos, xpos + 1),
         context_of(zpos, xpos - 1),
-        behind,
-        ahead,
     ):
         pl.semaphore_signal(barrier, inc=1, device_id={"context": other}, device_id_type=MESH)
-    pl.semaphore_wait(barrier, 6)
+    pl.semaphore_wait(barrier, 4)
 
     def copies(half, index, way, src, src_st, dst, dst_st):
         first = index < 8
@@ -734,12 +755,12 @@
     def forward(half, further):
         i, at = order.index(further), place(half, 2, further)
         start(
-            half, i, way_of(half, further), o_ref.at[at], st_ref.at[at],
+            half, i, way_of(further), o_ref.at[at], st_ref.at[at],
             relay.at[half, i], relay_st.at[half, i],
         )
 
     def direct(half, further):
-        way = -way_of(half, further)
+        way = -way_of(further)
         i, at, side = order.index(further), place(half, way, further), 0 if way == 1 else 1
         start(
             half, 4 + i, way, o_ref.at[at], st_ref.at[at],
@@ -747,7 +768,7 @@
         )
 
     def merged(half, further):
-        way = way_of(half, further)
+        way = way_of(further)
         i, at, side = order.index(further), place(half, way, further), 0 if way == 1 else 1
         part, st = relay.at[half, i], relay_st.at[half, i]
         arrive(half, i, part, st)
@@ -813,9 +834,6 @@
     for further in (1, 0):
         for half in halves:
             direct(half, further)
-    for i, ref in enumerate((k_ref, v_ref)):
-        last_rows = ref.at[pl.ds(token_count - span, span), :]
-        remote(last_rows, before.at[i], (send.at[4], precv, 0), 0, {"context": ahead}).start()
     for further in (1, 0):
         for half in halves:
             merged(half, further)
@@ -853,20 +871,29 @@
                 got2.at[half, side, rows], got2_st.at[half, side, side],
             )
 
-    remote(before, before, (send.at[4], precv, 0), 0, {"context": ahead}).wait_recv()
-    local(
-        0, lambda c: before[0, :, c], lambda c: before[1, :, c], jnp.where(me > 0, 0.0, NEG), False
-    )
     last = order.index(0)
     for half in halves:
         collect(half, 0)
+        part, st = mid.at[half, last], mid_st.at[half, last]
+        results = []
+        for h in every:
+            cols = slice(h * HDIM, (h + 1) * HDIM)
+            old, new = acc_st[half, h : h + 1, :], st[h : h + 1, :]
+            m = jnp.maximum(old, new)
+            decay, w = jnp.exp2(old - m), jnp.exp2(new - m)
+            l = acc_st[half, 8 + h : 9 + h, :] * decay + st[8 + h : 9 + h, :] * w
+            a = acc[half, cols, :] * decay + part[cols, :].astype(jnp.float32) * w
+            results.append((h, cols, m, l, a))
+        for h, cols, m, l, a in results:
+            acc_st[half, h : h + 1, :] = m
+            acc_st[half, 8 + h : 9 + h, :] = l
+            acc[half, cols, :] = a
     for half in halves:
         arrive(half, 10, got2.at[half], got2_st.at[half])
         for h in every:
             cols = slice(h * HDIM, (h + 1) * HDIM)
             which = 0 if h * HDIM < cut else 1
-            sources = [(mid.at[half, last], mid_st.at[half, last])]
-            sources += [(got2.at[half, i], got2_st.at[half, i, which]) for i in (0, 1)]
+            sources = [(got2.at[half, i], got2_st.at[half, i, which]) for i in (0, 1)]
             old = acc_st[half, h : h + 1, :]
             ms = [st[h : h + 1, :] for _, st in sources]
             m = functools.reduce(jnp.maximum, ms, old)
@@ -887,10 +914,10 @@
             st_ref.at[pl.ds(0, 3)],
             o_ref.at[pl.ds(0, 3), 0],
             st_ref.at[pl.ds(0, 3), pl.ds(0, 2)],
-            before,
         )
     ):
-        remote(ref, ref, (send.at[index], precv, 0), 0, {"context": ahead}).wait_send()
+        to = {"context": context_of(zpos, xpos + 1)}
+        remote(ref, ref, (send.at[index], recv, 0), 0, to).wait_send()
 
 
 def combine(o, st, q_all, k, v, heads):
@@ -915,7 +942,6 @@
         scratch_shapes=[
             part(2, 2, RING),
             pltpu.VMEM(k.shape, jnp.bfloat16),
-            pltpu.VMEM((2, span, width), jnp.bfloat16),
             part(2, RING),
             stats(2, RING),
             part(2, 2, RING),
@@ -929,7 +955,7 @@
             pltpu.VMEM((2, width, span), jnp.float32),
             stats(2),
         ]
-        + [pltpu.SemaphoreType.DMA((count,)) for count in (2, 5, 22, 22, 1)],
+        + [pltpu.SemaphoreType.DMA((count,)) for count in (2, 4, 22, 22)],
         compiler_params=pltpu.CompilerParams(
             collective_id=1, has_side_effects=True, vmem_limit_bytes=60 << 20
         ),
@@ -957,7 +983,7 @@
     q_all, k, v, table = gather_project(
         tokens, query_weight, key_weight, value_weight, selected, counts, block_slot, cap, stored
     )
-    o, st = owner_attention(table, q_all, cache_keys, cache_values, heads, cap)
+    o, st = owner_attention(table, q_all, cache_keys, cache_values, k, v, heads, cap)
     return combine(o, st, q_all, k, v, heads)
 
 

time: 154 us -> 154 us (level)
    pallas_call x1, Pallas kernels: 92.8 us -> 98.7 us  [gather_project(): pl.pallas_call(functools.partial(project_kernel, span_count, select_count...]
    pallas_call x1, Pallas kernels: 44.2 us -> 38.8 us  [combine(): pl.pallas_call(functools.partial(combine_kernel, heads), in_specs=[hbm, v...]
where the time goes in v9:
time: 154 us
  Pallas kernels  152 us (99%)
  local copies, waits for them, and re-layouts  1.73 us (1%)
    pallas_call x1, Pallas kernels, gather_project(): pl.pallas_call(functools.partial(project_kernel, span_count, select_count...  98.7 us
    pallas_call x1, Pallas kernels, combine(): pl.pallas_call(functools.partial(combine_kernel, heads), in_specs=[hbm, v...  38.8 us
    pallas_call x1, Pallas kernels, owner_attention(): pl.pallas_call(functools.partial(owner_kernel, heads, cap), grid_spec=plt...  14.9 us

profile of v9, /device:TPU:0, one launch (start us, length us, event | category | flops | bytes accessed | tf_op | source)
XLA Modules:
  0.0 154.1 jit_solution(6334163944946855701)
XLA Ops:
  0.0 98.7 %gather_project.1 = (bf16[4,4,272,640]{3,2,1,0:T(8,128)(2,1)}, bf16[256,640]{1,0:T(8,128)(2,1)}, bf16[256,640]{1,0:T(8,128)(2,1)}, s32[2,16,128]{2,1,0:T(8,128)}) custom-call(bf16[256,640]{1,0:T(8,128)(2,1)} %tok_ref.1, bf16[320,640]{1,0:T(8,128)(2,1)} %wq_ref.1, bf16[320,640]{1,0:T(8,128)(2,1)} %wk_ref.1, bf16[320,640]{1,0:T(8,128)(2,1)} %wv_ref.1, ...), custom_call_target="tpu_custom_call" | custom-call | tf_op jit(solution)/shard_map/gather_project/pallas_call | solution.py:525
  98.7 14.9 %owner_attention.1 = (bf16[16,2,640,128]{3,2,1,0:T(8,128)(2,1)}, f32[16,2,16,128]{3,2,1,0:T(8,128)}) custom-call(s32[2,16,128]{2,1,0:T(8,128)} %get-tuple-element.11.tab_ref, bf16[16,272,640]{2,1,0:T(8,128)(2,1)} %bitcast.3, bf16[32,64,640]{2,1,0:T(8,128)(2,1)} %k_ref.1, bf16[32,64,640]{2,1,0:T(8,128)(2,1)} %v_ref.1, ...), custom_call_target="tpu_custom_call" | custom-call | tf_op jit(solution)/shard_map/owner_attention/pallas_call | solution.py:640
  113.5 38.8 %combine.1 = bf16[256,640]{1,0:T(8,128)(2,1)} custom-call(bf16[4,4,2,640,128]{4,3,2,1,0:T(8,128)(2,1)} %bitcast.4, f32[4,4,2,16,128]{4,3,2,1,0:T(8,128)} %bitcast.5, bf16[4,4,272,640]{3,2,1,0:T(8,128)(2,1)} %get-tuple-element.12.q_ref, bf16[256,640]{1,0:T(8,128)(2,1)} %get-tuple-element.13.pk_ref.k_ref, bf16[256,640]{1,0:T(8,128)(2,1)} %get-tuple-element.14.pv_ref.v_ref), custom_call_target="tpu_custom_call" | custom-call | tf_op jit(solution)/shard_map/combine/pallas_call | solution.py:937
  152.4 1.7 %copy.11 = bf16[256,640]{1,0:T(8,128)(2,1)} copy(bf16[256,640]{1,0:T(8,128)(2,1)} %combine.1) | data formatting | bytes 655360

commit v10 on v9

--- a/solution.py
+++ b/solution.py
@@ -287,18 +287,18 @@
 
         def view(z, x, half, part):
             head = pl.ds(pl.multiple_of(z * HDIM, HDIM), HDIM)
-            low = (half * size, half * size, half * size + size // 2)[part]
+            low = halves.index(half) * size + (size // 2 if part == 2 else 0)
             rows = pl.ds(low, size if part == 0 else size // 2)
             return q_ref.at[wrap(z + o), x, rows, head]
 
         def own(half):
-            return done.at[0, wrap(zpos + o), pl.ds(half * size, size), pl.ds(0, HDIM)]
+            return done.at[0, wrap(zpos + o), pl.ds(halves.index(half) * size, size), pl.ds(0, HDIM)]
 
         return context_gather(view, own, (send.at[6], qrecv, base), zpos, xpos, halves)
 
     heads = {
         o: heads_of(o, *rest)
-        for o, *rest in ((0, 30, (0,)), (-1, 45, (0,)), (1, 60, (0, 1)), (2, 90, (0, 1)))
+        for o, *rest in ((0, 30, (0,)), (-1, 45, (0,)), (1, 60, (1,)), (2, 75, (1,)))
     }
 
     half_rows = token_count // 2
@@ -321,14 +321,15 @@
     last = context_gather(last_view, last_own, (send.at[7], qrecv, 0), zpos, xpos)
 
     token_load.wait()
-    ztok.whole()
     ytok[0].whole()
-    share(0, 0)
     keep(0)
     xw[0, 0].whole()
     exchange(0, 1)
     exchange(0, -1)
+    ztok.whole()
+    share(0, 0)
     keep(1)
+    xw[1, 0].whole()
 
     lane = lax.broadcasted_iota(jnp.int32, (EXTRA, HDIM), 1)
     line = lax.broadcasted_iota(jnp.int32, (EXTRA, HDIM), 0)
@@ -346,13 +347,12 @@
     small[token_count:, :] = chosen.astype(jnp.float32).astype(jnp.bfloat16)
 
     xw[0, 0].onward()
+    ytok[0].onward()
     ztok.onward()
-    ytok[0].onward()
     for o in (-1, 1):
         ytok[o].whole()
         share(0, o)
     exchange(0, 2)
-    xw[1, 0].whole()
     exchange(1, 1)
     exchange(1, -1)
     exchange(1, 2)
@@ -543,7 +543,7 @@
             pltpu.VMEM((token_count + EXTRA, HDIM), jnp.bfloat16),
             pltpu.VMEM((RING, RING, EXTRA, HDIM), jnp.bfloat16),
         ]
-        + [pltpu.SemaphoreType.DMA((count,)) for count in (8, 8, 19, 30, 2, 120)],
+        + [pltpu.SemaphoreType.DMA((count,)) for count in (8, 8, 19, 30, 2, 90)],
         compiler_params=pltpu.CompilerParams(
             collective_id=0, has_side_effects=True, vmem_limit_bytes=60 << 20
         ),

time: 154 us -> 147 us (0.955)
  Pallas kernels: 152 us -> 145 us
    pallas_call x1, Pallas kernels: 98.7 us -> 91.9 us  [gather_project(): pl.pallas_call(functools.partial(project_kernel, span_count, select_count...]
where the time goes in v10:
time: 147 us; the launch traced here: 146 us
  Pallas kernels  145 us (99%)
  local copies, waits for them, and re-layouts  1.73 us (1%)
    pallas_call x1, Pallas kernels, gather_project(): pl.pallas_call(functools.partial(project_kernel, span_count, select_count...  91.9 us
    pallas_call x1, Pallas kernels, combine(): pl.pallas_call(functools.partial(combine_kernel, heads), in_specs=[hbm, v...  37.9 us
    pallas_call x1, Pallas kernels, owner_attention(): pl.pallas_call(functools.partial(owner_kernel, heads, cap), grid_spec=plt...  14.9 us

profile of v10, /device:TPU:0, one launch (start us, length us, event | category | flops | bytes accessed | tf_op | source)
XLA Modules:
  0.0 146.5 jit_solution(12370913550058610445)
XLA Ops:
  0.0 91.9 %gather_project.1 = (bf16[4,4,272,640]{3,2,1,0:T(8,128)(2,1)}, bf16[256,640]{1,0:T(8,128)(2,1)}, bf16[256,640]{1,0:T(8,128)(2,1)}, s32[2,16,128]{2,1,0:T(8,128)}) custom-call(bf16[256,640]{1,0:T(8,128)(2,1)} %tok_ref.1, bf16[320,640]{1,0:T(8,128)(2,1)} %wq_ref.1, bf16[320,640]{1,0:T(8,128)(2,1)} %wk_ref.1, bf16[320,640]{1,0:T(8,128)(2,1)} %wv_ref.1, ...), custom_call_target="tpu_custom_call" | custom-call | tf_op jit(solution)/shard_map/gather_project/pallas_call | solution.py:525
  92.0 14.9 %owner_attention.1 = (bf16[16,2,640,128]{3,2,1,0:T(8,128)(2,1)}, f32[16,2,16,128]{3,2,1,0:T(8,128)}) custom-call(s32[2,16,128]{2,1,0:T(8,128)} %get-tuple-element.11.tab_ref, bf16[16,272,640]{2,1,0:T(8,128)(2,1)} %bitcast.3, bf16[32,64,640]{2,1,0:T(8,128)(2,1)} %k_ref.1, bf16[32,64,640]{2,1,0:T(8,128)(2,1)} %v_ref.1, ...), custom_call_target="tpu_custom_call" | custom-call | tf_op jit(solution)/shard_map/owner_attention/pallas_call | solution.py:640
  106.8 37.9 %combine.1 = bf16[256,640]{1,0:T(8,128)(2,1)} custom-call(bf16[4,4,2,640,128]{4,3,2,1,0:T(8,128)(2,1)} %bitcast.4, f32[4,4,2,16,128]{4,3,2,1,0:T(8,128)} %bitcast.5, bf16[4,4,272,640]{3,2,1,0:T(8,128)(2,1)} %get-tuple-element.12.q_ref, bf16[256,640]{1,0:T(8,128)(2,1)} %get-tuple-element.13.pk_ref.k_ref, bf16[256,640]{1,0:T(8,128)(2,1)} %get-tuple-element.14.pv_ref.v_ref), custom_call_target="tpu_custom_call" | custom-call | tf_op jit(solution)/shard_map/combine/pallas_call | solution.py:937
  144.7 1.7 %copy.11 = bf16[256,640]{1,0:T(8,128)(2,1)} copy(bf16[256,640]{1,0:T(8,128)(2,1)} %combine.1) | data formatting | bytes 655360

commit v11 on v10

--- a/solution.py
+++ b/solution.py
@@ -134,9 +134,10 @@
 
 def project_kernel(
     span_count, select_count, cap, stored,
-    tok_ref, wq_ref, wk_ref, wv_ref, sel_ref, count_ref, slot_ref,
-    q_ref, k_ref, v_ref, tab_ref,
-    tok, stage, w, acc, done, back, fifth, small, told,
+    tok_ref, wq_ref, wk_ref, wv_ref, sel_hbm, count_hbm, slot_hbm,
+    q_ref, k_out, v_out, tab_out,
+    tok, stage, w, acc, done, back, fifth, small, told, sel_ref, count_ref, slot_ref,
+    k_ref, v_ref, tab_ref,
     load_sem, send, trecv, wrecv, brecv, qrecv,
 ):
     me = lax.axis_index("context")
@@ -148,6 +149,14 @@
 
     token_load = pltpu.make_async_copy(tok_ref, tok.at[col, zpos], load_sem.at[0])
     token_load.start()
+    lists = [
+        pltpu.make_async_copy(src, dst, load_sem.at[8 + i])
+        for i, (src, dst) in enumerate(
+            ((sel_hbm, sel_ref), (count_hbm, count_ref), (slot_hbm, slot_ref))
+        )
+    ]
+    for load in lists:
+        load.start()
     for part in (0, 1):
         for to in range(RING):
             left = (wq_ref, wk_ref, wv_ref, wq_ref)[to]
@@ -333,6 +342,8 @@
 
     lane = lax.broadcasted_iota(jnp.int32, (EXTRA, HDIM), 1)
     line = lax.broadcasted_iota(jnp.int32, (EXTRA, HDIM), 0)
+    for load in lists:
+        load.wait()
     chosen = jnp.zeros((EXTRA, HDIM), jnp.int32)
     for half in range(span_count):
 
@@ -473,6 +484,13 @@
         v_ref[:, cols] = back[head, :, HDIM : 2 * HDIM]
     k_ref[:, RING * HDIM :] = fifth[1]
     v_ref[:, RING * HDIM :] = fifth[2]
+    puts = [
+        pltpu.make_async_copy(k_ref, k_out, load_sem.at[11]),
+        pltpu.make_async_copy(v_ref, v_out, load_sem.at[12]),
+        pltpu.make_async_copy(tab_ref, tab_out, load_sem.at[13]),
+    ]
+    puts[0].start()
+    puts[1].start()
     look.wait()
 
     devices = RING * RING
@@ -494,7 +512,10 @@
         if half == 0:
             table = jnp.where((lane == cap + 1) & (source == me + 1), 1.0, table)
         tab_ref[half] = table.astype(jnp.int32)
-
+    puts[2].start()
+
+    for put in puts:
+        put.wait()
     for index, ref in enumerate(
         (
             tok.at[pl.ds(0, 5), pl.ds(0, 3)],
@@ -517,15 +538,13 @@
     devices = lax.axis_size("context")
     columns = lax.axis_size("tensor")
     hbm = pl.BlockSpec(memory_space=pl.ANY)
-    vmem = pl.BlockSpec(memory_space=pltpu.VMEM)
-    smem = pl.BlockSpec(memory_space=pltpu.SMEM)
     own = jax.ShapeDtypeStruct((token_count, width), jnp.bfloat16)
     two = 2 * HDIM
 
     return pl.pallas_call(
         functools.partial(project_kernel, span_count, select_count, cap, stored),
-        in_specs=[hbm] * 4 + [smem] * 3,
-        out_specs=[hbm] + [vmem] * 3,
+        in_specs=[hbm] * 7,
+        out_specs=[hbm] * 4,
         out_shape=[
             jax.ShapeDtypeStruct((RING, RING, token_count + EXTRA, width), jnp.bfloat16),
             own,
@@ -542,8 +561,14 @@
             pltpu.VMEM((RING, token_count, HDIM), jnp.bfloat16),
             pltpu.VMEM((token_count + EXTRA, HDIM), jnp.bfloat16),
             pltpu.VMEM((RING, RING, EXTRA, HDIM), jnp.bfloat16),
+            pltpu.SMEM(selected.shape, jnp.int32),
+            pltpu.SMEM(counts.shape, jnp.int32),
+            pltpu.SMEM(block_slot.shape, jnp.int32),
+            pltpu.VMEM((token_count, width), jnp.bfloat16),
+            pltpu.VMEM((token_count, width), jnp.bfloat16),
+            pltpu.VMEM((span_count, devices, HDIM), jnp.int32),
         ]
-        + [pltpu.SemaphoreType.DMA((count,)) for count in (8, 8, 19, 30, 2, 90)],
+        + [pltpu.SemaphoreType.DMA((count,)) for count in (14, 8, 19, 30, 2, 90)],
         compiler_params=pltpu.CompilerParams(
             collective_id=0, has_side_effects=True, vmem_limit_bytes=60 << 20
         ),
@@ -667,7 +692,7 @@
     heads,
     o_ref, st_ref, q_ref, k_ref, v_ref,
     out_ref,
-    own, query, relay, relay_st, got, got_st, mid, mid_st,
+    own, query, keys, values, st_own, relay, relay_st, got, got_st, mid, mid_st,
     relay2, relay2_st, got2, got2_st, acc, acc_st,
     load_sem, send, recv, recv_st,
 ):
@@ -702,7 +727,9 @@
                 slot = (half, kind, order.index(further))
                 load(o_ref.at[place(half, step, further)], own.at[slot], 0).start()
     query_load = load(q_ref.at[zpos, xpos, pl.ds(0, token_count)], query, 1)
-    query_load.start()
+    others = [load(k_ref, keys, 2), load(v_ref, values, 3), load(st_ref, st_own, 4)]
+    for other in [query_load] + others:
+        other.start()
 
     barrier = pltpu.get_barrier_semaphore()
     for other in (
@@ -772,7 +799,7 @@
         i, at, side = order.index(further), place(half, way, further), 0 if way == 1 else 1
         part, st = relay.at[half, i], relay_st.at[half, i]
         arrive(half, i, part, st)
-        merge(part, st, [(part, st), (own.at[half, 0, i], st_ref.at[at])], every)
+        merge(part, st, [(part, st), (own.at[half, 0, i], st_own.at[at])], every)
         start(
             half, 4 + i, way, part, st, got.at[half, side, i], got_st.at[half, side, i]
         )
@@ -783,7 +810,7 @@
         arrive(half, 4 + i, got.at[half, both, i], got_st.at[half, both, i])
         merge(
             mid.at[half, i], mid_st.at[half, i],
-            [(own.at[half, 1, i], st_ref.at[place(half, 0, further)])]
+            [(own.at[half, 1, i], st_own.at[place(half, 0, further)])]
             + [(got.at[half, n, i], got_st.at[half, n, i]) for n in (0, 1)],
             every,
         )
@@ -822,11 +849,12 @@
             acc_st[half, 8 + h : 9 + h, :] = l
             acc[half, cols, :] = a
 
-    query_load.wait()
+    for other in [query_load] + others:
+        other.wait()
     load(own, own, 0).wait()
     for half in halves:
         rows = slice(half * span, (half + 1) * span)
-        local(half, lambda c, r=rows: k_ref[r, c], lambda c, r=rows: v_ref[r, c], None, True)
+        local(half, lambda c, r=rows: keys[r, c], lambda c, r=rows: values[r, c], None, True)
 
     for further in (2, -1):
         for half in halves:
@@ -837,7 +865,7 @@
     for further in (1, 0):
         for half in halves:
             merged(half, further)
-    local(1, lambda c: k_ref[0:span, c], lambda c: v_ref[0:span, c], 0.0, False)
+    local(1, lambda c: keys[0:span, c], lambda c: values[0:span, c], 0.0, False)
 
     for half in halves:
         collect(half, 2)
@@ -936,12 +964,15 @@
 
     return pl.pallas_call(
         functools.partial(combine_kernel, heads),
-        in_specs=[hbm, vmem, hbm, vmem, vmem],
+        in_specs=[hbm] * 5,
         out_specs=vmem,
         out_shape=jax.ShapeDtypeStruct(k.shape, jnp.bfloat16),
         scratch_shapes=[
             part(2, 2, RING),
             pltpu.VMEM(k.shape, jnp.bfloat16),
+            pltpu.VMEM(k.shape, jnp.bfloat16),
+            pltpu.VMEM(k.shape, jnp.bfloat16),
+            stats(RING, RING, span_count),
             part(2, RING),
             stats(2, RING),
             part(2, 2, RING),
@@ -955,7 +986,7 @@
             pltpu.VMEM((2, width, span), jnp.float32),
             stats(2),
         ]
-        + [pltpu.SemaphoreType.DMA((count,)) for count in (2, 4, 22, 22)],
+        + [pltpu.SemaphoreType.DMA((count,)) for count in (5, 4, 22, 22)],
         compiler_params=pltpu.CompilerParams(
             collective_id=1, has_side_effects=True, vmem_limit_bytes=60 << 20
         ),

time: 147 us -> 146 us (level)
    pallas_call x1, Pallas kernels: 14.9 us -> 16.9 us  [owner_attention(): pl.pallas_call(functools.partial(owner_kernel, heads, cap), grid_spec=plt...]
where the time goes in v11:
time: 146 us
  Pallas kernels  145 us (99%)
  local copies, waits for them, and re-layouts  1.73 us (1%)
    pallas_call x1, Pallas kernels, gather_project(): pl.pallas_call(functools.partial(project_kernel, span_count, select_count...  90.9 us
    pallas_call x1, Pallas kernels, combine(): pl.pallas_call(functools.partial(combine_kernel, heads), in_specs=[hbm] *...  36.9 us
    pallas_call x1, Pallas kernels, owner_attention(): pl.pallas_call(functools.partial(owner_kernel, heads, cap), grid_spec=plt...  16.9 us

profile of v11, /device:TPU:0, one launch (start us, length us, event | category | flops | bytes accessed | tf_op | source)
XLA Modules:
  0.0 146.5 jit_solution(14637866249077454510)
XLA Ops:
  0.0 90.9 %gather_project.1 = (bf16[4,4,272,640]{3,2,1,0:T(8,128)(2,1)}, bf16[256,640]{1,0:T(8,128)(2,1)}, bf16[256,640]{1,0:T(8,128)(2,1)}, s32[2,16,128]{2,1,0:T(8,128)}) custom-call(bf16[256,640]{1,0:T(8,128)(2,1)} %tok_ref.1, bf16[320,640]{1,0:T(8,128)(2,1)} %wq_ref.1, bf16[320,640]{1,0:T(8,128)(2,1)} %wk_ref.1, bf16[320,640]{1,0:T(8,128)(2,1)} %wv_ref.1, ...), custom_call_target="tpu_custom_call" | custom-call | tf_op jit(solution)/shard_map/gather_project/pallas_call | solution.py:544
  90.9 16.9 %owner_attention.1 = (bf16[16,2,640,128]{3,2,1,0:T(8,128)(2,1)}, f32[16,2,16,128]{3,2,1,0:T(8,128)}) custom-call(s32[2,16,128]{2,1,0:T(8,128)} %get-tuple-element.11.tab_ref, bf16[16,272,640]{2,1,0:T(8,128)(2,1)} %bitcast.3, bf16[32,64,640]{2,1,0:T(8,128)(2,1)} %k_ref.1, bf16[32,64,640]{2,1,0:T(8,128)(2,1)} %v_ref.1, ...), custom_call_target="tpu_custom_call" | custom-call | tf_op jit(solution)/shard_map/owner_attention/pallas_call | solution.py:665
  107.8 36.9 %combine.1 = bf16[256,640]{1,0:T(8,128)(2,1)} custom-call(bf16[4,4,2,640,128]{4,3,2,1,0:T(8,128)(2,1)} %bitcast.4, f32[4,4,2,16,128]{4,3,2,1,0:T(8,128)} %bitcast.5, bf16[4,4,272,640]{3,2,1,0:T(8,128)(2,1)} %get-tuple-element.12.q_ref, bf16[256,640]{1,0:T(8,128)(2,1)} %get-tuple-element.13.pk_ref.k_ref, bf16[256,640]{1,0:T(8,128)(2,1)} %get-tuple-element.14.pv_ref.v_ref), custom_call_target="tpu_custom_call" | custom-call | tf_op jit(solution)/shard_map/combine/pallas_call | solution.py:965
  144.8 1.7 %copy.11 = bf16[256,640]{1,0:T(8,128)(2,1)} copy(bf16[256,640]{1,0:T(8,128)(2,1)} %combine.1) | data formatting | bytes 655360

commit v12 on v11

--- a/solution.py
+++ b/solution.py
@@ -11,7 +11,7 @@
 NEG = -1e30
 MESH = pl.DeviceIdType.MESH
 EXTRA = 16
-GROUP = 2
+GROUP = 4
 SCALE = HDIM ** (-0.5) * 1.4426950408889634
 
 

time: 146 us -> 144 us (0.986); the launches traced: 146 us -> 142 us
  Pallas kernels: 145 us -> 140 us
    pallas_call x1, Pallas kernels: 36.9 us -> 34.4 us  [combine(): pl.pallas_call(functools.partial(combine_kernel, heads), in_specs=[hbm] *...]
    pallas_call x1, Pallas kernels: 16.9 us -> 15 us  [owner_attention(): pl.pallas_call(functools.partial(owner_kernel, heads, cap), grid_spec=plt...]
where the time goes in v12:
time: 144 us; the launch traced here: 142 us
  Pallas kernels  140 us (97%)
  local copies, waits for them, and re-layouts  1.73 us (1%)
    pallas_call x1, Pallas kernels, gather_project(): pl.pallas_call(functools.partial(project_kernel, span_count, select_count...  90.9 us
    pallas_call x1, Pallas kernels, combine(): pl.pallas_call(functools.partial(combine_kernel, heads), in_specs=[hbm] *...  34.4 us
    pallas_call x1, Pallas kernels, owner_attention(): pl.pallas_call(functools.partial(owner_kernel, heads, cap), grid_spec=plt...  15 us

profile of v12, /device:TPU:0, one launch (start us, length us, event | category | flops | bytes accessed | tf_op | source)
XLA Modules:
  0.0 142.1 jit_solution(952657710509432879)
XLA Ops:
  0.0 90.9 %gather_project.1 = (bf16[4,4,272,640]{3,2,1,0:T(8,128)(2,1)}, bf16[256,640]{1,0:T(8,128)(2,1)}, bf16[256,640]{1,0:T(8,128)(2,1)}, s32[2,16,128]{2,1,0:T(8,128)}) custom-call(bf16[256,640]{1,0:T(8,128)(2,1)} %tok_ref.1, bf16[320,640]{1,0:T(8,128)(2,1)} %wq_ref.1, bf16[320,640]{1,0:T(8,128)(2,1)} %wk_ref.1, bf16[320,640]{1,0:T(8,128)(2,1)} %wv_ref.1, ...), custom_call_target="tpu_custom_call" | custom-call | tf_op jit(solution)/shard_map/gather_project/pallas_call | solution.py:544
  90.9 15.0 %owner_attention.1 = (bf16[16,2,640,128]{3,2,1,0:T(8,128)(2,1)}, f32[16,2,16,128]{3,2,1,0:T(8,128)}) custom-call(s32[2,16,128]{2,1,0:T(8,128)} %get-tuple-element.11.tab_ref, bf16[16,272,640]{2,1,0:T(8,128)(2,1)} %bitcast.3, bf16[32,64,640]{2,1,0:T(8,128)(2,1)} %k_ref.1, bf16[32,64,640]{2,1,0:T(8,128)(2,1)} %v_ref.1, ...), custom_call_target="tpu_custom_call" | custom-call | tf_op jit(solution)/shard_map/owner_attention/pallas_call | solution.py:665
  105.9 34.4 %combine.1 = bf16[256,640]{1,0:T(8,128)(2,1)} custom-call(bf16[4,4,2,640,128]{4,3,2,1,0:T(8,128)(2,1)} %bitcast.4, f32[4,4,2,16,128]{4,3,2,1,0:T(8,128)} %bitcast.5, bf16[4,4,272,640]{3,2,1,0:T(8,128)(2,1)} %get-tuple-element.12.q_ref, bf16[256,640]{1,0:T(8,128)(2,1)} %get-tuple-element.13.pk_ref.k_ref, bf16[256,640]{1,0:T(8,128)(2,1)} %get-tuple-element.14.pv_ref.v_ref), custom_call_target="tpu_custom_call" | custom-call | tf_op jit(solution)/shard_map/combine/pallas_call | solution.py:965
  140.3 1.7 %copy.11 = bf16[256,640]{1,0:T(8,128)(2,1)} copy(bf16[256,640]{1,0:T(8,128)(2,1)} %combine.1) | data formatting | bytes 655360

commit v13 on v11

--- a/solution.py
+++ b/solution.py
@@ -307,7 +307,7 @@
 
     heads = {
         o: heads_of(o, *rest)
-        for o, *rest in ((0, 30, (0,)), (-1, 45, (0,)), (1, 60, (1,)), (2, 75, (1,)))
+        for o, *rest in ((0, 30, (0,)), (-1, 45, (1,)), (1, 60, (0,)), (2, 75, (1,)))
     }
 
     half_rows = token_count // 2

time: 146 us -> 144 us (0.986)
  Pallas kernels: 145 us -> 142 us
    pallas_call x1, Pallas kernels: 36.9 us -> 34.1 us  [combine(): pl.pallas_call(functools.partial(combine_kernel, heads), in_specs=[hbm] *...]
where the time goes in v13:
time: 144 us; the launch traced here: 143 us
  Pallas kernels  142 us (99%)
  local copies, waits for them, and re-layouts  1.73 us (1%)
    pallas_call x1, Pallas kernels, gather_project(): pl.pallas_call(functools.partial(project_kernel, span_count, select_count...  90.6 us
    pallas_call x1, Pallas kernels, combine(): pl.pallas_call(functools.partial(combine_kernel, heads), in_specs=[hbm] *...  34.1 us
    pallas_call x1, Pallas kernels, owner_attention(): pl.pallas_call(functools.partial(owner_kernel, heads, cap), grid_spec=plt...  16.9 us

profile of v13, /device:TPU:0, one launch (start us, length us, event | category | flops | bytes accessed | tf_op | source)
XLA Modules:
  0.0 143.3 jit_solution(17785570243691864388)
XLA Ops:
  0.0 90.6 %gather_project.1 = (bf16[4,4,272,640]{3,2,1,0:T(8,128)(2,1)}, bf16[256,640]{1,0:T(8,128)(2,1)}, bf16[256,640]{1,0:T(8,128)(2,1)}, s32[2,16,128]{2,1,0:T(8,128)}) custom-call(bf16[256,640]{1,0:T(8,128)(2,1)} %tok_ref.1, bf16[320,640]{1,0:T(8,128)(2,1)} %wq_ref.1, bf16[320,640]{1,0:T(8,128)(2,1)} %wk_ref.1, bf16[320,640]{1,0:T(8,128)(2,1)} %wv_ref.1, ...), custom_call_target="tpu_custom_call" | custom-call | tf_op jit(solution)/shard_map/gather_project/pallas_call | solution.py:544
  90.6 16.9 %owner_attention.1 = (bf16[16,2,640,128]{3,2,1,0:T(8,128)(2,1)}, f32[16,2,16,128]{3,2,1,0:T(8,128)}) custom-call(s32[2,16,128]{2,1,0:T(8,128)} %get-tuple-element.11.tab_ref, bf16[16,272,640]{2,1,0:T(8,128)(2,1)} %bitcast.3, bf16[32,64,640]{2,1,0:T(8,128)(2,1)} %k_ref.1, bf16[32,64,640]{2,1,0:T(8,128)(2,1)} %v_ref.1, ...), custom_call_target="tpu_custom_call" | custom-call | tf_op jit(solution)/shard_map/owner_attention/pallas_call | solution.py:665
  107.5 34.1 %combine.1 = bf16[256,640]{1,0:T(8,128)(2,1)} custom-call(bf16[4,4,2,640,128]{4,3,2,1,0:T(8,128)(2,1)} %bitcast.4, f32[4,4,2,16,128]{4,3,2,1,0:T(8,128)} %bitcast.5, bf16[4,4,272,640]{3,2,1,0:T(8,128)(2,1)} %get-tuple-element.12.q_ref, bf16[256,640]{1,0:T(8,128)(2,1)} %get-tuple-element.13.pk_ref.k_ref, bf16[256,640]{1,0:T(8,128)(2,1)} %get-tuple-element.14.pv_ref.v_ref), custom_call_target="tpu_custom_call" | custom-call | tf_op jit(solution)/shard_map/combine/pallas_call | solution.py:965
  141.6 1.7 %copy.11 = bf16[256,640]{1,0:T(8,128)(2,1)} copy(bf16[256,640]{1,0:T(8,128)(2,1)} %combine.1) | data formatting | bytes 655360
